TPU v7x, 128 devices: a whole 4x4x4 slice. The times are simulated.
128 devices in a mesh: lang: 8 (over z, y_lo), fsdp: 16 (over y_hi, x, core).
Axes of the slice: x: 4, y: 4 (y_hi: 2, y_lo: 2; y = y_hi * 2 + y_lo), z: 4, core: 2. Of those that a mesh axis runs over, the one named last changes fastest.
Arguments:
- tokens: bfloat16 [8, 768, 8192], P('lang', 'fsdp'), may hold values from -6 to 6
- grad_out: bfloat16 [8, 768, 8192], P('lang', 'fsdp'), may hold values from -24 to 24
- doc_ids: int32 [8, 768], P('lang'), may hold values from 0 to 95, never falling along the last dimension, each value on 1 to 64 neighbouring positions
- w_gate: bfloat16 [8192, 4096], P(None, 'fsdp'), may hold values from -0.0625 to 0.0625
- w_up: bfloat16 [8192, 4096], P(None, 'fsdp'), may hold values from -0.0625 to 0.0625
- w_down: bfloat16 [4096, 8192], P('fsdp'), may hold values from -0.09375 to 0.09375
Outputs:
- grad_tokens: bfloat16 [8, 768, 8192], P('lang', 'fsdp')
- grad_gate: bfloat16 [8192, 4096], P('lang', 'fsdp')
- grad_up: bfloat16 [8192, 4096], P('lang', 'fsdp')
- grad_down: bfloat16 [4096, 8192], P('fsdp', 'lang')
Inputs may be any that keep to these rules, and one draw needn't show every extreme that they name: `doc_ids`: document numbers never fall along a group's pack.
All inputs are finite; a program needn't handle non-finite values.
Results may differ from a plain program's by a relative error of at most 0.015.
Values may be sent and summed in bfloat16 or wider, within the bound.
No kernel may reach another device: no remote copies, remote signals or barrier semaphores. Data moves between devices by JAX's collectives and lax.ppermute only.
A program may use at most 192 MiB of HBM per device.

v0:
```python
import functools

import jax
import jax.numpy as jnp
from jax import lax
from jax.experimental import pallas as pl
from jax.experimental.pallas import tpu as pltpu
from jax.sharding import PartitionSpec as P


epsilon = 1e-06
INTERPRET = False
VMEM = 58 << 20

PLACES = ((0, 0), (-1, 0), (1, 0), (0, 1), (-1, 1), (1, 1), (2, 0), (2, 1))
BATCHES = ((0, 1, 2, 3), (4, 5, 6), (7,))
PIECES = (
    (2, 1, 0), (2, 1, 1), (1, 1, 1), (-1, 1, 0), (2, 0, 0), (2, 0, 1),
    (1, 1, 0), (-1, 1, 1), (1, 0, 0), (1, 0, 1), (-1, 0, 0), (-1, 0, 1),
    (0, 1, 0), (0, 1, 1), (0, 0, 0), (0, 0, 1),
)
EARLY = 4
ALONE = 2


def fsdp_pairs(dx, dy, dc):
    return [
        (y * 8 + x * 2 + c, (y ^ dy) * 8 + (x + dx) % 4 * 2 + (c ^ dc))
        for y in range(2)
        for x in range(4)
        for c in range(2)
    ]


def lang_pairs(dz, dy):
    return [(z * 2 + y, (z + dz) % 4 * 2 + (y ^ dy)) for z in range(4) for y in range(2)]


def to_x(value, step):
    return lax.ppermute(value, "fsdp", fsdp_pairs(step, 0, 0))


def to_y_half(value):
    return lax.ppermute(value, "fsdp", fsdp_pairs(0, 1, 0))


def to_core(value):
    return lax.ppermute(value, "fsdp", fsdp_pairs(0, 0, 1))


def to_z(value, step):
    return lax.ppermute(value, "lang", lang_pairs(step, 0))


def to_y_next(value):
    return lax.ppermute(value, "lang", lang_pairs(0, 1))


def after(value, *others):
    return lax.optimization_barrier((value, *others))[0]


def forward_kernel(n, *refs):
    toks, outs = refs[:n], refs[n : 2 * n]
    wg, wu, wd, inv, ggu_ref, hid_ref, gate, up, back = refs[2 * n :]
    step = pl.program_id(0)
    features = jnp.concatenate([r[...] for r in toks], axis=0)
    upstream = jnp.concatenate([r[...] for r in outs], axis=0)

    @pl.when(step == 0)
    def _():
        gate[...] = jnp.zeros_like(gate)
        up[...] = jnp.zeros_like(up)
        back[...] = jnp.zeros_like(back)

    gate[...] += jnp.dot(features, wg[...], preferred_element_type=jnp.float32)
    up[...] += jnp.dot(features, wu[...], preferred_element_type=jnp.float32)
    back[...] += contract_cols(upstream, wd[...])

    @pl.when(step == pl.num_programs(0) - 1)
    def _():
        width = gate.shape[1]
        inverse = inv[...]
        gate_pre = gate[...]
        up_pre = up[...]
        sig = 1.0 / (1.0 + jnp.exp(-gate_pre))
        act = gate_pre * sig
        hid_ref[...] = (act * up_pre * inverse).astype(hid_ref.dtype)
        hid_grad = back[...] * inverse
        gate_grad = hid_grad * up_pre * sig * (1.0 + gate_pre * (1.0 - sig))
        ggu_ref[:, :width] = gate_grad.astype(ggu_ref.dtype)
        ggu_ref[:, width:] = (hid_grad * act).astype(ggu_ref.dtype)


def forward(toks, outs, w_gate, w_up, w_down, inverse):
    n = len(toks)
    rows, depth = toks[0].shape
    hid = w_gate.shape[1]
    block = min(1024, depth)
    act = pl.BlockSpec((rows, block), lambda k: (0, k))
    wide = pl.BlockSpec((block, hid), lambda k: (k, 0))
    return pl.pallas_call(
        functools.partial(forward_kernel, n),
        name="forward",
        grid=(depth // block,),
        in_specs=[act] * (2 * n) + [wide, wide,
                  pl.BlockSpec((hid, block), lambda k: (0, k)),
                  pl.BlockSpec((n * rows, 1), lambda k: (0, 0))],
        out_specs=[pl.BlockSpec((n * rows, 2 * hid), lambda k: (0, 0)),
                   pl.BlockSpec((n * rows, hid), lambda k: (0, 0))],
        out_shape=[jax.ShapeDtypeStruct((n * rows, 2 * hid), jnp.bfloat16),
                   jax.ShapeDtypeStruct((n * rows, hid), jnp.bfloat16)],
        scratch_shapes=[pltpu.VMEM((n * rows, hid), jnp.float32)] * 3,
        compiler_params=pltpu.CompilerParams(
            dimension_semantics=("arbitrary",), vmem_limit_bytes=VMEM),
        interpret=INTERPRET,
    )(*toks, *outs, w_gate, w_up, w_down, inverse)


def input_kernel(n, *refs):
    ggus, (wg, wu, own, theirs) = refs[:n], refs[n:]
    hid = wg.shape[1]
    half = [r.shape[0] // 2 for r in ggus]
    ggu = jnp.concatenate(
        [r[:h] for r, h in zip(ggus, half)] + [r[h:] for r, h in zip(ggus, half)], axis=0
    )
    total = contract_cols(ggu[:, :hid], wg[...]) + contract_cols(ggu[:, hid:], wu[...])
    size = own.shape[0]
    own[...] = bf(total[:size])
    theirs[...] = bf(total[size:])


def input_gradient(ggus, w_gate, w_up):
    depth, hid = w_gate.shape
    block = min(1024, depth)
    size = sum(g.shape[0] for g in ggus) // 2
    wide = pl.BlockSpec((block, hid), lambda k: (k, 0))
    return pl.pallas_call(
        functools.partial(input_kernel, len(ggus)),
        name="input",
        grid=(depth // block,),
        in_specs=[pl.BlockSpec(g.shape, lambda k: (0, 0)) for g in ggus] + [wide, wide],
        out_specs=[pl.BlockSpec((size, block), lambda k: (0, k))] * 2,
        out_shape=[jax.ShapeDtypeStruct((size, depth), jnp.bfloat16)] * 2,
        compiler_params=pltpu.CompilerParams(
            dimension_semantics=("arbitrary",), vmem_limit_bytes=VMEM),
        interpret=INTERPRET,
    )(*ggus, w_gate, w_up)


def last_kernel(pieces, l0, l1, r0, r1, n0, n1, ratio, total, gate, up, down):
    block = pieces.shape[3]
    factor, divisor = ratio[...], total[...]
    for half, group in enumerate(((l0, r0, n0), (l1, r1, n1))):
        at = half * block
        for m, ref in enumerate((gate, up, down)):
            value = f32(pieces[half, m]) * factor
            for other in group:
                value += f32(other[m])
            value = value / divisor
            if m == 2:
                ref[:, at : at + block] = bf(value)
            else:
                ref[at : at + block, :] = bf(value.T)


def last_sum(pieces, others, ratio, total):
    count, _, hid, block = pieces.shape
    whole = [pl.BlockSpec(a.shape, lambda k, n=a.ndim: (0,) * n) for a in (*others, ratio, total)]
    shapes = [(2 * block, hid), (2 * block, hid), (hid, 2 * block)]
    return pl.pallas_call(
        last_kernel,
        name="last",
        grid=(1,),
        in_specs=[pl.BlockSpec((2, 3, hid, block), lambda k: (count // 2 - 1, 0, 0, 0))] + whole,
        out_specs=[pl.BlockSpec(shape, lambda k: (0, 0)) for shape in shapes],
        out_shape=[jax.ShapeDtypeStruct(shape, jnp.bfloat16) for shape in shapes],
        compiler_params=pltpu.CompilerParams(vmem_limit_bytes=VMEM),
        interpret=INTERPRET,
    )(pieces, *others, ratio, total)


def gradient_step(ggu_t, hid_t, toks, outs, write, moment):
    hid = hid_t.shape[0]
    features = jnp.concatenate([r[...] for r in toks], axis=0)
    upstream = jnp.concatenate([r[...] for r in outs], axis=0)
    first = jnp.dot(ggu_t[...], features, preferred_element_type=jnp.float32)
    second = jnp.dot(hid_t[...], upstream, preferred_element_type=jnp.float32)
    write(jnp.stack([bf(first[:hid]), bf(first[hid:]), bf(second)]))
    lanes = moment.shape[1]
    total = jnp.zeros(moment.shape, jnp.float32)
    for i in range(0, first.shape[1], lanes):
        a = first[:hid, i : i + lanes]
        b = first[hid:, i : i + lanes]
        c = second[:, i : i + lanes]
        total += a * a + b * b + c * c
    moment[...] += total


def to_one(step, alone, rest, value):
    for i, ref in enumerate(alone):
        @pl.when(step == i)
        def _():
            ref[...] = value

    if rest is not None:
        @pl.when(step >= len(alone))
        def _():
            rest[0] = value


def early_kernel(m, n, place, *refs):
    toks, outs = refs[:m], refs[m : 2 * m]
    ggus, hids = refs[2 * m : 2 * m + n], refs[2 * m + n : 2 * m + 2 * n]
    alone, (ggu_t, hid_t, moment) = refs[2 * m + 2 * n : -3], refs[-3:]
    step = pl.program_id(0)

    @pl.when(step == 0)
    def _():
        ggu = jnp.concatenate([r[...] for r in ggus], axis=0).astype(jnp.float32)
        ggu_t[...] = ggu.T.astype(ggu_t.dtype)
        hidden = jnp.concatenate([r[...] for r in hids], axis=0).astype(jnp.float32)
        hid_t[...] = hidden.T.astype(hid_t.dtype)
        moment[...] = jnp.zeros_like(moment)

    gradient_step(ggu_t, hid_t, toks, outs, functools.partial(to_one, step, alone, None), moment)


def late_kernel(m, depth, place, *refs):
    toks, outs = refs[:m], refs[m : 2 * m]
    ggu_t, hid_t, begun = refs[2 * m : 2 * m + 3]
    alone, (pieces, ratio, moment) = refs[2 * m + 3 : -3], refs[-3:]
    step = pl.program_id(0)

    @pl.when(step == 0)
    def _():
        moment[...] = begun[...]

    gradient_step(ggu_t, hid_t, toks, outs, functools.partial(to_one, step, alone, pieces), moment)

    @pl.when(step == pl.num_programs(0) - 1)
    def _():
        summed = jnp.sum(moment[...], axis=1, keepdims=True) / (3.0 * depth) + epsilon
        ratio[...] = jnp.broadcast_to(1.0 / summed, ratio.shape)


def same(array):
    zeros = (0,) * array.ndim
    return pl.BlockSpec(array.shape, lambda k, p: zeros)


def gradients_early(place, toks, outs, ggus, hids):
    n = len(ggus)
    depth, hid = toks[0].shape[1], hids[0].shape[1]
    rows = sum(t.shape[0] for t in toks)
    block = depth // len(PIECES)
    acts = [pl.BlockSpec((a.shape[0], block), lambda k, p: (0, p[k])) for a in (*toks, *outs)]
    out_shape = [
        *[jax.ShapeDtypeStruct((3, hid, block), jnp.bfloat16)] * EARLY,
        jax.ShapeDtypeStruct((2 * hid, rows), jnp.bfloat16),
        jax.ShapeDtypeStruct((hid, rows), jnp.bfloat16),
        jax.ShapeDtypeStruct((hid, min(128, block)), jnp.float32),
    ]
    return pl.pallas_call(
        functools.partial(early_kernel, len(toks), n),
        name="early",
        grid_spec=pltpu.PrefetchScalarGridSpec(
            num_scalar_prefetch=1,
            grid=(EARLY,),
            in_specs=acts + [same(a) for a in (*ggus, *hids)],
            out_specs=[same(a) for a in out_shape],
        ),
        out_shape=out_shape,
        compiler_params=pltpu.CompilerParams(
            dimension_semantics=("arbitrary",), vmem_limit_bytes=VMEM),
        interpret=INTERPRET,
    )(place, *toks, *outs, *ggus, *hids)


def gradients_late(place, toks, outs, ggu_t, hid_t, moment):
    depth, hid = toks[0].shape[1], hid_t.shape[0]
    block = depth // len(PIECES)
    late = len(PIECES) - EARLY
    alone = [jax.ShapeDtypeStruct((3, hid, block), jnp.bfloat16)] * ALONE
    acts = [pl.BlockSpec((a.shape[0], block), lambda k, p: (0, p[k])) for a in (*toks, *outs)]
    ratio = jax.ShapeDtypeStruct((hid, 128), jnp.float32)
    return pl.pallas_call(
        functools.partial(late_kernel, len(toks), depth),
        name="late",
        grid_spec=pltpu.PrefetchScalarGridSpec(
            num_scalar_prefetch=1,
            grid=(late,),
            in_specs=acts + [same(a) for a in (ggu_t, hid_t, moment)],
            out_specs=[same(a) for a in alone] + [
                pl.BlockSpec((1, 3, hid, block), lambda k, p: (jnp.maximum(k - ALONE, 0), 0, 0, 0)),
                same(ratio)],
            scratch_shapes=[pltpu.VMEM(moment.shape, jnp.float32)],
        ),
        out_shape=alone
        + [jax.ShapeDtypeStruct((late - ALONE, 3, hid, block), jnp.bfloat16), ratio],
        compiler_params=pltpu.CompilerParams(
            dimension_semantics=("arbitrary",), vmem_limit_bytes=VMEM),
        interpret=INTERPRET,
    )(place, *toks, *outs, ggu_t, hid_t, moment)


def contract_cols(left, right):
    return lax.dot_general(
        left, right, (((1,), (1,)), ((), ())), preferred_element_type=jnp.float32
    )


def bf(value):
    return value.astype(jnp.bfloat16)


def f32(value):
    return value.astype(jnp.float32)


def step(tokens, grad_out, doc_ids, w_gate, w_up, w_down):
    rows = tokens.shape[1]
    lang, fsdp = lax.axis_index("lang"), lax.axis_index("fsdp")
    z, y_lo = lang // 2, lang % 2
    y_hi, x, core = fsdp // 8, fsdp // 2 % 4, fsdp % 2

    t, o = {}, {}
    t[0], o[0] = tokens[0], grad_out[0]
    t[1], t[2], t[3] = to_x(t[0], 1), to_x(t[0], -1), to_y_half(t[0])
    o[1], o[2], o[3] = to_x(o[0], 1), to_x(o[0], -1), to_y_half(o[0])

    segment = doc_ids[0]
    same_document = (segment[:, None] == segment[None, :]).astype(jnp.float32)
    inverse = (1.0 / jnp.sum(same_document, axis=1)).reshape(16, rows)
    order = [(k, dc) for batch in BATCHES for dc in (0, 1) for k in batch]
    source = jnp.stack(
        [(y_hi ^ PLACES[k][1]) * 8 + (x + PLACES[k][0]) % 4 * 2 + (core ^ dc) for k, dc in order]
    )
    chosen = source[:, None] == jnp.arange(16)[None, :]
    inverse = jnp.sum(jnp.where(chosen[:, :, None], inverse[None], 0.0), axis=1)
    inverse = inverse.reshape(16 * rows, 1)
    target = jnp.stack([((z + dz) % 4 * 2 + (y_lo ^ dy)) * 2 + half for dz, dy, half in PIECES])
    target = target.astype(jnp.int32)

    t[4], t[5], t[6] = to_y_half(t[1]), to_x(t[3], -1), to_x(t[1], 1)
    o[5], o[4], o[6] = to_y_half(o[2]), to_x(o[3], 1), to_x(o[2], -1)

    t[7], o[7] = to_x(t[4], 1), to_x(o[5], -1)

    toks, outs, ggus, hids = [], [], [], []
    at = 0
    for batch in BATCHES:
        tok, out = [t[k] for k in batch], [o[k] for k in batch]
        tok += [to_core(v) for v in tok]
        out += [to_core(v) for v in out]
        size = rows * len(tok)
        ggu, hidden = forward(tok, out, w_gate, w_up, w_down, inverse[at : at + size])
        at += size
        toks += tok
        outs += out
        ggus.append(ggu)
        hids.append(hidden)
    near, near_p = input_gradient(ggus[:1], w_gate, w_up)
    near = bf(f32(near) + f32(to_core(near_p)))

    *first, ggu_t, hid_t, moment = gradients_early(target[:EARLY], toks, outs, ggus, hids)
    a, b = to_z(first[0], 1), to_z(first[1], -1)
    c, d = to_y_next(first[2]), to_y_next(first[3])
    far, far_p = input_gradient([after(ggus[1], moment), ggus[2]], w_gate, w_up)
    far_p, moment = lax.optimization_barrier((far_p, moment))
    far = bf(f32(far) + f32(to_core(far_p)))
    e, f, pieces, ratio = gradients_late(target[EARLY:], toks, outs, ggu_t, hid_t, moment)
    ratio = ratio[:, :1]
    from_low, from_high, from_next = to_z(ratio, 1), to_z(ratio, -1), to_y_next(ratio)

    def own(k):
        return f32(pieces[k - EARLY - ALONE]) * ratio[None]

    def theirs(value, factor):
        return f32(value) * factor[None]

    e, f = to_z(e, 1), to_z(f, -1)
    g = to_z(bf(own(6) + theirs(a, from_low)), 1)
    h = to_z(bf(own(7) + theirs(b, from_high)), -1)
    from_next = after(from_next, g, h)
    c, d, e, f = after(c, g, h), after(d, g, h), after(e, g, h), after(f, g, h)
    left_0 = to_z(bf(own(8) + theirs(e, from_low)), 1)
    left_1 = to_z(bf(own(9) + theirs(c, from_next)), 1)
    right_0 = to_z(bf(own(10) + theirs(d, from_next)), -1)
    right_1 = to_z(bf(own(11) + theirs(f, from_high)), -1)
    next_0 = to_y_next(bf(own(12) + f32(g)))
    next_1 = to_y_next(bf(own(13) + f32(h)))
    total = ratio + from_next
    total = total + to_z(total, 2)
    total = total + to_z(total, 1)
    others = (left_0, left_1, right_0, right_1, next_0, next_1)
    grad_gate, grad_up, grad_down = last_sum(pieces, others, ratio, total)

    part = [value[i : i + rows] for value in (near, far) for i in range(0, 4 * rows, rows)]
    far_0, far_1 = to_x(part[6], 1), to_x(part[7], -1)
    up_1, down_0 = to_x(part[5], 1), to_x(part[1], -1)
    up_0, down_1 = bf(f32(part[2]) + f32(far_0)), bf(f32(part[4]) + f32(far_1))
    up_0, down_1 = to_x(up_0, 1), to_x(down_1, -1)
    other = bf(f32(part[3]) + f32(up_1) + f32(down_1))
    other = to_y_half(other)
    grad_tokens = bf(f32(part[0]) + f32(up_0) + f32(down_0) + f32(other))[None]
    return (grad_tokens, grad_gate, grad_up, grad_down)


def solution(mesh):
    return jax.shard_map(
        step,
        mesh=mesh,
        in_specs=(
            P("lang", "fsdp", None),
            P("lang", "fsdp", None),
            P("lang", None),
            P(None, "fsdp"),
            P(None, "fsdp"),
            P("fsdp", None),
        ),
        out_specs=(
            P("lang", "fsdp", None),
            P("lang", "fsdp"),
            P("lang", "fsdp"),
            P("fsdp", "lang"),
        ),
        check_vma=False,
    )
```

profile of v0, /device:TPU:0, one launch (start us, length us, event | category | flops | bytes accessed | tf_op | source)
XLA Modules:
  0.0 368.1 jit_solution(3463144859724966038)
XLA Ops:
  0.6 1.7 collective-permute-start
  2.3 3.2 collective-permute-start.2
  5.8 1.6 collective-permute-start.8
  7.5 1.7 collective-permute-start.1
  9.1 12.2 %collective-permute-done.refs_1_ = bf16[48,8192]{1,0:T(8,128)(2,1)S(1)} collective-permute-done((bf16[48,8192]{1,0:T(8,128)(2,1)}, bf16[48,8192]{1,0:T(8,128)(2,1)S(1)}, u32[]{:S(2)}, u32[]{:S(2)}) %collective-permute-start) | collective-permute-done | bytes 786464 | tf_op jit(solution)/shard_map/ppermute | solution.py:40
  21.3 3.1 collective-permute-done.2.refs_3_
  24.4 1.5 collective-permute-start.7
  25.9 14.0 %collective-permute-done.9.refs_11_.refs_19_ = bf16[48,8192]{1,0:T(8,128)(2,1)S(1)} collective-permute-done((bf16[48,8192]{1,0:T(8,128)(2,1)}, bf16[48,8192]{1,0:T(8,128)(2,1)S(1)}, u32[]{:S(2)}, u32[]{:S(2)}) %collective-permute-start.9) | collective-permute-done | bytes 786464 | tf_op jit(solution)/shard_map/ppermute | solution.py:44
  39.9 3.3 collective-permute-start.15
  43.2 1.7 collective-permute-start.16
  45.2 1.5 collective-permute-start.21
  46.7 1.4 collective-permute-start.22
  48.1 13.9 %collective-permute-done.15.refs_0_.refs_8_ = bf16[48,8192]{1,0:T(8,128)(2,1)} collective-permute-done((bf16[48,8192]{1,0:T(8,128)(2,1)S(1)}, bf16[48,8192]{1,0:T(8,128)(2,1)}, u32[]{:S(2)}, u32[]{:S(2)}) %collective-permute-start.15) | collective-permute-done | bytes 786464 | tf_op jit(solution)/shard_map/ppermute | solution.py:44
  62.0 1.7 collective-permute-start.23
  63.7 2.9 collective-permute-done.17.refs_2_.refs_10_
  66.7 15.6 %collective-permute-done.21.refs_6_.refs_24_ = bf16[48,8192]{1,0:T(8,128)(2,1)S(1)} collective-permute-done((bf16[48,8192]{1,0:T(8,128)(2,1)S(1)}, bf16[48,8192]{1,0:T(8,128)(2,1)S(1)}, u32[]{:S(2)}, u32[]{:S(2)}) %collective-permute-start.21) | collective-permute-done | bytes 786464 | tf_op jit(solution)/shard_map/ppermute | solution.py:40
  83.4 1.1 collective-permute-done.6.refs_7_
  84.7 1.0 collective-permute-done.11.refs_13_.refs_21_
  85.8 1.0 collective-permute-done.12.refs_14_.refs_22_
  86.8 1.1 collective-permute-done.13.refs_15_.refs_23_
  88.0 2.2 collective-permute-start.29
  91.8 16.1 %collective-permute-done.27.refs_0_.refs_14_ = bf16[48,8192]{1,0:T(8,128)(2,1)} collective-permute-done((bf16[48,8192]{1,0:T(8,128)(2,1)}, bf16[48,8192]{1,0:T(8,128)(2,1)}, u32[]{:S(2)}, u32[]{:S(2)}) %collective-permute-start.27) | collective-permute-done | bytes 786464 | tf_op jit(solution)/shard_map/ppermute | solution.py:40
  109.3 0.8 slice.97.refs_15_
  110.0 0.8 slice.96.refs_19_
  112.2 13.9 %forward.3 = (bf16[384,512]{1,0:T(8,128)(2,1)}, bf16[384,256]{1,0:T(8,128)(2,1)}) custom-call(bf16[48,8192]{1,0:T(8,128)(2,1)} %bitcast.66, bf16[48,8192]{1,0:T(8,128)(2,1)} %copy-done, bf16[48,8192]{1,0:T(8,128)(2,1)} %copy-done.4, bf16[48,8192]{1,0:T(8,128)(2,1)} %copy-done.1, bf16[48,8192]{1,0:T(8,128)(2,1)} %copy-done.5, bf16[48,8192]{1,0:T(8,128)(2,1)} %copy-done.10, ...), custom_call_target="tpu_custom_call" | custom-call | tf_op jit(solution)/shard_map/forward/pallas_call | solution.py:102
  126.2 12.3 %forward.4 = (bf16[288,512]{1,0:T(8,128)(2,1)}, bf16[288,256]{1,0:T(8,128)(2,1)}) custom-call(bf16[48,8192]{1,0:T(8,128)(2,1)} %collective-permute-done.15.refs_0_.refs_8_, bf16[48,8192]{1,0:T(8,128)(2,1)} %collective-permute-done.16.refs_1_.refs_9_, bf16[48,8192]{1,0:T(8,128)(2,1)} %collective-permute-done.17.refs_2_.refs_10_, ...), custom_call_target="tpu_custom_call" | custom-call | tf_op jit(solution)/shard_map/forward/pallas_call | solution.py:102
  138.5 9.9 %forward.5 = (bf16[96,512]{1,0:T(8,128)(2,1)}, bf16[96,256]{1,0:T(8,128)(2,1)}) custom-call(bf16[48,8192]{1,0:T(8,128)(2,1)} %collective-permute-done.27.refs_0_.refs_14_, bf16[48,8192]{1,0:T(8,128)(2,1)} %collective-permute-done.28.refs_1_.refs_15_, bf16[48,8192]{1,0:T(8,128)(2,1)} %collective-permute-done.29.refs_2_.refs_30_, ...), custom_call_target="tpu_custom_call" | custom-call | tf_op jit(solution)/shard_map/forward/pallas_call | solution.py:102
  148.4 10.9 %early.1 = (bf16[3,256,512]{2,1,0:T(8,128)(2,1)}, bf16[3,256,512]{2,1,0:T(8,128)(2,1)}, bf16[3,256,512]{2,1,0:T(8,128)(2,1)}, bf16[3,256,512]{2,1,0:T(8,128)(2,1...) custom-call(s32[4]{0:T(128)} %pad_add_fusion.place, bf16[48,8192]{1,0:T(8,128)(2,1)} %bitcast.67, ...), custom_call_target="tpu_custom_call" | custom-call | tf_op jit(solution)/shard_map/early/pallas_call | solution.py:264
  159.3 9.8 %input.3 = (bf16[192,8192]{1,0:T(8,128)(2,1)}, bf16[192,8192]{1,0:T(8,128)(2,1)}) custom-call(bf16[288,512]{1,0:T(8,128)(2,1)} %get-tuple-element.45.refs_33_.refs_0_, bf16[96,512]{1,0:T(8,128)(2,1)} %get-tuple-element.40.refs_34_.refs_1_, bf16[8192,256]{1,0:T(8,128)(2,1)} %refs_2_.3, bf16[8192,256]{1,0:T(8,128)(2,1)} %refs_3_.1), custom_call_target="tpu_custom_call" | custom-call | tf_op jit(solution)/shard_map/input/pallas_call | solution.py:138
  169.1 4.1 %collective-permute-start.43 = (bf16[3,256,512]{2,1,0:T(8,128)(2,1)}, bf16[3,256,512]{2,1,0:T(8,128)(2,1)S(1)}, u32[]{:S(2)}, u32[]{:S(2)}) collective-permute-start(bf16[3,256,512]{2,1,0:T(8,128)(2,1)} %get-tuple-element.56), channel_id=1, source_target_pairs={{0,96},{16,112},{32,0},{48,16},{64,32},{80,48},{96,64},{112,80},{1... | collective-permute-start | bytes 2359304 | tf_op jit(solution)/shard_map/ppermute | solution.py:52
  173.8 23.2 %late.1 = (bf16[3,256,512]{2,1,0:T(8,128)(2,1)}, bf16[3,256,512]{2,1,0:T(8,128)(2,1)}, bf16[10,3,256,512]{3,2,1,0:T(8,128)(2,1)}, f32[256,128]{1,0:T(8,128)}) custom-call(s32[12]{0:T(128)} %stack.138.place, bf16[48,8192]{1,0:T(8,128)(2,1)} %bitcast.68, bf16[48,8192]{1,0:T(8,128)(2,1)} %copy-done, bf16[48,8192]{1,0:T(8,128)(2,1)} %copy-done.4, ...), custom_call_target="tpu_custom_call" | custom-call | tf_op jit(solution)/shard_map/late/pallas_call | solution.py:287
  197.0 1.0 slice_reduce_fusion
  198.1 3.3 collective-permute-start.44
  201.4 9.8 %input.2 = (bf16[192,8192]{1,0:T(8,128)(2,1)}, bf16[192,8192]{1,0:T(8,128)(2,1)}) custom-call(bf16[384,512]{1,0:T(8,128)(2,1)} %get-tuple-element.36.refs_0_.refs_32_, bf16[8192,256]{1,0:T(8,128)(2,1)} %refs_2_.3, bf16[8192,256]{1,0:T(8,128)(2,1)} %refs_3_.1), custom_call_target="tpu_custom_call" | custom-call | tf_op jit(solution)/shard_map/input/pallas_call | solution.py:138
  212.2 3.3 collective-permute-start.52
  215.5 1.4 collective-permute-start.47
  216.9 2.6 fusion.11
  219.9 3.1 add_convert_fusion
  223.2 10.5 %collective-permute-done.52 = bf16[3,256,512]{2,1,0:T(8,128)(2,1)S(1)} collective-permute-done((bf16[3,256,512]{2,1,0:T(8,128)(2,1)}, bf16[3,256,512]{2,1,0:T(8,128)(2,1)S(1)}, u32[]{:S(2)}, u32[]{:S(2)}) %collective-permute-start.52) | collective-permute-done | bytes 786464 | tf_op jit(solution)/shard_map/ppermute | solution.py:52
  233.7 3.0 collective-permute-start.36
  236.7 3.1 add_convert_fusion.1
  239.8 9.9 %collective-permute-done.45 = bf16[3,256,512]{2,1,0:T(8,128)(2,1)S(1)} collective-permute-done((bf16[3,256,512]{2,1,0:T(8,128)(2,1)S(1)}, bf16[3,256,512]{2,1,0:T(8,128)(2,1)S(1)}, u32[]{:S(2)}, u32[]{:S(2)}) %collective-permute-start.45) | collective-permute-done | bytes 786464 | tf_op jit(solution)/shard_map/ppermute | solution.py:52
  249.7 1.3 collective-permute-start.50
  251.1 2.5 collective-permute-done.42
  253.7 1.4 collective-permute-start.35
  255.3 2.0 collective-permute-start.37
  257.4 11.1 %collective-permute-done.50 = bf16[3,256,512]{2,1,0:T(8,128)(2,1)S(1)} collective-permute-done((bf16[3,256,512]{2,1,0:T(8,128)(2,1)S(1)}, bf16[3,256,512]{2,1,0:T(8,128)(2,1)S(1)}, u32[]{:S(2)}, u32[]{:S(2)}) %collective-permute-start.50) | collective-permute-done | bytes 786464 | tf_op jit(solution)/shard_map/ppermute | solution.py:56
  268.5 2.5 collective-permute-start.56
  271.0 2.5 collective-permute-done.39
  273.5 1.9 fusion.1
  275.5 0.9 slice.105
  276.6 3.2 collective-permute-start.51
  279.8 9.5 %collective-permute-done.35 = bf16[48,8192]{1,0:T(8,128)(2,1)S(1)} collective-permute-done((bf16[48,8192]{1,0:T(8,128)(2,1)S(1)}, bf16[48,8192]{1,0:T(8,128)(2,1)S(1)}, u32[]{:S(2)}, u32[]{:S(2)}) %collective-permute-start.35) | collective-permute-done | bytes 786464 | tf_op jit(solution)/shard_map/ppermute | solution.py:40
  289.3 2.9 collective-permute-start.53
  292.2 1.6 add_convert_fusion.5
  293.8 19.0 %collective-permute-done.57 = f32[256,1]{1,0:T(8,128)S(1)} collective-permute-done((f32[256,1]{1,0:T(8,128)S(1)}, f32[256,1]{1,0:T(8,128)S(1)}, u32[]{:S(2)}, u32[]{:S(2)}) %collective-permute-start.57) | collective-permute-done | bytes 1056 | tf_op jit(solution)/shard_map/ppermute | solution.py:52
  312.8 3.0 collective-permute-start.34
  315.7 1.4 collective-permute-start.54
  317.8 1.8 collective-permute-start.38
  320.3 16.0 %collective-permute-done.54.n0 = bf16[3,256,512]{2,1,0:T(8,128)(2,1)} collective-permute-done((bf16[3,256,512]{2,1,0:T(8,128)(2,1)S(1)}, bf16[3,256,512]{2,1,0:T(8,128)(2,1)}, u32[]{:S(2)}, u32[]{:S(2)}) %collective-permute-start.54) | collective-permute-done | bytes 786464 | tf_op jit(solution)/shard_map/ppermute | solution.py:56
  336.3 16.9 %collective-permute-done.55.n1 = bf16[3,256,512]{2,1,0:T(8,128)(2,1)} collective-permute-done((bf16[3,256,512]{2,1,0:T(8,128)(2,1)S(1)}, bf16[3,256,512]{2,1,0:T(8,128)(2,1)}, u32[]{:S(2)}, u32[]{:S(2)}) %collective-permute-start.55) | collective-permute-done | bytes 786464 | tf_op jit(solution)/shard_map/ppermute | solution.py:56
  353.1 5.1 %last.1 = (bf16[1024,256]{1,0:T(8,128)(2,1)}, bf16[1024,256]{1,0:T(8,128)(2,1)}, bf16[256,1024]{1,0:T(8,128)(2,1)}) custom-call(bf16[10,3,256,512]{3,2,1,0:T(8,128)(2,1)} %get-tuple-element.52.pieces, bf16[3,256,512]{2,1,0:T(8,128)(2,1)} %copy-done.20, bf16[3,256,512]{2,1,0:T(8,128)(2,1)} %copy-done.21, bf16[3,256,512]{2,1,0:T(8,128)(2,1)} %copy-done.22, ...), custom_call_target="tpu_custom_call" | custom-call | tf_op jit(solution)/shard_map/last/pallas_call | solution.py:171
  358.2 7.0 %collective-permute-done.38 = bf16[48,8192]{1,0:T(8,128)(2,1)} collective-permute-done((bf16[48,8192]{1,0:T(8,128)(2,1)}, bf16[48,8192]{1,0:T(8,128)(2,1)}, u32[]{:S(2)}, u32[]{:S(2)}) %collective-permute-start.38) | collective-permute-done | bytes 786464 | tf_op jit(solution)/shard_map/ppermute | solution.py:44
  365.2 2.9 fusion.16
  (151 shorter events, 10.4 us)
Async XLA Ops:
  0.6 20.7 %collective-permute-start = (bf16[48,8192]{1,0:T(8,128)(2,1)}, bf16[48,8192]{1,0:T(8,128)(2,1)S(1)}, u32[]{:S(2)}, u32[]{:S(2)}) collective-permute-start(bf16[48,8192]{1,0:T(8,128)(2,1)} %bitcast.62), channel_id=1, source_target_pairs={{0,2},{1,3},{2,4},{3,5},{4,6},{5,7},{6,0},{7,1},{8,10},{9,11},{10,... | collective-permute-start | bytes 2359304 | tf_op jit(solution)/shard_map/ppermute | solution.py:40
  2.3 22.1 %collective-permute-start.2 = (bf16[48,8192]{1,0:T(8,128)(2,1)}, bf16[48,8192]{1,0:T(8,128)(2,1)S(1)}, u32[]{:S(2)}, u32[]{:S(2)}) collective-permute-start(bf16[48,8192]{1,0:T(8,128)(2,1)} %bitcast.63), channel_id=1, source_target_pairs={{0,8},{1,9},{2,10},{3,11},{4,12},{5,13},{6,14},{7,15},{8,0},{9,1},... | collective-permute-start | bytes 2359304 | tf_op jit(solution)/shard_map/ppermute | solution.py:44
  5.5 34.4 %collective-permute-start.9 = (bf16[48,8192]{1,0:T(8,128)(2,1)}, bf16[48,8192]{1,0:T(8,128)(2,1)S(1)}, u32[]{:S(2)}, u32[]{:S(2)}) collective-permute-start(bf16[48,8192]{1,0:T(8,128)(2,1)} %bitcast.69), channel_id=1, source_target_pairs={{0,8},{1,9},{2,10},{3,11},{4,12},{5,13},{6,14},{7,15},{8,0},{9,1},... | collective-permute-start | bytes 2359304 | tf_op jit(solution)/shard_map/ppermute | solution.py:44
  5.8 34.1 %collective-permute-start.8 = (bf16[48,8192]{1,0:T(8,128)(2,1)}, bf16[48,8192]{1,0:T(8,128)(2,1)S(1)}, u32[]{:S(2)}, u32[]{:S(2)}) collective-permute-start(bf16[48,8192]{1,0:T(8,128)(2,1)} %bitcast.70), channel_id=1, source_target_pairs={{0,6},{1,7},{2,0},{3,1},{4,2},{5,3},{6,4},{7,5},{8,14},{9,15},{10,... | collective-permute-start | bytes 2359304 | tf_op jit(solution)/shard_map/ppermute | solution.py:40
  7.5 35.7 %collective-permute-start.1 = (bf16[48,8192]{1,0:T(8,128)(2,1)}, bf16[48,8192]{1,0:T(8,128)(2,1)S(1)}, u32[]{:S(2)}, u32[]{:S(2)}) collective-permute-start(bf16[48,8192]{1,0:T(8,128)(2,1)} %bitcast.64), channel_id=1, source_target_pairs={{0,6},{1,7},{2,0},{3,1},{4,2},{5,3},{6,4},{7,5},{8,14},{9,15},{10,... | collective-permute-start | bytes 2359304 | tf_op jit(solution)/shard_map/ppermute | solution.py:40
  21.3 90.9 %copy-start = (bf16[48,8192]{1,0:T(8,128)(2,1)}, bf16[48,8192]{1,0:T(8,128)(2,1)S(1)}, u32[]{:S(2)}) copy-start(bf16[48,8192]{1,0:T(8,128)(2,1)S(1)} %collective-permute-done.refs_1_) | copy-start | bytes 2359300
  21.3 23.6 %collective-permute-start.3 = (bf16[48,8192]{1,0:T(8,128)(2,1)}, bf16[48,8192]{1,0:T(8,128)(2,1)S(1)}, u32[]{:S(2)}, u32[]{:S(2)}) collective-permute-start(bf16[48,8192]{1,0:T(8,128)(2,1)} %bitcast.65), channel_id=1, source_target_pairs={{0,1},{1,0},{2,3},{3,2},{4,5},{5,4},{6,7},{7,6},{8,9},{9,8},{10,11... | collective-permute-start | bytes 2359304 | tf_op jit(solution)/shard_map/ppermute | solution.py:48
  24.4 87.8 %copy-start.1 = (bf16[48,8192]{1,0:T(8,128)(2,1)}, bf16[48,8192]{1,0:T(8,128)(2,1)S(1)}, u32[]{:S(2)}) copy-start(bf16[48,8192]{1,0:T(8,128)(2,1)S(1)} %collective-permute-done.2.refs_3_) | copy-start | bytes 2359300
  24.4 20.8 %collective-permute-start.7 = (bf16[48,8192]{1,0:T(8,128)(2,1)}, bf16[48,8192]{1,0:T(8,128)(2,1)S(1)}, u32[]{:S(2)}, u32[]{:S(2)}) collective-permute-start(bf16[48,8192]{1,0:T(8,128)(2,1)} %bitcast.71), channel_id=1, source_target_pairs={{0,2},{1,3},{2,4},{3,5},{4,6},{5,7},{6,0},{7,1},{8,10},{9,11},{10,... | collective-permute-start | bytes 2359304 | tf_op jit(solution)/shard_map/ppermute | solution.py:40
  39.9 72.3 %copy-start.2 = (bf16[48,8192]{1,0:T(8,128)(2,1)}, bf16[48,8192]{1,0:T(8,128)(2,1)S(1)}, u32[]{:S(2)}) copy-start(bf16[48,8192]{1,0:T(8,128)(2,1)S(1)} %collective-permute-done.9.refs_11_.refs_19_) | copy-start | bytes 2359300
  39.9 6.8 %collective-permute-start.10 = (bf16[48,8192]{1,0:T(8,128)(2,1)}, bf16[48,8192]{1,0:T(8,128)(2,1)S(1)}, u32[]{:S(2)}, u32[]{:S(2)}) collective-permute-start(bf16[48,8192]{1,0:T(8,128)(2,1)} %bitcast.72), channel_id=1, source_target_pairs={{0,1},{1,0},{2,3},{3,2},{4,5},{5,4},{6,7},{7,6},{8,9},{9,8},{10,11... | collective-permute-start | bytes 2359304 | tf_op jit(solution)/shard_map/ppermute | solution.py:48
  39.9 72.3 %copy-start.3 = (bf16[48,8192]{1,0:T(8,128)(2,1)}, bf16[48,8192]{1,0:T(8,128)(2,1)S(1)}, u32[]{:S(2)}) copy-start(bf16[48,8192]{1,0:T(8,128)(2,1)S(1)} %collective-permute-done.8.refs_10_.refs_18_) | copy-start | bytes 2359300
  39.9 22.1 %collective-permute-start.15 = (bf16[48,8192]{1,0:T(8,128)(2,1)S(1)}, bf16[48,8192]{1,0:T(8,128)(2,1)}, u32[]{:S(2)}, u32[]{:S(2)}) collective-permute-start(bf16[48,8192]{1,0:T(8,128)(2,1)S(1)} %collective-permute-done.refs_1_), channel_id=1, source_target_pairs={{0,8},{1,9},{2,10},{3,11},{4,12},{5,13},{6,14},{7,15},{8,0},{9,1},... | collective-permute-start | bytes 2359304 | tf_op jit(solution)/shard_map/ppermute | solution.py:44
  43.2 20.6 %collective-permute-start.16 = (bf16[48,8192]{1,0:T(8,128)(2,1)S(1)}, bf16[48,8192]{1,0:T(8,128)(2,1)}, u32[]{:S(2)}, u32[]{:S(2)}) collective-permute-start(bf16[48,8192]{1,0:T(8,128)(2,1)S(1)} %collective-permute-done.2.refs_3_), channel_id=1, source_target_pairs={{0,6},{1,7},{2,0},{3,1},{4,2},{5,3},{6,4},{7,5},{8,14},{9,15},{10,... | collective-permute-start | bytes 2359304 | tf_op jit(solution)/shard_map/ppermute | solution.py:40
  44.9 45.2 %copy-start.5 = (bf16[48,8192]{1,0:T(8,128)(2,1)}, bf16[48,8192]{1,0:T(8,128)(2,1)S(1)}, u32[]{:S(2)}) copy-start(bf16[48,8192]{1,0:T(8,128)(2,1)S(1)} %collective-permute-done.3.refs_4_) | copy-start | bytes 2359300
  44.9 21.7 %collective-permute-start.17 = (bf16[48,8192]{1,0:T(8,128)(2,1)S(1)}, bf16[48,8192]{1,0:T(8,128)(2,1)}, u32[]{:S(2)}, u32[]{:S(2)}) collective-permute-start(bf16[48,8192]{1,0:T(8,128)(2,1)S(1)} %collective-permute-done.refs_1_), channel_id=1, source_target_pairs={{0,2},{1,3},{2,4},{3,5},{4,6},{5,7},{6,0},{7,1},{8,10},{9,11},{10,... | collective-permute-start | bytes 2359304 | tf_op jit(solution)/shard_map/ppermute | solution.py:40
  45.2 37.1 %collective-permute-start.21 = (bf16[48,8192]{1,0:T(8,128)(2,1)S(1)}, bf16[48,8192]{1,0:T(8,128)(2,1)S(1)}, u32[]{:S(2)}, u32[]{:S(2)}) collective-permute-start(bf16[48,8192]{1,0:T(8,128)(2,1)S(1)} %collective-permute-done.9.refs_11_.refs_19_), channel_id=1, source_target_pairs={{0,2},{1,3},{2,4},{3,5},{4,6},{5,7},{6,0},{7,1},{8,10},{9,11},{10,... | collective-permute-start | bytes 2359304 | tf_op jit(solution)/shard_map/ppermute | solution.py:40
  46.7 35.6 %collective-permute-start.22 = (bf16[48,8192]{1,0:T(8,128)(2,1)S(1)}, bf16[48,8192]{1,0:T(8,128)(2,1)}, u32[]{:S(2)}, u32[]{:S(2)}) collective-permute-start(bf16[48,8192]{1,0:T(8,128)(2,1)S(1)} %collective-permute-done.8.refs_10_.refs_18_), channel_id=1, source_target_pairs={{0,8},{1,9},{2,10},{3,11},{4,12},{5,13},{6,14},{7,15},{8,0},{9,1},... | collective-permute-start | bytes 2359304 | tf_op jit(solution)/shard_map/ppermute | solution.py:44
  62.0 20.8 %collective-permute-start.23 = (bf16[48,8192]{1,0:T(8,128)(2,1)S(1)}, bf16[48,8192]{1,0:T(8,128)(2,1)S(1)}, u32[]{:S(2)}, u32[]{:S(2)}) collective-permute-start(bf16[48,8192]{1,0:T(8,128)(2,1)S(1)} %collective-permute-done.8.refs_10_.refs_18_), channel_id=1, source_target_pairs={{0,6},{1,7},{2,0},{3,1},{4,2},{5,3},{6,4},{7,5},{8,14},{9,15},{10,... | collective-permute-start | bytes 2359304 | tf_op jit(solution)/shard_map/ppermute | solution.py:40
  63.7 19.2 %collective-permute-start.4 = (bf16[48,8192]{1,0:T(8,128)(2,1)S(1)}, bf16[48,8192]{1,0:T(8,128)(2,1)S(1)}, u32[]{:S(2)}, u32[]{:S(2)}) collective-permute-start(bf16[48,8192]{1,0:T(8,128)(2,1)S(1)} %collective-permute-done.refs_1_), channel_id=1, source_target_pairs={{0,1},{1,0},{2,3},{3,2},{4,5},{5,4},{6,7},{7,6},{8,9},{9,8},{10,11... | collective-permute-start | bytes 2359304 | tf_op jit(solution)/shard_map/ppermute | solution.py:48
  66.7 16.7 %collective-permute-start.5 = (bf16[48,8192]{1,0:T(8,128)(2,1)S(1)}, bf16[48,8192]{1,0:T(8,128)(2,1)S(1)}, u32[]{:S(2)}, u32[]{:S(2)}) collective-permute-start(bf16[48,8192]{1,0:T(8,128)(2,1)S(1)} %collective-permute-done.1.refs_2_), channel_id=1, source_target_pairs={{0,1},{1,0},{2,3},{3,2},{4,5},{5,4},{6,7},{7,6},{8,9},{9,8},{10,11... | collective-permute-start | bytes 2359304 | tf_op jit(solution)/shard_map/ppermute | solution.py:48
  82.3 2.3 collective-permute-start.6
  82.3 3.4 collective-permute-start.11
  82.8 4.0 %collective-permute-start.12 = (bf16[48,8192]{1,0:T(8,128)(2,1)S(1)}, bf16[48,8192]{1,0:T(8,128)(2,1)S(1)}, u32[]{:S(2)}, u32[]{:S(2)}) collective-permute-start(bf16[48,8192]{1,0:T(8,128)(2,1)S(1)} %collective-permute-done.8.refs_10_.refs_18_), channel_id=1, source_target_pairs={{0,1},{1,0},{2,3},{3,2},{4,5},{5,4},{6,7},{7,6},{8,9},{9,8},{10,11... | collective-permute-start | bytes 2359304 | tf_op jit(solution)/shard_map/ppermute | solution.py:48
  82.9 5.0 %collective-permute-start.13 = (bf16[48,8192]{1,0:T(8,128)(2,1)S(1)}, bf16[48,8192]{1,0:T(8,128)(2,1)S(1)}, u32[]{:S(2)}, u32[]{:S(2)}) collective-permute-start(bf16[48,8192]{1,0:T(8,128)(2,1)S(1)} %collective-permute-done.9.refs_11_.refs_19_), channel_id=1, source_target_pairs={{0,1},{1,0},{2,3},{3,2},{4,5},{5,4},{6,7},{7,6},{8,9},{9,8},{10,11... | collective-permute-start | bytes 2359304 | tf_op jit(solution)/shard_map/ppermute | solution.py:48
  83.3 7.8 %collective-permute-start.18 = (bf16[48,8192]{1,0:T(8,128)(2,1)}, bf16[48,8192]{1,0:T(8,128)(2,1)}, u32[]{:S(2)}, u32[]{:S(2)}) collective-permute-start(bf16[48,8192]{1,0:T(8,128)(2,1)} %collective-permute-done.15.refs_0_.refs_8_), channel_id=1, source_target_pairs={{0,1},{1,0},{2,3},{3,2},{4,5},{5,4},{6,7},{7,6},{8,9},{9,8},{10,11... | collective-permute-start | bytes 2359304 | tf_op jit(solution)/shard_map/ppermute | solution.py:48
  84.6 6.6 %collective-permute-start.19 = (bf16[48,8192]{1,0:T(8,128)(2,1)}, bf16[48,8192]{1,0:T(8,128)(2,1)}, u32[]{:S(2)}, u32[]{:S(2)}) collective-permute-start(bf16[48,8192]{1,0:T(8,128)(2,1)} %collective-permute-done.16.refs_1_.refs_9_), channel_id=1, source_target_pairs={{0,1},{1,0},{2,3},{3,2},{4,5},{5,4},{6,7},{7,6},{8,9},{9,8},{10,11... | collective-permute-start | bytes 2359304 | tf_op jit(solution)/shard_map/ppermute | solution.py:48
  85.7 6.0 %collective-permute-start.20 = (bf16[48,8192]{1,0:T(8,128)(2,1)}, bf16[48,8192]{1,0:T(8,128)(2,1)}, u32[]{:S(2)}, u32[]{:S(2)}) collective-permute-start(bf16[48,8192]{1,0:T(8,128)(2,1)} %collective-permute-done.17.refs_2_.refs_10_), channel_id=1, source_target_pairs={{0,1},{1,0},{2,3},{3,2},{4,5},{5,4},{6,7},{7,6},{8,9},{9,8},{10,11... | collective-permute-start | bytes 2359304 | tf_op jit(solution)/shard_map/ppermute | solution.py:48
  86.8 21.1 %collective-permute-start.27 = (bf16[48,8192]{1,0:T(8,128)(2,1)}, bf16[48,8192]{1,0:T(8,128)(2,1)}, u32[]{:S(2)}, u32[]{:S(2)}) collective-permute-start(bf16[48,8192]{1,0:T(8,128)(2,1)} %collective-permute-done.15.refs_0_.refs_8_), channel_id=1, source_target_pairs={{0,2},{1,3},{2,4},{3,5},{4,6},{5,7},{6,0},{7,1},{8,10},{9,11},{10,... | collective-permute-start | bytes 2359304 | tf_op jit(solution)/shard_map/ppermute | solution.py:40
  88.0 20.0 %collective-permute-start.29 = (bf16[48,8192]{1,0:T(8,128)(2,1)}, bf16[48,8192]{1,0:T(8,128)(2,1)}, u32[]{:S(2)}, u32[]{:S(2)}) collective-permute-start(bf16[48,8192]{1,0:T(8,128)(2,1)} %collective-permute-done.22.refs_7_.refs_25_), channel_id=1, source_target_pairs={{0,6},{1,7},{2,0},{3,1},{4,2},{5,3},{6,4},{7,5},{8,14},{9,15},{10,... | collective-permute-start | bytes 2359304 | tf_op jit(solution)/shard_map/ppermute | solution.py:40
  91.1 35.0 %collective-permute-start.25 = (bf16[48,8192]{1,0:T(8,128)(2,1)}, bf16[48,8192]{1,0:T(8,128)(2,1)}, u32[]{:S(2)}, u32[]{:S(2)}) collective-permute-start(bf16[48,8192]{1,0:T(8,128)(2,1)} %collective-permute-done.22.refs_7_.refs_25_), channel_id=1, source_target_pairs={{0,1},{1,0},{2,3},{3,2},{4,5},{5,4},{6,7},{7,6},{8,9},{9,8},{10,11... | collective-permute-start | bytes 2359304 | tf_op jit(solution)/shard_map/ppermute | solution.py:48
  91.2 34.9 %collective-permute-start.24 = (bf16[48,8192]{1,0:T(8,128)(2,1)}, bf16[48,8192]{1,0:T(8,128)(2,1)}, u32[]{:S(2)}, u32[]{:S(2)}) collective-permute-start(bf16[48,8192]{1,0:T(8,128)(2,1)} %copy-done.8), channel_id=1, source_target_pairs={{0,1},{1,0},{2,3},{3,2},{4,5},{5,4},{6,7},{7,6},{8,9},{9,8},{10,11... | collective-permute-start | bytes 2359304 | tf_op jit(solution)/shard_map/ppermute | solution.py:48
  91.7 34.4 %collective-permute-start.26 = (bf16[48,8192]{1,0:T(8,128)(2,1)}, bf16[48,8192]{1,0:T(8,128)(2,1)}, u32[]{:S(2)}, u32[]{:S(2)}) collective-permute-start(bf16[48,8192]{1,0:T(8,128)(2,1)} %copy-done.9), channel_id=1, source_target_pairs={{0,1},{1,0},{2,3},{3,2},{4,5},{5,4},{6,7},{7,6},{8,9},{9,8},{10,11... | collective-permute-start | bytes 2359304 | tf_op jit(solution)/shard_map/ppermute | solution.py:48
  107.9 30.5 %collective-permute-start.28 = (bf16[48,8192]{1,0:T(8,128)(2,1)}, bf16[48,8192]{1,0:T(8,128)(2,1)}, u32[]{:S(2)}, u32[]{:S(2)}) collective-permute-start(bf16[48,8192]{1,0:T(8,128)(2,1)} %collective-permute-done.27.refs_0_.refs_14_), channel_id=1, source_target_pairs={{0,1},{1,0},{2,3},{3,2},{4,5},{5,4},{6,7},{7,6},{8,9},{9,8},{10,11... | collective-permute-start | bytes 2359304 | tf_op jit(solution)/shard_map/ppermute | solution.py:48
  107.9 30.5 %collective-permute-start.30 = (bf16[48,8192]{1,0:T(8,128)(2,1)}, bf16[48,8192]{1,0:T(8,128)(2,1)}, u32[]{:S(2)}, u32[]{:S(2)}) collective-permute-start(bf16[48,8192]{1,0:T(8,128)(2,1)} %collective-permute-done.29.refs_2_.refs_30_), channel_id=1, source_target_pairs={{0,1},{1,0},{2,3},{3,2},{4,5},{5,4},{6,7},{7,6},{8,9},{9,8},{10,11... | collective-permute-start | bytes 2359304 | tf_op jit(solution)/shard_map/ppermute | solution.py:48
  169.1 50.4 %collective-permute-start.31 = (bf16[192,8192]{1,0:T(8,128)(2,1)}, bf16[192,8192]{1,0:T(8,128)(2,1)}, u32[]{:S(2)}, u32[]{:S(2)}) collective-permute-start(bf16[192,8192]{1,0:T(8,128)(2,1)} %get-tuple-element.48), channel_id=1, source_target_pairs={{0,1},{1,0},{2,3},{3,2},{4,5},{5,4},{6,7},{7,6},{8,9},{9,8},{10,11... | collective-permute-start | bytes 9437192 | tf_op jit(solution)/shard_map/ppermute | solution.py:48
  169.1 43.1 %collective-permute-start.43 = (bf16[3,256,512]{2,1,0:T(8,128)(2,1)}, bf16[3,256,512]{2,1,0:T(8,128)(2,1)S(1)}, u32[]{:S(2)}, u32[]{:S(2)}) collective-permute-start(bf16[3,256,512]{2,1,0:T(8,128)(2,1)} %get-tuple-element.56), channel_id=1, source_target_pairs={{0,96},{16,112},{32,0},{48,16},{64,32},{80,48},{96,64},{112,80},{1... | collective-permute-start | bytes 2359304 | tf_op jit(solution)/shard_map/ppermute | solution.py:52
  173.2 42.3 %collective-permute-start.40 = (bf16[3,256,512]{2,1,0:T(8,128)(2,1)S(1)}, bf16[3,256,512]{2,1,0:T(8,128)(2,1)S(1)}, u32[]{:S(2)}, u32[]{:S(2)}) collective-permute-start(bf16[3,256,512]{2,1,0:T(8,128)(2,1)S(1)} %copy-done.27), channel_id=1, source_target_pairs={{0,32},{16,48},{32,64},{48,80},{64,96},{80,112},{96,0},{112,16},{1... | collective-permute-start | bytes 2359304 | tf_op jit(solution)/shard_map/ppermute | solution.py:52
  198.1 13.1 %collective-permute-start.44 = (f32[256,1]{1,0:T(8,128)S(1)}, f32[256,1]{1,0:T(8,128)S(1)}, u32[]{:S(2)}, u32[]{:S(2)}) collective-permute-start(f32[256,1]{1,0:T(8,128)S(1)} %get-tuple-element.86.ratio), channel_id=1, source_target_pairs={{0,96},{16,112},{32,0},{48,16},{64,32},{80,48},{96,64},{112,80},{1... | collective-permute-start | bytes 3080 | tf_op jit(solution)/shard_map/ppermute | solution.py:52
  201.4 9.9 %collective-permute-start.41 = (f32[256,1]{1,0:T(8,128)S(1)}, f32[256,1]{1,0:T(8,128)S(1)}, u32[]{:S(2)}, u32[]{:S(2)}) collective-permute-start(f32[256,1]{1,0:T(8,128)S(1)} %get-tuple-element.86.ratio), channel_id=1, source_target_pairs={{0,32},{16,48},{32,64},{48,80},{64,96},{80,112},{96,0},{112,16},{1... | collective-permute-start | bytes 3080 | tf_op jit(solution)/shard_map/ppermute | solution.py:52
  211.1 22.6 %collective-permute-start.14 = (bf16[192,8192]{1,0:T(8,128)(2,1)}, bf16[192,8192]{1,0:T(8,128)(2,1)}, u32[]{:S(2)}, u32[]{:S(2)}) collective-permute-start(bf16[192,8192]{1,0:T(8,128)(2,1)} %get-tuple-element.38), channel_id=1, source_target_pairs={{0,1},{1,0},{2,3},{3,2},{4,5},{5,4},{6,7},{7,6},{8,9},{9,8},{10,11... | collective-permute-start | bytes 9437192 | tf_op jit(solution)/shard_map/ppermute | solution.py:48
  211.3 42.3 %collective-permute-start.48 = (f32[256,1]{1,0:T(8,128)S(1)}, f32[256,1]{1,0:T(8,128)S(1)}, u32[]{:S(2)}, u32[]{:S(2)}) collective-permute-start(f32[256,1]{1,0:T(8,128)S(1)} %get-tuple-element.86.ratio), channel_id=1, source_target_pairs={{0,16},{16,0},{32,48},{48,32},{64,80},{80,64},{96,112},{112,96},{1... | collective-permute-start | bytes 3080 | tf_op jit(solution)/shard_map/ppermute | solution.py:56
  212.2 21.5 %collective-permute-start.52 = (bf16[3,256,512]{2,1,0:T(8,128)(2,1)}, bf16[3,256,512]{2,1,0:T(8,128)(2,1)S(1)}, u32[]{:S(2)}, u32[]{:S(2)}) collective-permute-start(bf16[3,256,512]{2,1,0:T(8,128)(2,1)} %get-tuple-element.63), channel_id=1, source_target_pairs={{0,96},{16,112},{32,0},{48,16},{64,32},{80,48},{96,64},{112,80},{1... | collective-permute-start | bytes 2359304 | tf_op jit(solution)/shard_map/ppermute | solution.py:52
  215.5 38.2 %collective-permute-start.47 = (bf16[3,256,512]{2,1,0:T(8,128)(2,1)}, bf16[3,256,512]{2,1,0:T(8,128)(2,1)S(1)}, u32[]{:S(2)}, u32[]{:S(2)}) collective-permute-start(bf16[3,256,512]{2,1,0:T(8,128)(2,1)} %get-tuple-element.58), channel_id=1, source_target_pairs={{0,16},{16,0},{32,48},{48,32},{64,80},{80,64},{96,112},{112,96},{1... | collective-permute-start | bytes 2359304 | tf_op jit(solution)/shard_map/ppermute | solution.py:56
  219.5 30.2 %collective-permute-start.45 = (bf16[3,256,512]{2,1,0:T(8,128)(2,1)S(1)}, bf16[3,256,512]{2,1,0:T(8,128)(2,1)S(1)}, u32[]{:S(2)}, u32[]{:S(2)}) collective-permute-start(bf16[3,256,512]{2,1,0:T(8,128)(2,1)S(1)} %get-tuple-element.76), channel_id=1, source_target_pairs={{0,96},{16,112},{32,0},{48,16},{64,32},{80,48},{96,64},{112,80},{1... | collective-permute-start | bytes 2359304 | tf_op jit(solution)/shard_map/ppermute | solution.py:52
  223.0 50.5 %slice-start = ((s8[7864320]{0:T(1024)(128)(4,1)}), s8[4194304]{0:T(1024)(128)(4,1)S(1)}, s32[]{:S(2)}) async-start(s8[7864320]{0:T(1024)(128)(4,1)} %bitcast.60), calls=%async_computation | async-start | bytes 8388608
  233.7 19.9 %collective-permute-start.42 = (bf16[3,256,512]{2,1,0:T(8,128)(2,1)S(1)}, bf16[3,256,512]{2,1,0:T(8,128)(2,1)S(1)}, u32[]{:S(2)}, u32[]{:S(2)}) collective-permute-start(bf16[3,256,512]{2,1,0:T(8,128)(2,1)S(1)} %get-tuple-element.77), channel_id=1, source_target_pairs={{0,32},{16,48},{32,64},{48,80},{64,96},{80,112},{96,0},{112,16},{1... | collective-permute-start | bytes 2359304 | tf_op jit(solution)/shard_map/ppermute | solution.py:52
  233.7 21.4 %collective-permute-start.36 = (bf16[48,8192]{1,0:T(8,128)(2,1)S(1)}, bf16[48,8192]{1,0:T(8,128)(2,1)S(1)}, u32[]{:S(2)}, u32[]{:S(2)}) collective-permute-start(bf16[48,8192]{1,0:T(8,128)(2,1)S(1)} %get-tuple-element.81), channel_id=1, source_target_pairs={{0,6},{1,7},{2,0},{3,1},{4,2},{5,3},{6,4},{7,5},{8,14},{9,15},{10,... | collective-permute-start | bytes 2359304 | tf_op jit(solution)/shard_map/ppermute | solution.py:40
  249.7 18.8 %collective-permute-start.50 = (bf16[3,256,512]{2,1,0:T(8,128)(2,1)S(1)}, bf16[3,256,512]{2,1,0:T(8,128)(2,1)S(1)}, u32[]{:S(2)}, u32[]{:S(2)}) collective-permute-start(bf16[3,256,512]{2,1,0:T(8,128)(2,1)S(1)} %copy-done.25), channel_id=1, source_target_pairs={{0,16},{16,0},{32,48},{48,32},{64,80},{80,64},{96,112},{112,96},{1... | collective-permute-start | bytes 2359304 | tf_op jit(solution)/shard_map/ppermute | solution.py:56
  253.6 19.9 %collective-permute-start.39 = (bf16[3,256,512]{2,1,0:T(8,128)(2,1)S(1)}, bf16[3,256,512]{2,1,0:T(8,128)(2,1)S(1)}, u32[]{:S(2)}, u32[]{:S(2)}) collective-permute-start(bf16[3,256,512]{2,1,0:T(8,128)(2,1)S(1)} %copy-done.26), channel_id=1, source_target_pairs={{0,32},{16,48},{32,64},{48,80},{64,96},{80,112},{96,0},{112,16},{1... | collective-permute-start | bytes 2359304 | tf_op jit(solution)/shard_map/ppermute | solution.py:52
  253.7 22.9 %collective-permute-start.32 = (bf16[48,8192]{1,0:T(8,128)(2,1)S(1)}, bf16[48,8192]{1,0:T(8,128)(2,1)S(1)}, u32[]{:S(2)}, u32[]{:S(2)}) collective-permute-start(bf16[48,8192]{1,0:T(8,128)(2,1)S(1)} %get-tuple-element.80), channel_id=1, source_target_pairs={{0,2},{1,3},{2,4},{3,5},{4,6},{5,7},{6,0},{7,1},{8,10},{9,11},{10,... | collective-permute-start | bytes 2359304 | tf_op jit(solution)/shard_map/ppermute | solution.py:40
  253.7 35.5 %collective-permute-start.35 = (bf16[48,8192]{1,0:T(8,128)(2,1)S(1)}, bf16[48,8192]{1,0:T(8,128)(2,1)S(1)}, u32[]{:S(2)}, u32[]{:S(2)}) collective-permute-start(bf16[48,8192]{1,0:T(8,128)(2,1)S(1)} %get-tuple-element.82), channel_id=1, source_target_pairs={{0,2},{1,3},{2,4},{3,5},{4,6},{5,7},{6,0},{7,1},{8,10},{9,11},{10,... | collective-permute-start | bytes 2359304 | tf_op jit(solution)/shard_map/ppermute | solution.py:40
  255.3 36.8 %collective-permute-start.37 = (bf16[48,8192]{1,0:T(8,128)(2,1)S(1)}, bf16[48,8192]{1,0:T(8,128)(2,1)S(1)}, u32[]{:S(2)}, u32[]{:S(2)}) collective-permute-start(bf16[48,8192]{1,0:T(8,128)(2,1)S(1)} %add_convert_fusion.4), channel_id=1, source_target_pairs={{0,6},{1,7},{2,0},{3,1},{4,2},{5,3},{6,4},{7,5},{8,14},{9,15},{10,... | collective-permute-start | bytes 2359304 | tf_op jit(solution)/shard_map/ppermute | solution.py:40
  268.5 7.9 %collective-permute-start.56 = (f32[256,1]{1,0:T(8,128)S(1)}, f32[256,1]{1,0:T(8,128)S(1)}, u32[]{:S(2)}, u32[]{:S(2)}) collective-permute-start(f32[256,1]{1,0:T(8,128)S(1)} %get-tuple-element.83), channel_id=1, source_target_pairs={{0,64},{16,80},{32,96},{48,112},{64,0},{80,16},{96,32},{112,48},{1... | collective-permute-start | bytes 3080 | tf_op jit(solution)/shard_map/ppermute | solution.py:52
  276.4 39.3 %collective-permute-start.46 = (bf16[3,256,512]{2,1,0:T(8,128)(2,1)S(1)}, bf16[3,256,512]{2,1,0:T(8,128)(2,1)S(1)}, u32[]{:S(2)}, u32[]{:S(2)}) collective-permute-start(bf16[3,256,512]{2,1,0:T(8,128)(2,1)S(1)} %get-tuple-element.75), channel_id=1, source_target_pairs={{0,32},{16,48},{32,64},{48,80},{64,96},{80,112},{96,0},{112,16},{1... | collective-permute-start | bytes 2359304 | tf_op jit(solution)/shard_map/ppermute | solution.py:52
  276.4 40.7 %collective-permute-start.49 = (bf16[3,256,512]{2,1,0:T(8,128)(2,1)S(1)}, bf16[3,256,512]{2,1,0:T(8,128)(2,1)S(1)}, u32[]{:S(2)}, u32[]{:S(2)}) collective-permute-start(bf16[3,256,512]{2,1,0:T(8,128)(2,1)S(1)} %get-tuple-element.73), channel_id=1, source_target_pairs={{0,32},{16,48},{32,64},{48,80},{64,96},{80,112},{96,0},{112,16},{1... | collective-permute-start | bytes 2359304 | tf_op jit(solution)/shard_map/ppermute | solution.py:52
  276.6 41.2 %collective-permute-start.51 = (bf16[3,256,512]{2,1,0:T(8,128)(2,1)S(1)}, bf16[3,256,512]{2,1,0:T(8,128)(2,1)S(1)}, u32[]{:S(2)}, u32[]{:S(2)}) collective-permute-start(bf16[3,256,512]{2,1,0:T(8,128)(2,1)S(1)} %get-tuple-element.74), channel_id=1, source_target_pairs={{0,96},{16,112},{32,0},{48,16},{64,32},{80,48},{96,64},{112,80},{1... | collective-permute-start | bytes 2359304 | tf_op jit(solution)/shard_map/ppermute | solution.py:52
  289.3 30.4 %collective-permute-start.53 = (bf16[3,256,512]{2,1,0:T(8,128)(2,1)S(1)}, bf16[3,256,512]{2,1,0:T(8,128)(2,1)}, u32[]{:S(2)}, u32[]{:S(2)}) collective-permute-start(bf16[3,256,512]{2,1,0:T(8,128)(2,1)S(1)} %get-tuple-element.72), channel_id=1, source_target_pairs={{0,96},{16,112},{32,0},{48,16},{64,32},{80,48},{96,64},{112,80},{1... | collective-permute-start | bytes 2359304 | tf_op jit(solution)/shard_map/ppermute | solution.py:52
  292.1 20.6 %collective-permute-start.57 = (f32[256,1]{1,0:T(8,128)S(1)}, f32[256,1]{1,0:T(8,128)S(1)}, u32[]{:S(2)}, u32[]{:S(2)}) collective-permute-start(f32[256,1]{1,0:T(8,128)S(1)} %add.368), channel_id=1, source_target_pairs={{0,32},{16,48},{32,64},{48,80},{64,96},{80,112},{96,0},{112,16},{1... | collective-permute-start | bytes 3080 | tf_op jit(solution)/shard_map/ppermute | solution.py:52
  312.8 45.4 %collective-permute-start.34 = (bf16[48,8192]{1,0:T(8,128)(2,1)}, bf16[48,8192]{1,0:T(8,128)(2,1)}, u32[]{:S(2)}, u32[]{:S(2)}) collective-permute-start(bf16[48,8192]{1,0:T(8,128)(2,1)} %slice.105), channel_id=1, source_target_pairs={{0,6},{1,7},{2,0},{3,1},{4,2},{5,3},{6,4},{7,5},{8,14},{9,15},{10,... | collective-permute-start | bytes 2359304 | tf_op jit(solution)/shard_map/ppermute | solution.py:40
  315.7 20.5 %collective-permute-start.54 = (bf16[3,256,512]{2,1,0:T(8,128)(2,1)S(1)}, bf16[3,256,512]{2,1,0:T(8,128)(2,1)}, u32[]{:S(2)}, u32[]{:S(2)}) collective-permute-start(bf16[3,256,512]{2,1,0:T(8,128)(2,1)S(1)} %get-tuple-element.71), channel_id=1, source_target_pairs={{0,16},{16,0},{32,48},{48,32},{64,80},{80,64},{96,112},{112,96},{1... | collective-permute-start | bytes 2359304 | tf_op jit(solution)/shard_map/ppermute | solution.py:56
  317.1 36.0 %collective-permute-start.55 = (bf16[3,256,512]{2,1,0:T(8,128)(2,1)S(1)}, bf16[3,256,512]{2,1,0:T(8,128)(2,1)}, u32[]{:S(2)}, u32[]{:S(2)}) collective-permute-start(bf16[3,256,512]{2,1,0:T(8,128)(2,1)S(1)} %get-tuple-element.70), channel_id=1, source_target_pairs={{0,16},{16,0},{32,48},{48,32},{64,80},{80,64},{96,112},{112,96},{1... | collective-permute-start | bytes 2359304 | tf_op jit(solution)/shard_map/ppermute | solution.py:56
  317.8 47.4 %collective-permute-start.38 = (bf16[48,8192]{1,0:T(8,128)(2,1)}, bf16[48,8192]{1,0:T(8,128)(2,1)}, u32[]{:S(2)}, u32[]{:S(2)}) collective-permute-start(bf16[48,8192]{1,0:T(8,128)(2,1)} %get-tuple-element.79), channel_id=1, source_target_pairs={{0,8},{1,9},{2,10},{3,11},{4,12},{5,13},{6,14},{7,15},{8,0},{9,1},... | collective-permute-start | bytes 2359304 | tf_op jit(solution)/shard_map/ppermute | solution.py:44
  319.6 45.6 %collective-permute-start.33 = (bf16[48,8192]{1,0:T(8,128)(2,1)}, bf16[48,8192]{1,0:T(8,128)(2,1)}, u32[]{:S(2)}, u32[]{:S(2)}) collective-permute-start(bf16[48,8192]{1,0:T(8,128)(2,1)} %get-tuple-element.78), channel_id=1, source_target_pairs={{0,2},{1,3},{2,4},{3,5},{4,6},{5,7},{6,0},{7,1},{8,10},{9,11},{10,... | collective-permute-start | bytes 2359304 | tf_op jit(solution)/shard_map/ppermute | solution.py:40
  (24 other events, 424.2 us)
where the time goes:
time: 369 us; the launch traced here: 368 us
  waiting for transfers between devices  187 us (51%)
  Pallas kernels  94.9 us (26%)
  starting transfers between devices  61.1 us (17%)
  other arithmetic  18.3 us (5%)
  local copies, waits for them, and re-layouts  5.37 us (1%)
    ppermute x16, waiting for transfers between devices, to_x(): return lax.ppermute(value, 'fsdp', fsdp_pairs(step, 0, 0))  56.4 us
    ppermute x14, waiting for transfers between devices, to_z(): return lax.ppermute(value, 'lang', lang_pairs(step, 0))  44.5 us
    ppermute x5, waiting for transfers between devices, to_y_next(): return lax.ppermute(value, 'lang', lang_pairs(0, 1))  44 us
    ppermute x5, waiting for transfers between devices, to_y_half(): return lax.ppermute(value, 'fsdp', fsdp_pairs(0, 1, 0))  38 us
    pallas_call x3, Pallas kernels, forward(): pl.pallas_call(functools.partial(forward_kernel, n), name='forward', grid...  36.1 us
    ppermute x16, starting transfers between devices, to_x(): return lax.ppermute(value, 'fsdp', fsdp_pairs(step, 0, 0))  23.2 us
    pallas_call x1, Pallas kernels, gradients_late(): pl.pallas_call(functools.partial(late_kernel, len(toks), depth), name='la...  23.2 us
    ppermute x14, starting transfers between devices, to_z(): return lax.ppermute(value, 'lang', lang_pairs(step, 0))  19.8 us
  transfers between devices with their start and end apart: 58, of which 21 were waited for; matrix products, arithmetic and copies ran while one was open for 6% of the time, Pallas kernels for 17%

commit v1 on v0

--- a/solution.py
+++ b/solution.py
@@ -10,7 +10,8 @@
 
 epsilon = 1e-06
 INTERPRET = False
-VMEM = 58 << 20
+VMEM = (64 << 20) - 400000
+VMEM_SMALL = 20 << 20
 
 PLACES = ((0, 0), (-1, 0), (1, 0), (0, 1), (-1, 1), (1, 1), (2, 0), (2, 1))
 BATCHES = ((0, 1, 2, 3), (4, 5, 6), (7,))
@@ -62,10 +63,12 @@
 
 def forward_kernel(n, *refs):
     toks, outs = refs[:n], refs[n : 2 * n]
-    wg, wu, wd, inv, ggu_ref, hid_ref, gate, up, back = refs[2 * n :]
+    wg, wu, wd, inv, ggu_ref, hid_ref, tok_ref, out_ref, gate, up, back = refs[2 * n :]
     step = pl.program_id(0)
     features = jnp.concatenate([r[...] for r in toks], axis=0)
     upstream = jnp.concatenate([r[...] for r in outs], axis=0)
+    tok_ref[...] = features
+    out_ref[...] = upstream
 
     @pl.when(step == 0)
     def _():
@@ -107,9 +110,11 @@
                   pl.BlockSpec((hid, block), lambda k: (0, k)),
                   pl.BlockSpec((n * rows, 1), lambda k: (0, 0))],
         out_specs=[pl.BlockSpec((n * rows, 2 * hid), lambda k: (0, 0)),
-                   pl.BlockSpec((n * rows, hid), lambda k: (0, 0))],
+                   pl.BlockSpec((n * rows, hid), lambda k: (0, 0))]
+        + [pl.BlockSpec((n * rows, block), lambda k: (0, k))] * 2,
         out_shape=[jax.ShapeDtypeStruct((n * rows, 2 * hid), jnp.bfloat16),
-                   jax.ShapeDtypeStruct((n * rows, hid), jnp.bfloat16)],
+                   jax.ShapeDtypeStruct((n * rows, hid), jnp.bfloat16)]
+        + [jax.ShapeDtypeStruct((n * rows, depth), jnp.bfloat16)] * 2,
         scratch_shapes=[pltpu.VMEM((n * rows, hid), jnp.float32)] * 3,
         compiler_params=pltpu.CompilerParams(
             dimension_semantics=("arbitrary",), vmem_limit_bytes=VMEM),
@@ -146,6 +151,29 @@
             dimension_semantics=("arbitrary",), vmem_limit_bytes=VMEM),
         interpret=INTERPRET,
     )(*ggus, w_gate, w_up)
+
+
+def relay_kernel(pieces, a, b, ratio, low, high, left, right):
+    factor = ratio[:, :1]
+    for half, (value, other, out) in enumerate(((a, low, left), (b, high, right))):
+        scale = other[:, :1]
+        for m in range(3):
+            out[m] = bf(f32(pieces[half, m]) * factor + f32(value[m]) * scale)
+
+
+def relay(pieces, a, b, ratio, low, high):
+    _, _, hid, block = pieces.shape
+    whole = [pl.BlockSpec(v.shape, lambda k, n=v.ndim: (0,) * n) for v in (a, b, ratio, low, high)]
+    return pl.pallas_call(
+        relay_kernel,
+        name="relay",
+        grid=(1,),
+        in_specs=[pl.BlockSpec((2, 3, hid, block), lambda k: (0, 0, 0, 0))] + whole,
+        out_specs=whole[:2],
+        out_shape=[jax.ShapeDtypeStruct(a.shape, jnp.bfloat16)] * 2,
+        compiler_params=pltpu.CompilerParams(vmem_limit_bytes=VMEM_SMALL),
+        interpret=INTERPRET,
+    )(pieces, a, b, ratio, low, high)
 
 
 def last_kernel(pieces, l0, l1, r0, r1, n0, n1, ratio, total, gate, up, down):
@@ -175,7 +203,7 @@
         in_specs=[pl.BlockSpec((2, 3, hid, block), lambda k: (count // 2 - 1, 0, 0, 0))] + whole,
         out_specs=[pl.BlockSpec(shape, lambda k: (0, 0)) for shape in shapes],
         out_shape=[jax.ShapeDtypeStruct(shape, jnp.bfloat16) for shape in shapes],
-        compiler_params=pltpu.CompilerParams(vmem_limit_bytes=VMEM),
+        compiler_params=pltpu.CompilerParams(vmem_limit_bytes=VMEM_SMALL),
         interpret=INTERPRET,
     )(pieces, *others, ratio, total)
 
@@ -354,10 +382,11 @@
         tok += [to_core(v) for v in tok]
         out += [to_core(v) for v in out]
         size = rows * len(tok)
-        ggu, hidden = forward(tok, out, w_gate, w_up, w_down, inverse[at : at + size])
+        ggu, hidden, tok, out = forward(
+            tok, out, w_gate, w_up, w_down, inverse[at : at + size])
         at += size
-        toks += tok
-        outs += out
+        toks.append(tok)
+        outs.append(out)
         ggus.append(ggu)
         hids.append(hidden)
     near, near_p = input_gradient(ggus[:1], w_gate, w_up)
@@ -370,8 +399,10 @@
     far_p, moment = lax.optimization_barrier((far_p, moment))
     far = bf(f32(far) + f32(to_core(far_p)))
     e, f, pieces, ratio = gradients_late(target[EARLY:], toks, outs, ggu_t, hid_t, moment)
+    low, high = to_z(ratio, 1), to_z(ratio, -1)
+    left, right = relay(pieces, a, b, ratio, low, high)
     ratio = ratio[:, :1]
-    from_low, from_high, from_next = to_z(ratio, 1), to_z(ratio, -1), to_y_next(ratio)
+    from_low, from_high, from_next = low[:, :1], high[:, :1], to_y_next(ratio)
 
     def own(k):
         return f32(pieces[k - EARLY - ALONE]) * ratio[None]
@@ -380,20 +411,25 @@
         return f32(value) * factor[None]
 
     e, f = to_z(e, 1), to_z(f, -1)
-    g = to_z(bf(own(6) + theirs(a, from_low)), 1)
-    h = to_z(bf(own(7) + theirs(b, from_high)), -1)
+    g, h = to_z(left, 1), to_z(right, -1)
     from_next = after(from_next, g, h)
     c, d, e, f = after(c, g, h), after(d, g, h), after(e, g, h), after(f, g, h)
-    left_0 = to_z(bf(own(8) + theirs(e, from_low)), 1)
-    left_1 = to_z(bf(own(9) + theirs(c, from_next)), 1)
-    right_0 = to_z(bf(own(10) + theirs(d, from_next)), -1)
-    right_1 = to_z(bf(own(11) + theirs(f, from_high)), -1)
-    next_0 = to_y_next(bf(own(12) + f32(g)))
-    next_1 = to_y_next(bf(own(13) + f32(h)))
+    third = (
+        bf(own(8) + theirs(e, from_low)),
+        bf(own(9) + theirs(c, from_next)),
+        bf(own(10) + theirs(d, from_next)),
+        bf(own(11) + theirs(f, from_high)),
+        bf(own(12) + f32(g)),
+        bf(own(13) + f32(h)),
+    )
+    others = (
+        to_z(third[0], 1), to_z(third[1], 1),
+        to_z(third[2], -1), to_z(third[3], -1),
+        to_y_next(third[4]), to_y_next(third[5]),
+    )
     total = ratio + from_next
     total = total + to_z(total, 2)
     total = total + to_z(total, 1)
-    others = (left_0, left_1, right_0, right_1, next_0, next_1)
     grad_gate, grad_up, grad_down = last_sum(pieces, others, ratio, total)
 
     part = [value[i : i + rows] for value in (near, far) for i in range(0, 4 * rows, rows)]
@@ -401,6 +437,7 @@
     up_1, down_0 = to_x(part[5], 1), to_x(part[1], -1)
     up_0, down_1 = bf(f32(part[2]) + f32(far_0)), bf(f32(part[4]) + f32(far_1))
     up_0, down_1 = to_x(up_0, 1), to_x(down_1, -1)
+    up_1, down_1 = after(up_1, *third), after(down_1, *third)
     other = bf(f32(part[3]) + f32(up_1) + f32(down_1))
     other = to_y_half(other)
     grad_tokens = bf(f32(part[0]) + f32(up_0) + f32(down_0) + f32(other))[None]

time: 369 us -> 367 us (level)
  other arithmetic: 18.3 us -> 10.1 us
    pallas_call x3, Pallas kernels: 36.1 us -> 43.9 us  [forward(): pl.pallas_call(functools.partial(forward_kernel, n), name='forward', grid...]
    convert_element_type x6 -> x5, other arithmetic: 12.6 us -> 6.75 us  [bf(): return value.astype(jnp.bfloat16)]
    ppermute x5, waiting for transfers between devices: 38 us -> 42.2 us  [to_y_half(): return lax.ppermute(value, 'fsdp', fsdp_pairs(0, 1, 0))]
    ppermute x5, waiting for transfers between devices: 44 us -> 39.8 us  [to_y_next(): return lax.ppermute(value, 'lang', lang_pairs(0, 1))]
  transfers between devices with their start and end apart: 58 -> 58, of which waited for: 21 -> 22; matrix products, arithmetic and copies ran while one was open for 6% -> 4% of each run, Pallas kernels for 17% -> 18%
where the time goes in v1:
time: 367 us; the launch traced here: 366 us
  waiting for transfers between devices  187 us (51%)
  Pallas kernels  97 us (26%)
  starting transfers between devices  62.8 us (17%)
  other arithmetic  10.1 us (3%)
  local copies, waits for them, and re-layouts  7.76 us (2%)
    ppermute x16, waiting for transfers between devices, to_x(): return lax.ppermute(value, 'fsdp', fsdp_pairs(step, 0, 0))  58.7 us
    pallas_call x3, Pallas kernels, forward(): pl.pallas_call(functools.partial(forward_kernel, n), name='forward', grid...  43.9 us
    ppermute x14, waiting for transfers between devices, to_z(): return lax.ppermute(value, 'lang', lang_pairs(step, 0))  42.3 us
    ppermute x5, waiting for transfers between devices, to_y_half(): return lax.ppermute(value, 'fsdp', fsdp_pairs(0, 1, 0))  42.2 us
    ppermute x5, waiting for transfers between devices, to_y_next(): return lax.ppermute(value, 'lang', lang_pairs(0, 1))  39.8 us
    ppermute x16, starting transfers between devices, to_x(): return lax.ppermute(value, 'fsdp', fsdp_pairs(step, 0, 0))  23.1 us
    ppermute x14, starting transfers between devices, to_z(): return lax.ppermute(value, 'lang', lang_pairs(step, 0))  21.8 us
    pallas_call x2, Pallas kernels, input_gradient(): pl.pallas_call(functools.partial(input_kernel, len(ggus)), name='input',...  19.7 us
  transfers between devices with their start and end apart: 58, of which 22 were waited for; matrix products, arithmetic and copies ran while one was open for 4% of the time, Pallas kernels for 18%

profile of v1, /device:TPU:0, one launch (start us, length us, event | category | flops | bytes accessed | tf_op | source)
XLA Modules:
  0.0 366.1 jit_solution(9020483325384063970)
XLA Ops:
  0.6 1.7 collective-permute-start
  2.3 3.2 collective-permute-start.2
  5.8 1.6 collective-permute-start.8
  7.5 1.7 collective-permute-start.1
  9.1 12.2 %collective-permute-done.refs_1_ = bf16[48,8192]{1,0:T(8,128)(2,1)S(1)} collective-permute-done((bf16[48,8192]{1,0:T(8,128)(2,1)}, bf16[48,8192]{1,0:T(8,128)(2,1)S(1)}, u32[]{:S(2)}, u32[]{:S(2)}) %collective-permute-start) | collective-permute-done | bytes 786464 | tf_op jit(solution)/shard_map/ppermute | solution.py:41
  21.3 3.1 collective-permute-done.2.refs_3_
  24.4 1.5 collective-permute-start.7
  25.9 14.0 %collective-permute-done.9.refs_11_ = bf16[48,8192]{1,0:T(8,128)(2,1)S(1)} collective-permute-done((bf16[48,8192]{1,0:T(8,128)(2,1)}, bf16[48,8192]{1,0:T(8,128)(2,1)S(1)}, u32[]{:S(2)}, u32[]{:S(2)}) %collective-permute-start.9) | collective-permute-done | bytes 786464 | tf_op jit(solution)/shard_map/ppermute | solution.py:45
  39.9 3.3 collective-permute-start.15
  43.2 1.7 collective-permute-start.16
  45.2 1.5 collective-permute-start.21
  46.7 1.4 collective-permute-start.22
  48.1 13.8 %collective-permute-done.15.refs_0_ = bf16[48,8192]{1,0:T(8,128)(2,1)S(1)} collective-permute-done((bf16[48,8192]{1,0:T(8,128)(2,1)S(1)}, bf16[48,8192]{1,0:T(8,128)(2,1)S(1)}, u32[]{:S(2)}, u32[]{:S(2)}) %collective-permute-start.15) | collective-permute-done | bytes 786464 | tf_op jit(solution)/shard_map/ppermute | solution.py:45
  61.9 1.7 collective-permute-start.23
  63.7 2.8 collective-permute-done.17.refs_2_
  66.6 15.8 %collective-permute-done.21.refs_6_ = bf16[48,8192]{1,0:T(8,128)(2,1)} collective-permute-done((bf16[48,8192]{1,0:T(8,128)(2,1)S(1)}, bf16[48,8192]{1,0:T(8,128)(2,1)}, u32[]{:S(2)}, u32[]{:S(2)}) %collective-permute-start.21) | collective-permute-done | bytes 786464 | tf_op jit(solution)/shard_map/ppermute | solution.py:41
  83.6 1.1 collective-permute-done.6.refs_7_
  84.8 1.0 collective-permute-done.11.refs_13_
  85.9 1.0 collective-permute-done.12.refs_14_
  86.9 1.1 collective-permute-done.13.refs_15_
  88.1 2.2 collective-permute-start.29
  91.9 15.9 %collective-permute-done.27.refs_0_ = bf16[48,8192]{1,0:T(8,128)(2,1)} collective-permute-done((bf16[48,8192]{1,0:T(8,128)(2,1)S(1)}, bf16[48,8192]{1,0:T(8,128)(2,1)}, u32[]{:S(2)}, u32[]{:S(2)}) %collective-permute-start.27) | collective-permute-done | bytes 786464 | tf_op jit(solution)/shard_map/ppermute | solution.py:41
  112.3 17.8 %forward.3 = (bf16[384,512]{1,0:T(8,128)(2,1)}, bf16[384,256]{1,0:T(8,128)(2,1)}, bf16[384,8192]{1,0:T(8,128)(2,1)}, bf16[384,8192]{1,0:T(8,128)(2,1)}) custom-call(bf16[48,8192]{1,0:T(8,128)(2,1)} %bitcast.63, bf16[48,8192]{1,0:T(8,128)(2,1)} %copy-done.4, bf16[48,8192]{1,0:T(8,128)(2,1)} %copy-done.8, bf16[48,8192]{1,0:T(8,128)(2,1)} %copy-done.5, ...), custom_call_target="tpu_custom_call" | custom-call | tf_op jit(solution)/shard_map/forward/pallas_call | solution.py:105
  130.2 15.3 %forward.4 = (bf16[288,512]{1,0:T(8,128)(2,1)}, bf16[288,256]{1,0:T(8,128)(2,1)}, bf16[288,8192]{1,0:T(8,128)(2,1)}, bf16[288,8192]{1,0:T(8,128)(2,1)}) custom-call(bf16[48,8192]{1,0:T(8,128)(2,1)} %copy-done.9, bf16[48,8192]{1,0:T(8,128)(2,1)} %copy-done.11, bf16[48,8192]{1,0:T(8,128)(2,1)} %copy-done.13, bf16[48,8192]{1,0:T(8,128)(2,1)} %copy-done.18, ...), custom_call_target="tpu_custom_call" | custom-call | tf_op jit(solution)/shard_map/forward/pallas_call | solution.py:105
  145.5 10.8 %forward.5 = (bf16[96,512]{1,0:T(8,128)(2,1)}, bf16[96,256]{1,0:T(8,128)(2,1)}, bf16[96,8192]{1,0:T(8,128)(2,1)}, bf16[96,8192]{1,0:T(8,128)(2,1)}) custom-call(bf16[48,8192]{1,0:T(8,128)(2,1)} %collective-permute-done.27.refs_0_, bf16[48,8192]{1,0:T(8,128)(2,1)} %collective-permute-done.28.refs_1_, bf16[48,8192]{1,0:T(8,128)(2,1)} %collective-permute-done.29.refs_2_, ...), custom_call_target="tpu_custom_call" | custom-call | tf_op jit(solution)/shard_map/forward/pallas_call | solution.py:105
  156.3 9.4 %early.1 = (bf16[3,256,512]{2,1,0:T(8,128)(2,1)}, bf16[3,256,512]{2,1,0:T(8,128)(2,1)}, bf16[3,256,512]{2,1,0:T(8,128)(2,1)}, bf16[3,256,512]{2,1,0:T(8,128)(2,1...) custom-call(s32[4]{0:T(128)} %pad_add_fusion.place, ...), custom_call_target="tpu_custom_call" | custom-call | tf_op jit(solution)/shard_map/early/pallas_call | solution.py:292
  165.7 9.9 %input.3 = (bf16[192,8192]{1,0:T(8,128)(2,1)}, bf16[192,8192]{1,0:T(8,128)(2,1)}) custom-call(bf16[288,512]{1,0:T(8,128)(2,1)} %get-tuple-element.61.refs_7_.refs_0_, bf16[96,512]{1,0:T(8,128)(2,1)} %get-tuple-element.56.refs_8_.refs_1_, bf16[8192,256]{1,0:T(8,128)(2,1)} %refs_2_.3, bf16[8192,256]{1,0:T(8,128)(2,1)} %refs_3_.1), custom_call_target="tpu_custom_call" | custom-call | tf_op jit(solution)/shard_map/input/pallas_call | solution.py:143
  175.6 2.0 collective-permute-start.37
  177.6 2.2 collective-permute-start.38
  180.3 19.5 %late.1 = (bf16[3,256,512]{2,1,0:T(8,128)(2,1)}, bf16[3,256,512]{2,1,0:T(8,128)(2,1)}, bf16[10,3,256,512]{3,2,1,0:T(8,128)(2,1)}, f32[256,128]{1,0:T(8,128)}) custom-call(s32[12]{0:T(128)} %stack.138.place, bf16[384,8192]{1,0:T(8,128)(2,1)} %get-tuple-element.50.refs_0_, bf16[288,8192]{1,0:T(8,128)(2,1)} %get-tuple-element.51.refs_1_, ...), custom_call_target="tpu_custom_call" | custom-call | tf_op jit(solution)/shard_map/late/pallas_call | solution.py:315
  199.9 2.0 collective-permute-start.40
  202.0 9.8 %input.2 = (bf16[192,8192]{1,0:T(8,128)(2,1)}, bf16[192,8192]{1,0:T(8,128)(2,1)}) custom-call(bf16[384,512]{1,0:T(8,128)(2,1)} %get-tuple-element.46.refs_0_.refs_6_, bf16[8192,256]{1,0:T(8,128)(2,1)} %refs_2_.3, bf16[8192,256]{1,0:T(8,128)(2,1)} %refs_3_.1), custom_call_target="tpu_custom_call" | custom-call | tf_op jit(solution)/shard_map/input/pallas_call | solution.py:143
  212.7 1.0 slice_reduce_fusion.1
  213.7 3.2 collective-permute-start.46
  216.9 1.4 collective-permute-start.43
  218.3 3.2 copy-done
  221.5 2.2 relay.1
  224.1 3.1 add_convert_fusion
  227.5 2.0 collective-permute-start.41
  229.5 2.9 collective-permute-start.47
  232.4 1.1 add_convert_fusion.1
  233.5 17.7 %collective-permute-done.42 = bf16[3,256,512]{2,1,0:T(8,128)(2,1)S(1)} collective-permute-done((bf16[3,256,512]{2,1,0:T(8,128)(2,1)S(1)}, bf16[3,256,512]{2,1,0:T(8,128)(2,1)S(1)}, u32[]{:S(2)}, u32[]{:S(2)}) %collective-permute-start.42) | collective-permute-done | bytes 786464 | tf_op jit(solution)/shard_map/ppermute | solution.py:53
  251.2 1.3 collective-permute-start.45
  252.6 1.4 collective-permute-start.35
  254.2 2.0 collective-permute-start.48
  256.4 13.6 %collective-permute-done.45 = bf16[3,256,512]{2,1,0:T(8,128)(2,1)S(1)} collective-permute-done((bf16[3,256,512]{2,1,0:T(8,128)(2,1)S(1)}, bf16[3,256,512]{2,1,0:T(8,128)(2,1)S(1)}, u32[]{:S(2)}, u32[]{:S(2)}) %collective-permute-start.45) | collective-permute-done | bytes 786464 | tf_op jit(solution)/shard_map/ppermute | solution.py:57
  270.0 2.5 collective-permute-start.56
  272.5 1.0 collective-permute-done.36
  273.4 1.9 fusion.1
  275.4 1.2 collective-permute-start.50
  277.5 11.7 %collective-permute-done.35 = bf16[48,8192]{1,0:T(8,128)(2,1)S(1)} collective-permute-done((bf16[48,8192]{1,0:T(8,128)(2,1)S(1)}, bf16[48,8192]{1,0:T(8,128)(2,1)S(1)}, u32[]{:S(2)}, u32[]{:S(2)}) %collective-permute-start.35) | collective-permute-done | bytes 786464 | tf_op jit(solution)/shard_map/ppermute | solution.py:41
  289.2 3.7 %collective-permute-start.52 = (bf16[3,256,512]{2,1,0:T(8,128)(2,1)S(1)}, bf16[3,256,512]{2,1,0:T(8,128)(2,1)S(1)}, u32[]{:S(2)}, u32[]{:S(2)}) collective-permute-start(bf16[3,256,512]{2,1,0:T(8,128)(2,1)S(1)} %get-tuple-element.94), channel_id=1, source_target_pairs={{0,96},{16,112},{32,0},{48,16},{64,32},{80,48},{96,64},{112,80},{1... | collective-permute-start | bytes 2359304 | tf_op jit(solution)/shard_map/ppermute | solution.py:53
  292.9 1.7 collective-permute-start.53
  295.4 18.5 %collective-permute-done.57 = f32[256,1]{1,0:T(8,128)S(1)} collective-permute-done((f32[256,1]{1,0:T(8,128)S(1)}, f32[256,1]{1,0:T(8,128)S(1)}, u32[]{:S(2)}, u32[]{:S(2)}) %collective-permute-start.57) | collective-permute-done | bytes 1056 | tf_op jit(solution)/shard_map/ppermute | solution.py:53
  313.9 0.8 collective-permute-start.54
  314.8 1.2 collective-permute-start.55
  315.9 2.9 collective-permute-start.34
  318.8 1.3 collective-permute-start.49
  320.2 4.8 %collective-permute-done.53.r1 = bf16[3,256,512]{2,1,0:T(8,128)(2,1)S(1)} collective-permute-done((bf16[3,256,512]{2,1,0:T(8,128)(2,1)S(1)}, bf16[3,256,512]{2,1,0:T(8,128)(2,1)S(1)}, u32[]{:S(2)}, u32[]{:S(2)}) %collective-permute-start.53) | collective-permute-done | bytes 786464 | tf_op jit(solution)/shard_map/ppermute | solution.py:53
  325.0 9.3 %collective-permute-done.54.n0 = bf16[3,256,512]{2,1,0:T(8,128)(2,1)S(1)} collective-permute-done((bf16[3,256,512]{2,1,0:T(8,128)(2,1)S(1)}, bf16[3,256,512]{2,1,0:T(8,128)(2,1)S(1)}, u32[]{:S(2)}, u32[]{:S(2)}) %collective-permute-start.54) | collective-permute-done | bytes 786464 | tf_op jit(solution)/shard_map/ppermute | solution.py:57
  334.3 16.9 %collective-permute-done.55.n1 = bf16[3,256,512]{2,1,0:T(8,128)(2,1)S(1)} collective-permute-done((bf16[3,256,512]{2,1,0:T(8,128)(2,1)S(1)}, bf16[3,256,512]{2,1,0:T(8,128)(2,1)S(1)}, u32[]{:S(2)}, u32[]{:S(2)}) %collective-permute-start.55) | collective-permute-done | bytes 786464 | tf_op jit(solution)/shard_map/ppermute | solution.py:57
  351.2 2.3 last.1
  353.5 11.3 %collective-permute-done.49 = bf16[48,8192]{1,0:T(8,128)(2,1)S(1)} collective-permute-done((bf16[48,8192]{1,0:T(8,128)(2,1)S(1)}, bf16[48,8192]{1,0:T(8,128)(2,1)S(1)}, u32[]{:S(2)}, u32[]{:S(2)}) %collective-permute-start.49) | collective-permute-done | bytes 786464 | tf_op jit(solution)/shard_map/ppermute | solution.py:45
  364.9 1.3 fusion.12
  (142 shorter events, 12.5 us)
Async XLA Ops:
  0.6 20.7 %collective-permute-start = (bf16[48,8192]{1,0:T(8,128)(2,1)}, bf16[48,8192]{1,0:T(8,128)(2,1)S(1)}, u32[]{:S(2)}, u32[]{:S(2)}) collective-permute-start(bf16[48,8192]{1,0:T(8,128)(2,1)} %bitcast.59), channel_id=1, source_target_pairs={{0,2},{1,3},{2,4},{3,5},{4,6},{5,7},{6,0},{7,1},{8,10},{9,11},{10,... | collective-permute-start | bytes 2359304 | tf_op jit(solution)/shard_map/ppermute | solution.py:41
  2.3 22.1 %collective-permute-start.2 = (bf16[48,8192]{1,0:T(8,128)(2,1)}, bf16[48,8192]{1,0:T(8,128)(2,1)S(1)}, u32[]{:S(2)}, u32[]{:S(2)}) collective-permute-start(bf16[48,8192]{1,0:T(8,128)(2,1)} %bitcast.60), channel_id=1, source_target_pairs={{0,8},{1,9},{2,10},{3,11},{4,12},{5,13},{6,14},{7,15},{8,0},{9,1},... | collective-permute-start | bytes 2359304 | tf_op jit(solution)/shard_map/ppermute | solution.py:45
  5.5 34.4 %collective-permute-start.9 = (bf16[48,8192]{1,0:T(8,128)(2,1)}, bf16[48,8192]{1,0:T(8,128)(2,1)S(1)}, u32[]{:S(2)}, u32[]{:S(2)}) collective-permute-start(bf16[48,8192]{1,0:T(8,128)(2,1)} %bitcast.64), channel_id=1, source_target_pairs={{0,8},{1,9},{2,10},{3,11},{4,12},{5,13},{6,14},{7,15},{8,0},{9,1},... | collective-permute-start | bytes 2359304 | tf_op jit(solution)/shard_map/ppermute | solution.py:45
  5.8 34.1 %collective-permute-start.8 = (bf16[48,8192]{1,0:T(8,128)(2,1)}, bf16[48,8192]{1,0:T(8,128)(2,1)S(1)}, u32[]{:S(2)}, u32[]{:S(2)}) collective-permute-start(bf16[48,8192]{1,0:T(8,128)(2,1)} %bitcast.65), channel_id=1, source_target_pairs={{0,6},{1,7},{2,0},{3,1},{4,2},{5,3},{6,4},{7,5},{8,14},{9,15},{10,... | collective-permute-start | bytes 2359304 | tf_op jit(solution)/shard_map/ppermute | solution.py:41
  7.5 35.7 %collective-permute-start.1 = (bf16[48,8192]{1,0:T(8,128)(2,1)}, bf16[48,8192]{1,0:T(8,128)(2,1)S(1)}, u32[]{:S(2)}, u32[]{:S(2)}) collective-permute-start(bf16[48,8192]{1,0:T(8,128)(2,1)} %bitcast.61), channel_id=1, source_target_pairs={{0,6},{1,7},{2,0},{3,1},{4,2},{5,3},{6,4},{7,5},{8,14},{9,15},{10,... | collective-permute-start | bytes 2359304 | tf_op jit(solution)/shard_map/ppermute | solution.py:41
  21.3 23.6 %collective-permute-start.3 = (bf16[48,8192]{1,0:T(8,128)(2,1)}, bf16[48,8192]{1,0:T(8,128)(2,1)S(1)}, u32[]{:S(2)}, u32[]{:S(2)}) collective-permute-start(bf16[48,8192]{1,0:T(8,128)(2,1)} %bitcast.62), channel_id=1, source_target_pairs={{0,1},{1,0},{2,3},{3,2},{4,5},{5,4},{6,7},{7,6},{8,9},{9,8},{10,11... | collective-permute-start | bytes 2359304 | tf_op jit(solution)/shard_map/ppermute | solution.py:49
  24.4 58.6 %copy-start.5 = (bf16[48,8192]{1,0:T(8,128)(2,1)}, bf16[48,8192]{1,0:T(8,128)(2,1)S(1)}, u32[]{:S(2)}) copy-start(bf16[48,8192]{1,0:T(8,128)(2,1)S(1)} %collective-permute-done.2.refs_3_) | copy-start | bytes 2359300
  24.4 20.8 %collective-permute-start.7 = (bf16[48,8192]{1,0:T(8,128)(2,1)}, bf16[48,8192]{1,0:T(8,128)(2,1)S(1)}, u32[]{:S(2)}, u32[]{:S(2)}) collective-permute-start(bf16[48,8192]{1,0:T(8,128)(2,1)} %bitcast.66), channel_id=1, source_target_pairs={{0,2},{1,3},{2,4},{3,5},{4,6},{5,7},{6,0},{7,1},{8,10},{9,11},{10,... | collective-permute-start | bytes 2359304 | tf_op jit(solution)/shard_map/ppermute | solution.py:41
  39.9 6.8 %collective-permute-start.10 = (bf16[48,8192]{1,0:T(8,128)(2,1)}, bf16[48,8192]{1,0:T(8,128)(2,1)S(1)}, u32[]{:S(2)}, u32[]{:S(2)}) collective-permute-start(bf16[48,8192]{1,0:T(8,128)(2,1)} %bitcast.67), channel_id=1, source_target_pairs={{0,1},{1,0},{2,3},{3,2},{4,5},{5,4},{6,7},{7,6},{8,9},{9,8},{10,11... | collective-permute-start | bytes 2359304 | tf_op jit(solution)/shard_map/ppermute | solution.py:49
  39.9 48.2 %copy-start.7 = (bf16[48,8192]{1,0:T(8,128)(2,1)}, bf16[48,8192]{1,0:T(8,128)(2,1)S(1)}, u32[]{:S(2)}) copy-start(bf16[48,8192]{1,0:T(8,128)(2,1)S(1)} %collective-permute-done.8.refs_10_) | copy-start | bytes 2359300
  39.9 22.0 %collective-permute-start.15 = (bf16[48,8192]{1,0:T(8,128)(2,1)S(1)}, bf16[48,8192]{1,0:T(8,128)(2,1)S(1)}, u32[]{:S(2)}, u32[]{:S(2)}) collective-permute-start(bf16[48,8192]{1,0:T(8,128)(2,1)S(1)} %collective-permute-done.refs_1_), channel_id=1, source_target_pairs={{0,8},{1,9},{2,10},{3,11},{4,12},{5,13},{6,14},{7,15},{8,0},{9,1},... | collective-permute-start | bytes 2359304 | tf_op jit(solution)/shard_map/ppermute | solution.py:45
  43.2 47.1 %copy-start.8 = (bf16[48,8192]{1,0:T(8,128)(2,1)}, bf16[48,8192]{1,0:T(8,128)(2,1)S(1)}, u32[]{:S(2)}) copy-start(bf16[48,8192]{1,0:T(8,128)(2,1)S(1)} %collective-permute-done.1.refs_2_) | copy-start | bytes 2359300
  43.2 20.4 %collective-permute-start.16 = (bf16[48,8192]{1,0:T(8,128)(2,1)S(1)}, bf16[48,8192]{1,0:T(8,128)(2,1)S(1)}, u32[]{:S(2)}, u32[]{:S(2)}) collective-permute-start(bf16[48,8192]{1,0:T(8,128)(2,1)S(1)} %collective-permute-done.2.refs_3_), channel_id=1, source_target_pairs={{0,6},{1,7},{2,0},{3,1},{4,2},{5,3},{6,4},{7,5},{8,14},{9,15},{10,... | collective-permute-start | bytes 2359304 | tf_op jit(solution)/shard_map/ppermute | solution.py:41
  44.9 45.3 %copy-start.10 = (bf16[48,8192]{1,0:T(8,128)(2,1)}, bf16[48,8192]{1,0:T(8,128)(2,1)S(1)}, u32[]{:S(2)}) copy-start(bf16[48,8192]{1,0:T(8,128)(2,1)S(1)} %collective-permute-done.3.refs_4_) | copy-start | bytes 2359300
  44.9 21.6 %collective-permute-start.17 = (bf16[48,8192]{1,0:T(8,128)(2,1)S(1)}, bf16[48,8192]{1,0:T(8,128)(2,1)S(1)}, u32[]{:S(2)}, u32[]{:S(2)}) collective-permute-start(bf16[48,8192]{1,0:T(8,128)(2,1)S(1)} %collective-permute-done.refs_1_), channel_id=1, source_target_pairs={{0,2},{1,3},{2,4},{3,5},{4,6},{5,7},{6,0},{7,1},{8,10},{9,11},{10,... | collective-permute-start | bytes 2359304 | tf_op jit(solution)/shard_map/ppermute | solution.py:41
  45.2 45.0 %copy-start.12 = (bf16[48,8192]{1,0:T(8,128)(2,1)}, bf16[48,8192]{1,0:T(8,128)(2,1)S(1)}, u32[]{:S(2)}) copy-start(bf16[48,8192]{1,0:T(8,128)(2,1)S(1)} %collective-permute-done.7.refs_9_) | copy-start | bytes 2359300
  45.2 37.2 %collective-permute-start.21 = (bf16[48,8192]{1,0:T(8,128)(2,1)S(1)}, bf16[48,8192]{1,0:T(8,128)(2,1)}, u32[]{:S(2)}, u32[]{:S(2)}) collective-permute-start(bf16[48,8192]{1,0:T(8,128)(2,1)S(1)} %collective-permute-done.9.refs_11_), channel_id=1, source_target_pairs={{0,2},{1,3},{2,4},{3,5},{4,6},{5,7},{6,0},{7,1},{8,10},{9,11},{10,... | collective-permute-start | bytes 2359304 | tf_op jit(solution)/shard_map/ppermute | solution.py:41
  46.7 35.7 %collective-permute-start.22 = (bf16[48,8192]{1,0:T(8,128)(2,1)S(1)}, bf16[48,8192]{1,0:T(8,128)(2,1)}, u32[]{:S(2)}, u32[]{:S(2)}) collective-permute-start(bf16[48,8192]{1,0:T(8,128)(2,1)S(1)} %collective-permute-done.8.refs_10_), channel_id=1, source_target_pairs={{0,8},{1,9},{2,10},{3,11},{4,12},{5,13},{6,14},{7,15},{8,0},{9,1},... | collective-permute-start | bytes 2359304 | tf_op jit(solution)/shard_map/ppermute | solution.py:45
  61.9 21.0 %collective-permute-start.23 = (bf16[48,8192]{1,0:T(8,128)(2,1)S(1)}, bf16[48,8192]{1,0:T(8,128)(2,1)}, u32[]{:S(2)}, u32[]{:S(2)}) collective-permute-start(bf16[48,8192]{1,0:T(8,128)(2,1)S(1)} %collective-permute-done.8.refs_10_), channel_id=1, source_target_pairs={{0,6},{1,7},{2,0},{3,1},{4,2},{5,3},{6,4},{7,5},{8,14},{9,15},{10,... | collective-permute-start | bytes 2359304 | tf_op jit(solution)/shard_map/ppermute | solution.py:41
  63.6 19.4 %collective-permute-start.4 = (bf16[48,8192]{1,0:T(8,128)(2,1)S(1)}, bf16[48,8192]{1,0:T(8,128)(2,1)S(1)}, u32[]{:S(2)}, u32[]{:S(2)}) collective-permute-start(bf16[48,8192]{1,0:T(8,128)(2,1)S(1)} %collective-permute-done.refs_1_), channel_id=1, source_target_pairs={{0,1},{1,0},{2,3},{3,2},{4,5},{5,4},{6,7},{7,6},{8,9},{9,8},{10,11... | collective-permute-start | bytes 2359304 | tf_op jit(solution)/shard_map/ppermute | solution.py:49
  66.5 17.0 %collective-permute-start.5 = (bf16[48,8192]{1,0:T(8,128)(2,1)S(1)}, bf16[48,8192]{1,0:T(8,128)(2,1)S(1)}, u32[]{:S(2)}, u32[]{:S(2)}) collective-permute-start(bf16[48,8192]{1,0:T(8,128)(2,1)S(1)} %collective-permute-done.1.refs_2_), channel_id=1, source_target_pairs={{0,1},{1,0},{2,3},{3,2},{4,5},{5,4},{6,7},{7,6},{8,9},{9,8},{10,11... | collective-permute-start | bytes 2359304 | tf_op jit(solution)/shard_map/ppermute | solution.py:49
  82.4 2.3 collective-permute-start.6
  82.4 3.4 collective-permute-start.11
  82.9 4.0 %collective-permute-start.12 = (bf16[48,8192]{1,0:T(8,128)(2,1)S(1)}, bf16[48,8192]{1,0:T(8,128)(2,1)S(1)}, u32[]{:S(2)}, u32[]{:S(2)}) collective-permute-start(bf16[48,8192]{1,0:T(8,128)(2,1)S(1)} %collective-permute-done.8.refs_10_), channel_id=1, source_target_pairs={{0,1},{1,0},{2,3},{3,2},{4,5},{5,4},{6,7},{7,6},{8,9},{9,8},{10,11... | collective-permute-start | bytes 2359304 | tf_op jit(solution)/shard_map/ppermute | solution.py:49
  83.0 5.0 %collective-permute-start.13 = (bf16[48,8192]{1,0:T(8,128)(2,1)S(1)}, bf16[48,8192]{1,0:T(8,128)(2,1)S(1)}, u32[]{:S(2)}, u32[]{:S(2)}) collective-permute-start(bf16[48,8192]{1,0:T(8,128)(2,1)S(1)} %collective-permute-done.9.refs_11_), channel_id=1, source_target_pairs={{0,1},{1,0},{2,3},{3,2},{4,5},{5,4},{6,7},{7,6},{8,9},{9,8},{10,11... | collective-permute-start | bytes 2359304 | tf_op jit(solution)/shard_map/ppermute | solution.py:49
  83.5 7.7 %collective-permute-start.18 = (bf16[48,8192]{1,0:T(8,128)(2,1)S(1)}, bf16[48,8192]{1,0:T(8,128)(2,1)S(1)}, u32[]{:S(2)}, u32[]{:S(2)}) collective-permute-start(bf16[48,8192]{1,0:T(8,128)(2,1)S(1)} %collective-permute-done.15.refs_0_), channel_id=1, source_target_pairs={{0,1},{1,0},{2,3},{3,2},{4,5},{5,4},{6,7},{7,6},{8,9},{9,8},{10,11... | collective-permute-start | bytes 2359304 | tf_op jit(solution)/shard_map/ppermute | solution.py:49
  84.7 6.6 %collective-permute-start.19 = (bf16[48,8192]{1,0:T(8,128)(2,1)S(1)}, bf16[48,8192]{1,0:T(8,128)(2,1)}, u32[]{:S(2)}, u32[]{:S(2)}) collective-permute-start(bf16[48,8192]{1,0:T(8,128)(2,1)S(1)} %collective-permute-done.16.refs_1_), channel_id=1, source_target_pairs={{0,1},{1,0},{2,3},{3,2},{4,5},{5,4},{6,7},{7,6},{8,9},{9,8},{10,11... | collective-permute-start | bytes 2359304 | tf_op jit(solution)/shard_map/ppermute | solution.py:49
  85.8 6.0 %collective-permute-start.20 = (bf16[48,8192]{1,0:T(8,128)(2,1)S(1)}, bf16[48,8192]{1,0:T(8,128)(2,1)}, u32[]{:S(2)}, u32[]{:S(2)}) collective-permute-start(bf16[48,8192]{1,0:T(8,128)(2,1)S(1)} %collective-permute-done.17.refs_2_), channel_id=1, source_target_pairs={{0,1},{1,0},{2,3},{3,2},{4,5},{5,4},{6,7},{7,6},{8,9},{9,8},{10,11... | collective-permute-start | bytes 2359304 | tf_op jit(solution)/shard_map/ppermute | solution.py:49
  86.9 20.9 %collective-permute-start.27 = (bf16[48,8192]{1,0:T(8,128)(2,1)S(1)}, bf16[48,8192]{1,0:T(8,128)(2,1)}, u32[]{:S(2)}, u32[]{:S(2)}) collective-permute-start(bf16[48,8192]{1,0:T(8,128)(2,1)S(1)} %collective-permute-done.15.refs_0_), channel_id=1, source_target_pairs={{0,2},{1,3},{2,4},{3,5},{4,6},{5,7},{6,0},{7,1},{8,10},{9,11},{10,... | collective-permute-start | bytes 2359304 | tf_op jit(solution)/shard_map/ppermute | solution.py:41
  88.1 19.9 %collective-permute-start.29 = (bf16[48,8192]{1,0:T(8,128)(2,1)}, bf16[48,8192]{1,0:T(8,128)(2,1)}, u32[]{:S(2)}, u32[]{:S(2)}) collective-permute-start(bf16[48,8192]{1,0:T(8,128)(2,1)} %collective-permute-done.22.refs_7_), channel_id=1, source_target_pairs={{0,6},{1,7},{2,0},{3,1},{4,2},{5,3},{6,4},{7,5},{8,14},{9,15},{10,... | collective-permute-start | bytes 2359304 | tf_op jit(solution)/shard_map/ppermute | solution.py:41
  91.2 38.9 %collective-permute-start.25 = (bf16[48,8192]{1,0:T(8,128)(2,1)}, bf16[48,8192]{1,0:T(8,128)(2,1)}, u32[]{:S(2)}, u32[]{:S(2)}) collective-permute-start(bf16[48,8192]{1,0:T(8,128)(2,1)} %collective-permute-done.22.refs_7_), channel_id=1, source_target_pairs={{0,1},{1,0},{2,3},{3,2},{4,5},{5,4},{6,7},{7,6},{8,9},{9,8},{10,11... | collective-permute-start | bytes 2359304 | tf_op jit(solution)/shard_map/ppermute | solution.py:49
  91.3 38.8 %collective-permute-start.24 = (bf16[48,8192]{1,0:T(8,128)(2,1)}, bf16[48,8192]{1,0:T(8,128)(2,1)}, u32[]{:S(2)}, u32[]{:S(2)}) collective-permute-start(bf16[48,8192]{1,0:T(8,128)(2,1)} %collective-permute-done.21.refs_6_), channel_id=1, source_target_pairs={{0,1},{1,0},{2,3},{3,2},{4,5},{5,4},{6,7},{7,6},{8,9},{9,8},{10,11... | collective-permute-start | bytes 2359304 | tf_op jit(solution)/shard_map/ppermute | solution.py:49
  91.8 38.4 %collective-permute-start.26 = (bf16[48,8192]{1,0:T(8,128)(2,1)}, bf16[48,8192]{1,0:T(8,128)(2,1)}, u32[]{:S(2)}, u32[]{:S(2)}) collective-permute-start(bf16[48,8192]{1,0:T(8,128)(2,1)} %collective-permute-done.23.refs_8_), channel_id=1, source_target_pairs={{0,1},{1,0},{2,3},{3,2},{4,5},{5,4},{6,7},{7,6},{8,9},{9,8},{10,11... | collective-permute-start | bytes 2359304 | tf_op jit(solution)/shard_map/ppermute | solution.py:49
  107.8 37.7 %collective-permute-start.28 = (bf16[48,8192]{1,0:T(8,128)(2,1)}, bf16[48,8192]{1,0:T(8,128)(2,1)}, u32[]{:S(2)}, u32[]{:S(2)}) collective-permute-start(bf16[48,8192]{1,0:T(8,128)(2,1)} %collective-permute-done.27.refs_0_), channel_id=1, source_target_pairs={{0,1},{1,0},{2,3},{3,2},{4,5},{5,4},{6,7},{7,6},{8,9},{9,8},{10,11... | collective-permute-start | bytes 2359304 | tf_op jit(solution)/shard_map/ppermute | solution.py:49
  108.0 37.5 %collective-permute-start.30 = (bf16[48,8192]{1,0:T(8,128)(2,1)}, bf16[48,8192]{1,0:T(8,128)(2,1)}, u32[]{:S(2)}, u32[]{:S(2)}) collective-permute-start(bf16[48,8192]{1,0:T(8,128)(2,1)} %collective-permute-done.29.refs_2_), channel_id=1, source_target_pairs={{0,1},{1,0},{2,3},{3,2},{4,5},{5,4},{6,7},{7,6},{8,9},{9,8},{10,11... | collective-permute-start | bytes 2359304 | tf_op jit(solution)/shard_map/ppermute | solution.py:49
  175.6 48.1 %collective-permute-start.31 = (bf16[192,8192]{1,0:T(8,128)(2,1)}, bf16[192,8192]{1,0:T(8,128)(2,1)}, u32[]{:S(2)}, u32[]{:S(2)}) collective-permute-start(bf16[192,8192]{1,0:T(8,128)(2,1)} %get-tuple-element.64), channel_id=1, source_target_pairs={{0,1},{1,0},{2,3},{3,2},{4,5},{5,4},{6,7},{7,6},{8,9},{9,8},{10,11... | collective-permute-start | bytes 9437192 | tf_op jit(solution)/shard_map/ppermute | solution.py:49
  175.6 38.1 %collective-permute-start.37 = (bf16[3,256,512]{2,1,0:T(8,128)(2,1)}, bf16[3,256,512]{2,1,0:T(8,128)(2,1)}, u32[]{:S(2)}, u32[]{:S(2)}) collective-permute-start(bf16[3,256,512]{2,1,0:T(8,128)(2,1)} %get-tuple-element.71), channel_id=1, source_target_pairs={{0,32},{16,48},{32,64},{48,80},{64,96},{80,112},{96,0},{112,16},{1... | collective-permute-start | bytes 2359304 | tf_op jit(solution)/shard_map/ppermute | solution.py:53
  177.6 39.4 %collective-permute-start.38 = (bf16[3,256,512]{2,1,0:T(8,128)(2,1)}, bf16[3,256,512]{2,1,0:T(8,128)(2,1)}, u32[]{:S(2)}, u32[]{:S(2)}) collective-permute-start(bf16[3,256,512]{2,1,0:T(8,128)(2,1)} %get-tuple-element.72), channel_id=1, source_target_pairs={{0,96},{16,112},{32,0},{48,16},{64,32},{80,48},{96,64},{112,80},{1... | collective-permute-start | bytes 2359304 | tf_op jit(solution)/shard_map/ppermute | solution.py:53
  199.9 11.9 %collective-permute-start.40 = (f32[256,128]{1,0:T(8,128)}, f32[256,128]{1,0:T(8,128)S(1)}, u32[]{:S(2)}, u32[]{:S(2)}) collective-permute-start(f32[256,128]{1,0:T(8,128)} %get-tuple-element.69.ratio), channel_id=1, source_target_pairs={{0,96},{16,112},{32,0},{48,16},{64,32},{80,48},{96,64},{112,80},{1... | collective-permute-start | bytes 393224 | tf_op jit(solution)/shard_map/ppermute | solution.py:53
  201.9 10.0 %collective-permute-start.39 = (f32[256,128]{1,0:T(8,128)}, f32[256,128]{1,0:T(8,128)}, u32[]{:S(2)}, u32[]{:S(2)}) collective-permute-start(f32[256,128]{1,0:T(8,128)} %get-tuple-element.69.ratio), channel_id=1, source_target_pairs={{0,32},{16,48},{32,64},{48,80},{64,96},{80,112},{96,0},{112,16},{1... | collective-permute-start | bytes 393224 | tf_op jit(solution)/shard_map/ppermute | solution.py:53
  211.8 17.7 %collective-permute-start.14 = (bf16[192,8192]{1,0:T(8,128)(2,1)}, bf16[192,8192]{1,0:T(8,128)(2,1)S(1)}, u32[]{:S(2)}, u32[]{:S(2)}) collective-permute-start(bf16[192,8192]{1,0:T(8,128)(2,1)} %get-tuple-element.48), channel_id=1, source_target_pairs={{0,1},{1,0},{2,3},{3,2},{4,5},{5,4},{6,7},{7,6},{8,9},{9,8},{10,11... | collective-permute-start | bytes 9437192 | tf_op jit(solution)/shard_map/ppermute | solution.py:49
  211.9 15.5 %collective-permute-start.44 = (f32[256,1]{1,0:T(8,128)S(1)}, f32[256,1]{1,0:T(8,128)S(1)}, u32[]{:S(2)}, u32[]{:S(2)}) collective-permute-start(f32[256,1]{1,0:T(8,128)S(1)} %bitcast.57), channel_id=1, source_target_pairs={{0,16},{16,0},{32,48},{48,32},{64,80},{80,64},{96,112},{112,96},{1... | collective-permute-start | bytes 3080 | tf_op jit(solution)/shard_map/ppermute | solution.py:57
  213.7 38.8 %collective-permute-start.46 = (bf16[3,256,512]{2,1,0:T(8,128)(2,1)}, bf16[3,256,512]{2,1,0:T(8,128)(2,1)S(1)}, u32[]{:S(2)}, u32[]{:S(2)}) collective-permute-start(bf16[3,256,512]{2,1,0:T(8,128)(2,1)} %get-tuple-element.81), channel_id=1, source_target_pairs={{0,96},{16,112},{32,0},{48,16},{64,32},{80,48},{96,64},{112,80},{1... | collective-permute-start | bytes 2359304 | tf_op jit(solution)/shard_map/ppermute | solution.py:53
  216.9 35.6 %collective-permute-start.43 = (bf16[3,256,512]{2,1,0:T(8,128)(2,1)}, bf16[3,256,512]{2,1,0:T(8,128)(2,1)S(1)}, u32[]{:S(2)}, u32[]{:S(2)}) collective-permute-start(bf16[3,256,512]{2,1,0:T(8,128)(2,1)} %get-tuple-element.76), channel_id=1, source_target_pairs={{0,16},{16,0},{32,48},{48,32},{64,80},{80,64},{96,112},{112,96},{1... | collective-permute-start | bytes 2359304 | tf_op jit(solution)/shard_map/ppermute | solution.py:57
  223.7 27.5 %collective-permute-start.42 = (bf16[3,256,512]{2,1,0:T(8,128)(2,1)S(1)}, bf16[3,256,512]{2,1,0:T(8,128)(2,1)S(1)}, u32[]{:S(2)}, u32[]{:S(2)}) collective-permute-start(bf16[3,256,512]{2,1,0:T(8,128)(2,1)S(1)} %get-tuple-element.74), channel_id=1, source_target_pairs={{0,96},{16,112},{32,0},{48,16},{64,32},{80,48},{96,64},{112,80},{1... | collective-permute-start | bytes 2359304 | tf_op jit(solution)/shard_map/ppermute | solution.py:53
  227.2 46.2 %slice-start = ((s8[7864320]{0:T(1024)(128)(4,1)}), s8[4194304]{0:T(1024)(128)(4,1)S(1)}, s32[]{:S(2)}) async-start(s8[7864320]{0:T(1024)(128)(4,1)} %bitcast.55), calls=%async_computation | async-start | bytes 8388608
  227.5 25.1 %collective-permute-start.41 = (bf16[3,256,512]{2,1,0:T(8,128)(2,1)S(1)}, bf16[3,256,512]{2,1,0:T(8,128)(2,1)S(1)}, u32[]{:S(2)}, u32[]{:S(2)}) collective-permute-start(bf16[3,256,512]{2,1,0:T(8,128)(2,1)S(1)} %get-tuple-element.73), channel_id=1, source_target_pairs={{0,32},{16,48},{32,64},{48,80},{64,96},{80,112},{96,0},{112,16},{1... | collective-permute-start | bytes 2359304 | tf_op jit(solution)/shard_map/ppermute | solution.py:53
  229.5 24.5 %collective-permute-start.47 = (bf16[48,8192]{1,0:T(8,128)(2,1)S(1)}, bf16[48,8192]{1,0:T(8,128)(2,1)S(1)}, u32[]{:S(2)}, u32[]{:S(2)}) collective-permute-start(bf16[48,8192]{1,0:T(8,128)(2,1)S(1)} %get-tuple-element.99), channel_id=1, source_target_pairs={{0,6},{1,7},{2,0},{3,1},{4,2},{5,3},{6,4},{7,5},{8,14},{9,15},{10,... | collective-permute-start | bytes 2359304 | tf_op jit(solution)/shard_map/ppermute | solution.py:41
  251.2 18.8 %collective-permute-start.45 = (bf16[3,256,512]{2,1,0:T(8,128)(2,1)S(1)}, bf16[3,256,512]{2,1,0:T(8,128)(2,1)S(1)}, u32[]{:S(2)}, u32[]{:S(2)}) collective-permute-start(bf16[3,256,512]{2,1,0:T(8,128)(2,1)S(1)} %copy-done.22), channel_id=1, source_target_pairs={{0,16},{16,0},{32,48},{48,32},{64,80},{80,64},{96,112},{112,96},{1... | collective-permute-start | bytes 2359304 | tf_op jit(solution)/shard_map/ppermute | solution.py:57
  252.5 20.9 %collective-permute-start.36 = (bf16[3,256,512]{2,1,0:T(8,128)(2,1)S(1)}, bf16[3,256,512]{2,1,0:T(8,128)(2,1)S(1)}, u32[]{:S(2)}, u32[]{:S(2)}) collective-permute-start(bf16[3,256,512]{2,1,0:T(8,128)(2,1)S(1)} %copy-done.23), channel_id=1, source_target_pairs={{0,32},{16,48},{32,64},{48,80},{64,96},{80,112},{96,0},{112,16},{1... | collective-permute-start | bytes 2359304 | tf_op jit(solution)/shard_map/ppermute | solution.py:53
  252.6 42.0 %collective-permute-start.32 = (bf16[48,8192]{1,0:T(8,128)(2,1)S(1)}, bf16[48,8192]{1,0:T(8,128)(2,1)S(1)}, u32[]{:S(2)}, u32[]{:S(2)}) collective-permute-start(bf16[48,8192]{1,0:T(8,128)(2,1)S(1)} %get-tuple-element.98), channel_id=1, source_target_pairs={{0,2},{1,3},{2,4},{3,5},{4,6},{5,7},{6,0},{7,1},{8,10},{9,11},{10,... | collective-permute-start | bytes 2359304 | tf_op jit(solution)/shard_map/ppermute | solution.py:41
  252.6 36.6 %collective-permute-start.35 = (bf16[48,8192]{1,0:T(8,128)(2,1)S(1)}, bf16[48,8192]{1,0:T(8,128)(2,1)S(1)}, u32[]{:S(2)}, u32[]{:S(2)}) collective-permute-start(bf16[48,8192]{1,0:T(8,128)(2,1)S(1)} %get-tuple-element.100), channel_id=1, source_target_pairs={{0,2},{1,3},{2,4},{3,5},{4,6},{5,7},{6,0},{7,1},{8,10},{9,11},{10,... | collective-permute-start | bytes 2359304 | tf_op jit(solution)/shard_map/ppermute | solution.py:41
  254.2 38.7 %collective-permute-start.48 = (bf16[48,8192]{1,0:T(8,128)(2,1)S(1)}, bf16[48,8192]{1,0:T(8,128)(2,1)S(1)}, u32[]{:S(2)}, u32[]{:S(2)}) collective-permute-start(bf16[48,8192]{1,0:T(8,128)(2,1)S(1)} %add_convert_fusion.4), channel_id=1, source_target_pairs={{0,6},{1,7},{2,0},{3,1},{4,2},{5,3},{6,4},{7,5},{8,14},{9,15},{10,... | collective-permute-start | bytes 2359304 | tf_op jit(solution)/shard_map/ppermute | solution.py:41
  270.0 7.0 %collective-permute-start.56 = (f32[256,1]{1,0:T(8,128)S(1)}, f32[256,1]{1,0:T(8,128)S(1)}, u32[]{:S(2)}, u32[]{:S(2)}) collective-permute-start(f32[256,1]{1,0:T(8,128)S(1)} %get-tuple-element.101), channel_id=1, source_target_pairs={{0,64},{16,80},{32,96},{48,112},{64,0},{80,16},{96,32},{112,48},{1... | collective-permute-start | bytes 3080 | tf_op jit(solution)/shard_map/ppermute | solution.py:53
  275.4 39.3 %collective-permute-start.50 = (bf16[3,256,512]{2,1,0:T(8,128)(2,1)S(1)}, bf16[3,256,512]{2,1,0:T(8,128)(2,1)S(1)}, u32[]{:S(2)}, u32[]{:S(2)}) collective-permute-start(bf16[3,256,512]{2,1,0:T(8,128)(2,1)S(1)} %get-tuple-element.95), channel_id=1, source_target_pairs={{0,32},{16,48},{32,64},{48,80},{64,96},{80,112},{96,0},{112,16},{1... | collective-permute-start | bytes 2359304 | tf_op jit(solution)/shard_map/ppermute | solution.py:53
  277.0 38.9 %collective-permute-start.51 = (bf16[3,256,512]{2,1,0:T(8,128)(2,1)S(1)}, bf16[3,256,512]{2,1,0:T(8,128)(2,1)S(1)}, u32[]{:S(2)}, u32[]{:S(2)}) collective-permute-start(bf16[3,256,512]{2,1,0:T(8,128)(2,1)S(1)} %get-tuple-element.93), channel_id=1, source_target_pairs={{0,32},{16,48},{32,64},{48,80},{64,96},{80,112},{96,0},{112,16},{1... | collective-permute-start | bytes 2359304 | tf_op jit(solution)/shard_map/ppermute | solution.py:53
  289.2 29.6 %collective-permute-start.52 = (bf16[3,256,512]{2,1,0:T(8,128)(2,1)S(1)}, bf16[3,256,512]{2,1,0:T(8,128)(2,1)S(1)}, u32[]{:S(2)}, u32[]{:S(2)}) collective-permute-start(bf16[3,256,512]{2,1,0:T(8,128)(2,1)S(1)} %get-tuple-element.94), channel_id=1, source_target_pairs={{0,96},{16,112},{32,0},{48,16},{64,32},{80,48},{96,64},{112,80},{1... | collective-permute-start | bytes 2359304 | tf_op jit(solution)/shard_map/ppermute | solution.py:53
  292.9 32.0 %collective-permute-start.53 = (bf16[3,256,512]{2,1,0:T(8,128)(2,1)S(1)}, bf16[3,256,512]{2,1,0:T(8,128)(2,1)S(1)}, u32[]{:S(2)}, u32[]{:S(2)}) collective-permute-start(bf16[3,256,512]{2,1,0:T(8,128)(2,1)S(1)} %get-tuple-element.92), channel_id=1, source_target_pairs={{0,96},{16,112},{32,0},{48,16},{64,32},{80,48},{96,64},{112,80},{1... | collective-permute-start | bytes 2359304 | tf_op jit(solution)/shard_map/ppermute | solution.py:53
  294.6 19.3 %collective-permute-start.57 = (f32[256,1]{1,0:T(8,128)S(1)}, f32[256,1]{1,0:T(8,128)S(1)}, u32[]{:S(2)}, u32[]{:S(2)}) collective-permute-start(f32[256,1]{1,0:T(8,128)S(1)} %add.360), channel_id=1, source_target_pairs={{0,32},{16,48},{32,64},{48,80},{64,96},{80,112},{96,0},{112,16},{1... | collective-permute-start | bytes 3080 | tf_op jit(solution)/shard_map/ppermute | solution.py:53
  313.9 20.4 %collective-permute-start.54 = (bf16[3,256,512]{2,1,0:T(8,128)(2,1)S(1)}, bf16[3,256,512]{2,1,0:T(8,128)(2,1)S(1)}, u32[]{:S(2)}, u32[]{:S(2)}) collective-permute-start(bf16[3,256,512]{2,1,0:T(8,128)(2,1)S(1)} %get-tuple-element.91), channel_id=1, source_target_pairs={{0,16},{16,0},{32,48},{48,32},{64,80},{80,64},{96,112},{112,96},{1... | collective-permute-start | bytes 2359304 | tf_op jit(solution)/shard_map/ppermute | solution.py:57
  314.8 36.4 %collective-permute-start.55 = (bf16[3,256,512]{2,1,0:T(8,128)(2,1)S(1)}, bf16[3,256,512]{2,1,0:T(8,128)(2,1)S(1)}, u32[]{:S(2)}, u32[]{:S(2)}) collective-permute-start(bf16[3,256,512]{2,1,0:T(8,128)(2,1)S(1)} %get-tuple-element.90), channel_id=1, source_target_pairs={{0,16},{16,0},{32,48},{48,32},{64,80},{80,64},{96,112},{112,96},{1... | collective-permute-start | bytes 2359304 | tf_op jit(solution)/shard_map/ppermute | solution.py:57
  315.9 37.6 %collective-permute-start.34 = (bf16[48,8192]{1,0:T(8,128)(2,1)S(1)}, bf16[48,8192]{1,0:T(8,128)(2,1)S(1)}, u32[]{:S(2)}, u32[]{:S(2)}) collective-permute-start(bf16[48,8192]{1,0:T(8,128)(2,1)S(1)} %slice.105), channel_id=1, source_target_pairs={{0,6},{1,7},{2,0},{3,1},{4,2},{5,3},{6,4},{7,5},{8,14},{9,15},{10,... | collective-permute-start | bytes 2359304 | tf_op jit(solution)/shard_map/ppermute | solution.py:41
  318.8 46.0 %collective-permute-start.49 = (bf16[48,8192]{1,0:T(8,128)(2,1)S(1)}, bf16[48,8192]{1,0:T(8,128)(2,1)S(1)}, u32[]{:S(2)}, u32[]{:S(2)}) collective-permute-start(bf16[48,8192]{1,0:T(8,128)(2,1)S(1)} %get-tuple-element.97), channel_id=1, source_target_pairs={{0,8},{1,9},{2,10},{3,11},{4,12},{5,13},{6,14},{7,15},{8,0},{9,1},... | collective-permute-start | bytes 2359304 | tf_op jit(solution)/shard_map/ppermute | solution.py:45
  325.0 39.9 %collective-permute-start.33 = (bf16[48,8192]{1,0:T(8,128)(2,1)S(1)}, bf16[48,8192]{1,0:T(8,128)(2,1)S(1)}, u32[]{:S(2)}, u32[]{:S(2)}) collective-permute-start(bf16[48,8192]{1,0:T(8,128)(2,1)S(1)} %get-tuple-element.96), channel_id=1, source_target_pairs={{0,2},{1,3},{2,4},{3,5},{4,6},{5,7},{6,0},{7,1},{8,10},{9,11},{10,... | collective-permute-start | bytes 2359304 | tf_op jit(solution)/shard_map/ppermute | solution.py:41
  (20 other events, 397.2 us)

commit v2 on v1

--- a/solution.py
+++ b/solution.py
@@ -11,7 +11,7 @@
 epsilon = 1e-06
 INTERPRET = False
 VMEM = (64 << 20) - 400000
-VMEM_SMALL = 20 << 20
+VMEM_SMALL = 16 << 20
 
 PLACES = ((0, 0), (-1, 0), (1, 0), (0, 1), (-1, 1), (1, 1), (2, 0), (2, 1))
 BATCHES = ((0, 1, 2, 3), (4, 5, 6), (7,))
@@ -21,7 +21,7 @@
     (0, 1, 0), (0, 1, 1), (0, 0, 0), (0, 0, 1),
 )
 EARLY = 4
-ALONE = 2
+ALONE = 4
 
 
 def fsdp_pairs(dx, dy, dc):
@@ -153,27 +153,48 @@
     )(*ggus, w_gate, w_up)
 
 
-def relay_kernel(pieces, a, b, ratio, low, high, left, right):
+def relay_kernel(own_a, own_b, a, b, ratio, low, high, left, right):
     factor = ratio[:, :1]
-    for half, (value, other, out) in enumerate(((a, low, left), (b, high, right))):
+    for own, value, other, out in ((own_a, a, low, left), (own_b, b, high, right)):
         scale = other[:, :1]
         for m in range(3):
-            out[m] = bf(f32(pieces[half, m]) * factor + f32(value[m]) * scale)
-
-
-def relay(pieces, a, b, ratio, low, high):
-    _, _, hid, block = pieces.shape
-    whole = [pl.BlockSpec(v.shape, lambda k, n=v.ndim: (0,) * n) for v in (a, b, ratio, low, high)]
+            out[m] = bf(f32(own[m]) * factor + f32(value[m]) * scale)
+
+
+def relay(*arrays):
+    whole = [pl.BlockSpec(v.shape, lambda k, n=v.ndim: (0,) * n) for v in arrays]
     return pl.pallas_call(
         relay_kernel,
         name="relay",
         grid=(1,),
-        in_specs=[pl.BlockSpec((2, 3, hid, block), lambda k: (0, 0, 0, 0))] + whole,
+        in_specs=whole,
+        out_specs=whole[:2],
+        out_shape=[jax.ShapeDtypeStruct(arrays[0].shape, jnp.bfloat16)] * 2,
+        compiler_params=pltpu.CompilerParams(vmem_limit_bytes=VMEM_SMALL),
+        interpret=INTERPRET,
+    )(*arrays)
+
+
+def join_kernel(pieces, a, b, ratio, left, right):
+    factor = ratio[:, :1]
+    for half, (value, out) in enumerate(((a, left), (b, right))):
+        for m in range(3):
+            out[m] = bf(f32(pieces[half, m]) * factor + f32(value[m]))
+
+
+def join(pieces, first, a, b, ratio):
+    _, _, hid, block = pieces.shape
+    whole = [pl.BlockSpec(v.shape, lambda k, n=v.ndim: (0,) * n) for v in (a, b, ratio)]
+    return pl.pallas_call(
+        join_kernel,
+        name="join",
+        grid=(1,),
+        in_specs=[pl.BlockSpec((2, 3, hid, block), lambda k: (first // 2, 0, 0, 0))] + whole,
         out_specs=whole[:2],
         out_shape=[jax.ShapeDtypeStruct(a.shape, jnp.bfloat16)] * 2,
-        compiler_params=pltpu.CompilerParams(vmem_limit_bytes=VMEM_SMALL),
-        interpret=INTERPRET,
-    )(pieces, a, b, ratio, low, high)
+        compiler_params=pltpu.CompilerParams(vmem_limit_bytes=VMEM),
+        interpret=INTERPRET,
+    )(pieces, a, b, ratio)
 
 
 def last_kernel(pieces, l0, l1, r0, r1, n0, n1, ratio, total, gate, up, down):
@@ -389,19 +410,17 @@
         outs.append(out)
         ggus.append(ggu)
         hids.append(hidden)
-    near, near_p = input_gradient(ggus[:1], w_gate, w_up)
-    near = bf(f32(near) + f32(to_core(near_p)))
-
     *first, ggu_t, hid_t, moment = gradients_early(target[:EARLY], toks, outs, ggus, hids)
     a, b = to_z(first[0], 1), to_z(first[1], -1)
     c, d = to_y_next(first[2]), to_y_next(first[3])
     far, far_p = input_gradient([after(ggus[1], moment), ggus[2]], w_gate, w_up)
     far_p, moment = lax.optimization_barrier((far_p, moment))
-    far = bf(f32(far) + f32(to_core(far_p)))
-    e, f, pieces, ratio = gradients_late(target[EARLY:], toks, outs, ggu_t, hid_t, moment)
+    far_p = to_core(far_p)
+    far = bf(f32(far) + f32(far_p))
+    e, f, own_g, own_h, pieces, ratio = gradients_late(target[EARLY:], toks, outs, ggu_t, hid_t, moment)
     low, high = to_z(ratio, 1), to_z(ratio, -1)
-    left, right = relay(pieces, a, b, ratio, low, high)
-    ratio = ratio[:, :1]
+    left, right = relay(own_g, own_h, a, b, ratio, low, high)
+    ratio_lanes, ratio = ratio, ratio[:, :1]
     from_low, from_high, from_next = low[:, :1], high[:, :1], to_y_next(ratio)
 
     def own(k):
@@ -412,26 +431,25 @@
 
     e, f = to_z(e, 1), to_z(f, -1)
     g, h = to_z(left, 1), to_z(right, -1)
+    third_y = join(pieces, 12 - EARLY - ALONE, g, h, ratio_lanes)
     from_next = after(from_next, g, h)
-    c, d, e, f = after(c, g, h), after(d, g, h), after(e, g, h), after(f, g, h)
     third = (
         bf(own(8) + theirs(e, from_low)),
         bf(own(9) + theirs(c, from_next)),
         bf(own(10) + theirs(d, from_next)),
         bf(own(11) + theirs(f, from_high)),
-        bf(own(12) + f32(g)),
-        bf(own(13) + f32(h)),
     )
     others = (
         to_z(third[0], 1), to_z(third[1], 1),
         to_z(third[2], -1), to_z(third[3], -1),
-        to_y_next(third[4]), to_y_next(third[5]),
+        to_y_next(third_y[0]), to_y_next(third_y[1]),
     )
     total = ratio + from_next
-    total = total + to_z(total, 2)
-    total = total + to_z(total, 1)
+    total = total + to_z(total, 1) + to_z(total, -1) + to_z(total, 2)
     grad_gate, grad_up, grad_down = last_sum(pieces, others, ratio, total)
 
+    near, near_p = input_gradient([after(ggus[0], left)], w_gate, w_up)
+    near = bf(f32(near) + f32(to_core(near_p)))
     part = [value[i : i + rows] for value in (near, far) for i in range(0, 4 * rows, rows)]
     far_0, far_1 = to_x(part[6], 1), to_x(part[7], -1)
     up_1, down_0 = to_x(part[5], 1), to_x(part[1], -1)

time: 367 us -> 388 us (1.057)
  waiting for transfers between devices: 187 us -> 202 us
  other arithmetic: 10.1 us -> 17.6 us
  starting transfers between devices: 62.8 us -> 56 us
  Pallas kernels: 97 us -> 101 us
    ppermute x14 -> x15, waiting for transfers between devices: 42.3 us -> 59.6 us  [to_z(): return lax.ppermute(value, 'lang', lang_pairs(step, 0))]
    ppermute x16, waiting for transfers between devices: 58.7 us -> 69.2 us  [to_x(): return lax.ppermute(value, 'fsdp', fsdp_pairs(step, 0, 0))]
    ppermute x5, waiting for transfers between devices: 39.8 us -> 30.9 us  [to_y_next(): return lax.ppermute(value, 'lang', lang_pairs(0, 1))]
    convert_element_type x5, other arithmetic: 6.75 us -> 13.4 us  [bf(): return value.astype(jnp.bfloat16)]
    ppermute x5, waiting for transfers between devices: 42.2 us -> 37.5 us  [to_y_half(): return lax.ppermute(value, 'fsdp', fsdp_pairs(0, 1, 0))]
    ppermute x14 -> x15, starting transfers between devices: 21.8 us -> 17.8 us  [to_z(): return lax.ppermute(value, 'lang', lang_pairs(step, 0))]
  transfers between devices with their start and end apart: 58 -> 59, of which waited for: 22 -> 21; matrix products, arithmetic and copies ran while one was open for 4% -> 6% of each run, Pallas kernels for 18% -> 18%
where the time goes in v2:
time: 388 us; the launch traced here: 387 us
  waiting for transfers between devices  202 us (52%)
  Pallas kernels  101 us (26%)
  starting transfers between devices  56 us (14%)
  other arithmetic  17.6 us (5%)
  local copies, waits for them, and re-layouts  10.1 us (3%)
    ppermute x16, waiting for transfers between devices, to_x(): return lax.ppermute(value, 'fsdp', fsdp_pairs(step, 0, 0))  69.2 us
    ppermute x15, waiting for transfers between devices, to_z(): return lax.ppermute(value, 'lang', lang_pairs(step, 0))  59.6 us
    pallas_call x3, Pallas kernels, forward(): pl.pallas_call(functools.partial(forward_kernel, n), name='forward', grid...  44 us
    ppermute x5, waiting for transfers between devices, to_y_half(): return lax.ppermute(value, 'fsdp', fsdp_pairs(0, 1, 0))  37.5 us
    ppermute x5, waiting for transfers between devices, to_y_next(): return lax.ppermute(value, 'lang', lang_pairs(0, 1))  30.9 us
    ppermute x16, starting transfers between devices, to_x(): return lax.ppermute(value, 'fsdp', fsdp_pairs(step, 0, 0))  21.3 us
    pallas_call x1, Pallas kernels, gradients_late(): pl.pallas_call(functools.partial(late_kernel, len(toks), depth), name='la...  19.7 us
    pallas_call x2, Pallas kernels, input_gradient(): pl.pallas_call(functools.partial(input_kernel, len(ggus)), name='input',...  19.6 us
  transfers between devices with their start and end apart: 59, of which 21 were waited for; matrix products, arithmetic and copies ran while one was open for 6% of the time, Pallas kernels for 18%

profile of v2, /device:TPU:0, one launch (start us, length us, event | category | flops | bytes accessed | tf_op | source)
XLA Modules:
  0.0 387.1 jit_solution(16451173464510946034)
XLA Ops:
  0.6 1.7 collective-permute-start
  2.3 3.2 collective-permute-start.2
  5.8 1.6 collective-permute-start.8
  7.5 1.7 collective-permute-start.1
  9.1 12.2 %collective-permute-done.refs_1_ = bf16[48,8192]{1,0:T(8,128)(2,1)S(1)} collective-permute-done((bf16[48,8192]{1,0:T(8,128)(2,1)}, bf16[48,8192]{1,0:T(8,128)(2,1)S(1)}, u32[]{:S(2)}, u32[]{:S(2)}) %collective-permute-start) | collective-permute-done | bytes 786464 | tf_op jit(solution)/shard_map/ppermute | solution.py:41
  21.3 3.1 collective-permute-done.2.refs_3_
  24.4 1.5 collective-permute-start.7
  25.9 14.0 %collective-permute-done.9.refs_11_ = bf16[48,8192]{1,0:T(8,128)(2,1)S(1)} collective-permute-done((bf16[48,8192]{1,0:T(8,128)(2,1)}, bf16[48,8192]{1,0:T(8,128)(2,1)S(1)}, u32[]{:S(2)}, u32[]{:S(2)}) %collective-permute-start.9) | collective-permute-done | bytes 786464 | tf_op jit(solution)/shard_map/ppermute | solution.py:45
  39.9 3.3 collective-permute-start.14
  43.2 1.7 collective-permute-start.15
  45.2 1.5 collective-permute-start.20
  46.7 1.4 collective-permute-start.21
  48.1 13.8 %collective-permute-done.14.refs_0_ = bf16[48,8192]{1,0:T(8,128)(2,1)S(1)} collective-permute-done((bf16[48,8192]{1,0:T(8,128)(2,1)S(1)}, bf16[48,8192]{1,0:T(8,128)(2,1)S(1)}, u32[]{:S(2)}, u32[]{:S(2)}) %collective-permute-start.14) | collective-permute-done | bytes 786464 | tf_op jit(solution)/shard_map/ppermute | solution.py:45
  61.9 1.7 collective-permute-start.22
  63.7 2.8 collective-permute-done.16.refs_2_
  66.6 15.8 %collective-permute-done.20.refs_6_ = bf16[48,8192]{1,0:T(8,128)(2,1)} collective-permute-done((bf16[48,8192]{1,0:T(8,128)(2,1)S(1)}, bf16[48,8192]{1,0:T(8,128)(2,1)}, u32[]{:S(2)}, u32[]{:S(2)}) %collective-permute-start.20) | collective-permute-done | bytes 786464 | tf_op jit(solution)/shard_map/ppermute | solution.py:41
  83.6 1.1 collective-permute-done.6.refs_7_
  84.8 1.0 collective-permute-done.11.refs_13_
  85.9 1.0 collective-permute-done.12.refs_14_
  86.9 1.1 collective-permute-done.13.refs_15_
  88.1 2.2 collective-permute-start.28
  91.9 15.9 %collective-permute-done.26.refs_0_ = bf16[48,8192]{1,0:T(8,128)(2,1)} collective-permute-done((bf16[48,8192]{1,0:T(8,128)(2,1)S(1)}, bf16[48,8192]{1,0:T(8,128)(2,1)}, u32[]{:S(2)}, u32[]{:S(2)}) %collective-permute-start.26) | collective-permute-done | bytes 786464 | tf_op jit(solution)/shard_map/ppermute | solution.py:41
  112.3 17.8 %forward.3 = (bf16[384,512]{1,0:T(8,128)(2,1)}, bf16[384,256]{1,0:T(8,128)(2,1)}, bf16[384,8192]{1,0:T(8,128)(2,1)}, bf16[384,8192]{1,0:T(8,128)(2,1)}) custom-call(bf16[48,8192]{1,0:T(8,128)(2,1)} %bitcast.57, bf16[48,8192]{1,0:T(8,128)(2,1)} %copy-done.9, bf16[48,8192]{1,0:T(8,128)(2,1)} %copy-done.13, bf16[48,8192]{1,0:T(8,128)(2,1)} %copy-done.10, ...), custom_call_target="tpu_custom_call" | custom-call | tf_op jit(solution)/shard_map/forward/pallas_call | solution.py:105
  130.1 15.3 %forward.4 = (bf16[288,512]{1,0:T(8,128)(2,1)}, bf16[288,256]{1,0:T(8,128)(2,1)}, bf16[288,8192]{1,0:T(8,128)(2,1)}, bf16[288,8192]{1,0:T(8,128)(2,1)}) custom-call(bf16[48,8192]{1,0:T(8,128)(2,1)} %copy-done.14, bf16[48,8192]{1,0:T(8,128)(2,1)} %copy-done.16, bf16[48,8192]{1,0:T(8,128)(2,1)} %copy-done.18, bf16[48,8192]{1,0:T(8,128)(2,1)} %copy-done.23, ...), custom_call_target="tpu_custom_call" | custom-call | tf_op jit(solution)/shard_map/forward/pallas_call | solution.py:105
  145.5 10.8 %forward.5 = (bf16[96,512]{1,0:T(8,128)(2,1)}, bf16[96,256]{1,0:T(8,128)(2,1)}, bf16[96,8192]{1,0:T(8,128)(2,1)}, bf16[96,8192]{1,0:T(8,128)(2,1)}) custom-call(bf16[48,8192]{1,0:T(8,128)(2,1)} %collective-permute-done.26.refs_0_, bf16[48,8192]{1,0:T(8,128)(2,1)} %collective-permute-done.27.refs_1_, bf16[48,8192]{1,0:T(8,128)(2,1)} %collective-permute-done.28.refs_2_, ...), custom_call_target="tpu_custom_call" | custom-call | tf_op jit(solution)/shard_map/forward/pallas_call | solution.py:105
  156.3 9.4 %early.1 = (bf16[3,256,512]{2,1,0:T(8,128)(2,1)}, bf16[3,256,512]{2,1,0:T(8,128)(2,1)}, bf16[3,256,512]{2,1,0:T(8,128)(2,1)}, bf16[3,256,512]{2,1,0:T(8,128)(2,1...) custom-call(s32[4]{0:T(128)} %pad_add_fusion.place, ...), custom_call_target="tpu_custom_call" | custom-call | tf_op jit(solution)/shard_map/early/pallas_call | solution.py:313
  165.7 9.9 %input.2 = (bf16[192,8192]{1,0:T(8,128)(2,1)}, bf16[192,8192]{1,0:T(8,128)(2,1)}) custom-call(bf16[288,512]{1,0:T(8,128)(2,1)} %get-tuple-element.62.refs_7_.refs_0_, bf16[96,512]{1,0:T(8,128)(2,1)} %get-tuple-element.55.refs_8_.refs_1_, bf16[8192,256]{1,0:T(8,128)(2,1)} %refs_1_.1, bf16[8192,256]{1,0:T(8,128)(2,1)} %refs_2_.3), custom_call_target="tpu_custom_call" | custom-call | tf_op jit(solution)/shard_map/input/pallas_call | solution.py:143
  175.6 2.0 collective-permute-start.30
  177.6 2.2 collective-permute-start.31
  180.5 19.7 %late.1 = (bf16[3,256,512]{2,1,0:T(8,128)(2,1)}, bf16[3,256,512]{2,1,0:T(8,128)(2,1)}, bf16[3,256,512]{2,1,0:T(8,128)(2,1)}, bf16[3,256,512]{2,1,0:T(8,128)(2,1)...) custom-call(s32[12]{0:T(128)} %stack.133.place, bf16[384,8192]{1,0:T(8,128)(2,1)} %get-tuple-element.48.refs_0_, ...), custom_call_target="tpu_custom_call" | custom-call | tf_op jit(solution)/shard_map/late/pallas_call | solution.py:336
  200.2 3.2 collective-permute-start.33
  203.4 3.7 collective-permute-done.32.low
  207.8 1.4 collective-permute-start.42
  209.8 2.3 collective-permute-start.46
  213.0 1.1 copy-done.2
  214.1 1.1 copy-done.3
  215.3 2.0 relay.1
  219.1 9.8 %input.3 = (bf16[192,8192]{1,0:T(8,128)(2,1)}, bf16[192,8192]{1,0:T(8,128)(2,1)}) custom-call(bf16[384,512]{1,0:T(8,128)(2,1)} %get-tuple-element.71.refs_6_.refs_0_, bf16[8192,256]{1,0:T(8,128)(2,1)} %refs_1_.1, bf16[8192,256]{1,0:T(8,128)(2,1)} %refs_2_.3), custom_call_target="tpu_custom_call" | custom-call | tf_op jit(solution)/shard_map/input/pallas_call | solution.py:143
  228.9 4.0 %add_convert_fusion = bf16[192,8192]{1,0:T(8,128)(2,1)S(1)} fusion(bf16[192,8192]{1,0:T(8,128)(2,1)} %collective-permute-done.35, bf16[192,8192]{1,0:T(8,128)(2,1)} %get-tuple-element.74), kind=kLoop, calls=%fused_computation | loop fusion | flops 6291456 | bytes 9437184 | tf_op jit(solution)/shard_map/convert_element_type | solution.py:363
  233.3 17.4 %collective-permute-done.43.a = bf16[3,256,512]{2,1,0:T(8,128)(2,1)S(1)} collective-permute-done((bf16[3,256,512]{2,1,0:T(8,128)(2,1)}, bf16[3,256,512]{2,1,0:T(8,128)(2,1)S(1)}, u32[]{:S(2)}, u32[]{:S(2)}) %collective-permute-start.43) | collective-permute-done | bytes 786464 | tf_op jit(solution)/shard_map/ppermute | solution.py:53
  250.7 1.6 fusion.9
  252.4 12.1 %collective-permute-done.44.b = bf16[3,256,512]{2,1,0:T(8,128)(2,1)S(1)} collective-permute-done((bf16[3,256,512]{2,1,0:T(8,128)(2,1)S(1)}, bf16[3,256,512]{2,1,0:T(8,128)(2,1)S(1)}, u32[]{:S(2)}, u32[]{:S(2)}) %collective-permute-start.44) | collective-permute-done | bytes 786464 | tf_op jit(solution)/shard_map/ppermute | solution.py:53
  264.6 2.2 collective-permute-start.47
  267.0 3.5 join.1
  270.5 1.0 slice_add_fusion
  271.6 2.2 collective-permute-start.57
  273.9 4.2 %fusion.3 = (bf16[3,256,512]{2,1,0:T(8,128)(2,1)S(1)}, bf16[3,256,512]{2,1,0:T(8,128)(2,1)S(1)}, bf16[3,256,512]{2,1,0:T(8,128)(2,1)S(1)}, bf16[3,256,512]{2,1,0:T(8,128)(2,1)S(1)}) fusion(bf16[3,256,512]{2,1,0:T(8,128)(2,1)} %collective-permute-done.45, bf16[8,3,256,512]{3,2,1,0:T(8,128)(2,1)} %get-tuple-element.76.pieces, f32[256]{0:T(256)S(1)} %get-tuple-element.101, ...), kind=kLoop, calls=%fused_computation.8 | loop fusion | flops 9437184 | bytes 9441280 | tf_op jit(solution)/shard_map/convert_element_type | solution.py:363
  278.1 2.1 collective-permute-done.47
  280.2 1.7 add_convert_fusion.4
  282.0 3.3 collective-permute-start.48
  285.3 3.1 add_convert_fusion.1
  288.4 20.2 %collective-permute-done.39 = bf16[48,8192]{1,0:T(8,128)(2,1)S(1)} collective-permute-done((bf16[48,8192]{1,0:T(8,128)(2,1)S(1)}, bf16[48,8192]{1,0:T(8,128)(2,1)S(1)}, u32[]{:S(2)}, u32[]{:S(2)}) %collective-permute-start.39) | collective-permute-done | bytes 786464 | tf_op jit(solution)/shard_map/ppermute | solution.py:41
  308.7 1.8 collective-permute-start.51
  310.5 1.6 collective-permute-start.52
  312.1 1.9 collective-permute-start.53
  314.6 26.4 %collective-permute-done.56 = f32[256,1]{1,0:T(8,128)S(1)} collective-permute-done((f32[256,1]{1,0:T(8,128)S(1)}, f32[256,1]{1,0:T(8,128)S(1)}, u32[]{:S(2)}, u32[]{:S(2)}) %collective-permute-start.56) | collective-permute-done | bytes 1056 | tf_op jit(solution)/shard_map/ppermute | solution.py:53
  341.0 2.0 collective-permute-start.55
  343.0 1.0 collective-permute-start.49
  344.0 1.9 collective-permute-start.37
  346.0 15.4 %collective-permute-done.54.n0 = bf16[3,256,512]{2,1,0:T(8,128)(2,1)S(1)} collective-permute-done((bf16[3,256,512]{2,1,0:T(8,128)(2,1)S(1)}, bf16[3,256,512]{2,1,0:T(8,128)(2,1)S(1)}, u32[]{:S(2)}, u32[]{:S(2)}) %collective-permute-start.54) | collective-permute-done | bytes 786464 | tf_op jit(solution)/shard_map/ppermute | solution.py:57
  361.4 15.5 %collective-permute-done.55.n1 = bf16[3,256,512]{2,1,0:T(8,128)(2,1)S(1)} collective-permute-done((bf16[3,256,512]{2,1,0:T(8,128)(2,1)S(1)}, bf16[3,256,512]{2,1,0:T(8,128)(2,1)S(1)}, u32[]{:S(2)}, u32[]{:S(2)}) %collective-permute-start.55) | collective-permute-done | bytes 786464 | tf_op jit(solution)/shard_map/ppermute | solution.py:57
  376.9 2.3 last.1
  379.2 6.6 %collective-permute-done.49 = bf16[48,8192]{1,0:T(8,128)(2,1)S(1)} collective-permute-done((bf16[48,8192]{1,0:T(8,128)(2,1)S(1)}, bf16[48,8192]{1,0:T(8,128)(2,1)S(1)}, u32[]{:S(2)}, u32[]{:S(2)}) %collective-permute-start.49) | collective-permute-done | bytes 786464 | tf_op jit(solution)/shard_map/ppermute | solution.py:45
  385.8 1.3 fusion.8
  (162 shorter events, 14.5 us)
Async XLA Ops:
  0.6 20.7 %collective-permute-start = (bf16[48,8192]{1,0:T(8,128)(2,1)}, bf16[48,8192]{1,0:T(8,128)(2,1)S(1)}, u32[]{:S(2)}, u32[]{:S(2)}) collective-permute-start(bf16[48,8192]{1,0:T(8,128)(2,1)} %bitcast.53), channel_id=1, source_target_pairs={{0,2},{1,3},{2,4},{3,5},{4,6},{5,7},{6,0},{7,1},{8,10},{9,11},{10,... | collective-permute-start | bytes 2359304 | tf_op jit(solution)/shard_map/ppermute | solution.py:41
  2.3 22.1 %collective-permute-start.2 = (bf16[48,8192]{1,0:T(8,128)(2,1)}, bf16[48,8192]{1,0:T(8,128)(2,1)S(1)}, u32[]{:S(2)}, u32[]{:S(2)}) collective-permute-start(bf16[48,8192]{1,0:T(8,128)(2,1)} %bitcast.54), channel_id=1, source_target_pairs={{0,8},{1,9},{2,10},{3,11},{4,12},{5,13},{6,14},{7,15},{8,0},{9,1},... | collective-permute-start | bytes 2359304 | tf_op jit(solution)/shard_map/ppermute | solution.py:45
  5.5 34.4 %collective-permute-start.9 = (bf16[48,8192]{1,0:T(8,128)(2,1)}, bf16[48,8192]{1,0:T(8,128)(2,1)S(1)}, u32[]{:S(2)}, u32[]{:S(2)}) collective-permute-start(bf16[48,8192]{1,0:T(8,128)(2,1)} %bitcast.58), channel_id=1, source_target_pairs={{0,8},{1,9},{2,10},{3,11},{4,12},{5,13},{6,14},{7,15},{8,0},{9,1},... | collective-permute-start | bytes 2359304 | tf_op jit(solution)/shard_map/ppermute | solution.py:45
  5.8 34.1 %collective-permute-start.8 = (bf16[48,8192]{1,0:T(8,128)(2,1)}, bf16[48,8192]{1,0:T(8,128)(2,1)S(1)}, u32[]{:S(2)}, u32[]{:S(2)}) collective-permute-start(bf16[48,8192]{1,0:T(8,128)(2,1)} %bitcast.59), channel_id=1, source_target_pairs={{0,6},{1,7},{2,0},{3,1},{4,2},{5,3},{6,4},{7,5},{8,14},{9,15},{10,... | collective-permute-start | bytes 2359304 | tf_op jit(solution)/shard_map/ppermute | solution.py:41
  7.5 35.7 %collective-permute-start.1 = (bf16[48,8192]{1,0:T(8,128)(2,1)}, bf16[48,8192]{1,0:T(8,128)(2,1)S(1)}, u32[]{:S(2)}, u32[]{:S(2)}) collective-permute-start(bf16[48,8192]{1,0:T(8,128)(2,1)} %bitcast.55), channel_id=1, source_target_pairs={{0,6},{1,7},{2,0},{3,1},{4,2},{5,3},{6,4},{7,5},{8,14},{9,15},{10,... | collective-permute-start | bytes 2359304 | tf_op jit(solution)/shard_map/ppermute | solution.py:41
  21.3 23.6 %collective-permute-start.3 = (bf16[48,8192]{1,0:T(8,128)(2,1)}, bf16[48,8192]{1,0:T(8,128)(2,1)S(1)}, u32[]{:S(2)}, u32[]{:S(2)}) collective-permute-start(bf16[48,8192]{1,0:T(8,128)(2,1)} %bitcast.56), channel_id=1, source_target_pairs={{0,1},{1,0},{2,3},{3,2},{4,5},{5,4},{6,7},{7,6},{8,9},{9,8},{10,11... | collective-permute-start | bytes 2359304 | tf_op jit(solution)/shard_map/ppermute | solution.py:49
  24.4 58.6 %copy-start.10 = (bf16[48,8192]{1,0:T(8,128)(2,1)}, bf16[48,8192]{1,0:T(8,128)(2,1)S(1)}, u32[]{:S(2)}) copy-start(bf16[48,8192]{1,0:T(8,128)(2,1)S(1)} %collective-permute-done.2.refs_3_) | copy-start | bytes 2359300
  24.4 20.8 %collective-permute-start.7 = (bf16[48,8192]{1,0:T(8,128)(2,1)}, bf16[48,8192]{1,0:T(8,128)(2,1)S(1)}, u32[]{:S(2)}, u32[]{:S(2)}) collective-permute-start(bf16[48,8192]{1,0:T(8,128)(2,1)} %bitcast.60), channel_id=1, source_target_pairs={{0,2},{1,3},{2,4},{3,5},{4,6},{5,7},{6,0},{7,1},{8,10},{9,11},{10,... | collective-permute-start | bytes 2359304 | tf_op jit(solution)/shard_map/ppermute | solution.py:41
  39.9 6.8 %collective-permute-start.10 = (bf16[48,8192]{1,0:T(8,128)(2,1)}, bf16[48,8192]{1,0:T(8,128)(2,1)S(1)}, u32[]{:S(2)}, u32[]{:S(2)}) collective-permute-start(bf16[48,8192]{1,0:T(8,128)(2,1)} %bitcast.61), channel_id=1, source_target_pairs={{0,1},{1,0},{2,3},{3,2},{4,5},{5,4},{6,7},{7,6},{8,9},{9,8},{10,11... | collective-permute-start | bytes 2359304 | tf_op jit(solution)/shard_map/ppermute | solution.py:49
  39.9 48.2 %copy-start.12 = (bf16[48,8192]{1,0:T(8,128)(2,1)}, bf16[48,8192]{1,0:T(8,128)(2,1)S(1)}, u32[]{:S(2)}) copy-start(bf16[48,8192]{1,0:T(8,128)(2,1)S(1)} %collective-permute-done.8.refs_10_) | copy-start | bytes 2359300
  39.9 22.0 %collective-permute-start.14 = (bf16[48,8192]{1,0:T(8,128)(2,1)S(1)}, bf16[48,8192]{1,0:T(8,128)(2,1)S(1)}, u32[]{:S(2)}, u32[]{:S(2)}) collective-permute-start(bf16[48,8192]{1,0:T(8,128)(2,1)S(1)} %collective-permute-done.refs_1_), channel_id=1, source_target_pairs={{0,8},{1,9},{2,10},{3,11},{4,12},{5,13},{6,14},{7,15},{8,0},{9,1},... | collective-permute-start | bytes 2359304 | tf_op jit(solution)/shard_map/ppermute | solution.py:45
  43.2 47.1 %copy-start.13 = (bf16[48,8192]{1,0:T(8,128)(2,1)}, bf16[48,8192]{1,0:T(8,128)(2,1)S(1)}, u32[]{:S(2)}) copy-start(bf16[48,8192]{1,0:T(8,128)(2,1)S(1)} %collective-permute-done.1.refs_2_) | copy-start | bytes 2359300
  43.2 20.4 %collective-permute-start.15 = (bf16[48,8192]{1,0:T(8,128)(2,1)S(1)}, bf16[48,8192]{1,0:T(8,128)(2,1)S(1)}, u32[]{:S(2)}, u32[]{:S(2)}) collective-permute-start(bf16[48,8192]{1,0:T(8,128)(2,1)S(1)} %collective-permute-done.2.refs_3_), channel_id=1, source_target_pairs={{0,6},{1,7},{2,0},{3,1},{4,2},{5,3},{6,4},{7,5},{8,14},{9,15},{10,... | collective-permute-start | bytes 2359304 | tf_op jit(solution)/shard_map/ppermute | solution.py:41
  44.9 21.6 %collective-permute-start.16 = (bf16[48,8192]{1,0:T(8,128)(2,1)S(1)}, bf16[48,8192]{1,0:T(8,128)(2,1)S(1)}, u32[]{:S(2)}, u32[]{:S(2)}) collective-permute-start(bf16[48,8192]{1,0:T(8,128)(2,1)S(1)} %collective-permute-done.refs_1_), channel_id=1, source_target_pairs={{0,2},{1,3},{2,4},{3,5},{4,6},{5,7},{6,0},{7,1},{8,10},{9,11},{10,... | collective-permute-start | bytes 2359304 | tf_op jit(solution)/shard_map/ppermute | solution.py:41
  45.2 37.2 %collective-permute-start.20 = (bf16[48,8192]{1,0:T(8,128)(2,1)S(1)}, bf16[48,8192]{1,0:T(8,128)(2,1)}, u32[]{:S(2)}, u32[]{:S(2)}) collective-permute-start(bf16[48,8192]{1,0:T(8,128)(2,1)S(1)} %collective-permute-done.9.refs_11_), channel_id=1, source_target_pairs={{0,2},{1,3},{2,4},{3,5},{4,6},{5,7},{6,0},{7,1},{8,10},{9,11},{10,... | collective-permute-start | bytes 2359304 | tf_op jit(solution)/shard_map/ppermute | solution.py:41
  46.7 35.7 %collective-permute-start.21 = (bf16[48,8192]{1,0:T(8,128)(2,1)S(1)}, bf16[48,8192]{1,0:T(8,128)(2,1)}, u32[]{:S(2)}, u32[]{:S(2)}) collective-permute-start(bf16[48,8192]{1,0:T(8,128)(2,1)S(1)} %collective-permute-done.8.refs_10_), channel_id=1, source_target_pairs={{0,8},{1,9},{2,10},{3,11},{4,12},{5,13},{6,14},{7,15},{8,0},{9,1},... | collective-permute-start | bytes 2359304 | tf_op jit(solution)/shard_map/ppermute | solution.py:45
  61.9 21.0 %collective-permute-start.22 = (bf16[48,8192]{1,0:T(8,128)(2,1)S(1)}, bf16[48,8192]{1,0:T(8,128)(2,1)}, u32[]{:S(2)}, u32[]{:S(2)}) collective-permute-start(bf16[48,8192]{1,0:T(8,128)(2,1)S(1)} %collective-permute-done.8.refs_10_), channel_id=1, source_target_pairs={{0,6},{1,7},{2,0},{3,1},{4,2},{5,3},{6,4},{7,5},{8,14},{9,15},{10,... | collective-permute-start | bytes 2359304 | tf_op jit(solution)/shard_map/ppermute | solution.py:41
  63.6 19.4 %collective-permute-start.4 = (bf16[48,8192]{1,0:T(8,128)(2,1)S(1)}, bf16[48,8192]{1,0:T(8,128)(2,1)S(1)}, u32[]{:S(2)}, u32[]{:S(2)}) collective-permute-start(bf16[48,8192]{1,0:T(8,128)(2,1)S(1)} %collective-permute-done.refs_1_), channel_id=1, source_target_pairs={{0,1},{1,0},{2,3},{3,2},{4,5},{5,4},{6,7},{7,6},{8,9},{9,8},{10,11... | collective-permute-start | bytes 2359304 | tf_op jit(solution)/shard_map/ppermute | solution.py:49
  66.5 17.0 %collective-permute-start.5 = (bf16[48,8192]{1,0:T(8,128)(2,1)S(1)}, bf16[48,8192]{1,0:T(8,128)(2,1)S(1)}, u32[]{:S(2)}, u32[]{:S(2)}) collective-permute-start(bf16[48,8192]{1,0:T(8,128)(2,1)S(1)} %collective-permute-done.1.refs_2_), channel_id=1, source_target_pairs={{0,1},{1,0},{2,3},{3,2},{4,5},{5,4},{6,7},{7,6},{8,9},{9,8},{10,11... | collective-permute-start | bytes 2359304 | tf_op jit(solution)/shard_map/ppermute | solution.py:49
  82.4 2.3 collective-permute-start.6
  82.4 3.4 collective-permute-start.11
  82.9 4.0 %collective-permute-start.12 = (bf16[48,8192]{1,0:T(8,128)(2,1)S(1)}, bf16[48,8192]{1,0:T(8,128)(2,1)S(1)}, u32[]{:S(2)}, u32[]{:S(2)}) collective-permute-start(bf16[48,8192]{1,0:T(8,128)(2,1)S(1)} %collective-permute-done.8.refs_10_), channel_id=1, source_target_pairs={{0,1},{1,0},{2,3},{3,2},{4,5},{5,4},{6,7},{7,6},{8,9},{9,8},{10,11... | collective-permute-start | bytes 2359304 | tf_op jit(solution)/shard_map/ppermute | solution.py:49
  83.0 5.0 %collective-permute-start.13 = (bf16[48,8192]{1,0:T(8,128)(2,1)S(1)}, bf16[48,8192]{1,0:T(8,128)(2,1)S(1)}, u32[]{:S(2)}, u32[]{:S(2)}) collective-permute-start(bf16[48,8192]{1,0:T(8,128)(2,1)S(1)} %collective-permute-done.9.refs_11_), channel_id=1, source_target_pairs={{0,1},{1,0},{2,3},{3,2},{4,5},{5,4},{6,7},{7,6},{8,9},{9,8},{10,11... | collective-permute-start | bytes 2359304 | tf_op jit(solution)/shard_map/ppermute | solution.py:49
  83.5 7.7 %collective-permute-start.17 = (bf16[48,8192]{1,0:T(8,128)(2,1)S(1)}, bf16[48,8192]{1,0:T(8,128)(2,1)S(1)}, u32[]{:S(2)}, u32[]{:S(2)}) collective-permute-start(bf16[48,8192]{1,0:T(8,128)(2,1)S(1)} %collective-permute-done.14.refs_0_), channel_id=1, source_target_pairs={{0,1},{1,0},{2,3},{3,2},{4,5},{5,4},{6,7},{7,6},{8,9},{9,8},{10,11... | collective-permute-start | bytes 2359304 | tf_op jit(solution)/shard_map/ppermute | solution.py:49
  84.7 6.6 %collective-permute-start.18 = (bf16[48,8192]{1,0:T(8,128)(2,1)S(1)}, bf16[48,8192]{1,0:T(8,128)(2,1)}, u32[]{:S(2)}, u32[]{:S(2)}) collective-permute-start(bf16[48,8192]{1,0:T(8,128)(2,1)S(1)} %collective-permute-done.15.refs_1_), channel_id=1, source_target_pairs={{0,1},{1,0},{2,3},{3,2},{4,5},{5,4},{6,7},{7,6},{8,9},{9,8},{10,11... | collective-permute-start | bytes 2359304 | tf_op jit(solution)/shard_map/ppermute | solution.py:49
  85.8 6.0 %collective-permute-start.19 = (bf16[48,8192]{1,0:T(8,128)(2,1)S(1)}, bf16[48,8192]{1,0:T(8,128)(2,1)}, u32[]{:S(2)}, u32[]{:S(2)}) collective-permute-start(bf16[48,8192]{1,0:T(8,128)(2,1)S(1)} %collective-permute-done.16.refs_2_), channel_id=1, source_target_pairs={{0,1},{1,0},{2,3},{3,2},{4,5},{5,4},{6,7},{7,6},{8,9},{9,8},{10,11... | collective-permute-start | bytes 2359304 | tf_op jit(solution)/shard_map/ppermute | solution.py:49
  86.9 20.9 %collective-permute-start.26 = (bf16[48,8192]{1,0:T(8,128)(2,1)S(1)}, bf16[48,8192]{1,0:T(8,128)(2,1)}, u32[]{:S(2)}, u32[]{:S(2)}) collective-permute-start(bf16[48,8192]{1,0:T(8,128)(2,1)S(1)} %collective-permute-done.14.refs_0_), channel_id=1, source_target_pairs={{0,2},{1,3},{2,4},{3,5},{4,6},{5,7},{6,0},{7,1},{8,10},{9,11},{10,... | collective-permute-start | bytes 2359304 | tf_op jit(solution)/shard_map/ppermute | solution.py:41
  88.1 19.9 %collective-permute-start.28 = (bf16[48,8192]{1,0:T(8,128)(2,1)}, bf16[48,8192]{1,0:T(8,128)(2,1)}, u32[]{:S(2)}, u32[]{:S(2)}) collective-permute-start(bf16[48,8192]{1,0:T(8,128)(2,1)} %collective-permute-done.21.refs_7_), channel_id=1, source_target_pairs={{0,6},{1,7},{2,0},{3,1},{4,2},{5,3},{6,4},{7,5},{8,14},{9,15},{10,... | collective-permute-start | bytes 2359304 | tf_op jit(solution)/shard_map/ppermute | solution.py:41
  91.2 38.9 %collective-permute-start.24 = (bf16[48,8192]{1,0:T(8,128)(2,1)}, bf16[48,8192]{1,0:T(8,128)(2,1)}, u32[]{:S(2)}, u32[]{:S(2)}) collective-permute-start(bf16[48,8192]{1,0:T(8,128)(2,1)} %collective-permute-done.21.refs_7_), channel_id=1, source_target_pairs={{0,1},{1,0},{2,3},{3,2},{4,5},{5,4},{6,7},{7,6},{8,9},{9,8},{10,11... | collective-permute-start | bytes 2359304 | tf_op jit(solution)/shard_map/ppermute | solution.py:49
  91.3 38.8 %collective-permute-start.23 = (bf16[48,8192]{1,0:T(8,128)(2,1)}, bf16[48,8192]{1,0:T(8,128)(2,1)}, u32[]{:S(2)}, u32[]{:S(2)}) collective-permute-start(bf16[48,8192]{1,0:T(8,128)(2,1)} %collective-permute-done.20.refs_6_), channel_id=1, source_target_pairs={{0,1},{1,0},{2,3},{3,2},{4,5},{5,4},{6,7},{7,6},{8,9},{9,8},{10,11... | collective-permute-start | bytes 2359304 | tf_op jit(solution)/shard_map/ppermute | solution.py:49
  91.8 38.3 %collective-permute-start.25 = (bf16[48,8192]{1,0:T(8,128)(2,1)}, bf16[48,8192]{1,0:T(8,128)(2,1)}, u32[]{:S(2)}, u32[]{:S(2)}) collective-permute-start(bf16[48,8192]{1,0:T(8,128)(2,1)} %collective-permute-done.22.refs_8_), channel_id=1, source_target_pairs={{0,1},{1,0},{2,3},{3,2},{4,5},{5,4},{6,7},{7,6},{8,9},{9,8},{10,11... | collective-permute-start | bytes 2359304 | tf_op jit(solution)/shard_map/ppermute | solution.py:49
  107.8 37.6 %collective-permute-start.27 = (bf16[48,8192]{1,0:T(8,128)(2,1)}, bf16[48,8192]{1,0:T(8,128)(2,1)}, u32[]{:S(2)}, u32[]{:S(2)}) collective-permute-start(bf16[48,8192]{1,0:T(8,128)(2,1)} %collective-permute-done.26.refs_0_), channel_id=1, source_target_pairs={{0,1},{1,0},{2,3},{3,2},{4,5},{5,4},{6,7},{7,6},{8,9},{9,8},{10,11... | collective-permute-start | bytes 2359304 | tf_op jit(solution)/shard_map/ppermute | solution.py:49
  108.0 37.5 %collective-permute-start.29 = (bf16[48,8192]{1,0:T(8,128)(2,1)}, bf16[48,8192]{1,0:T(8,128)(2,1)}, u32[]{:S(2)}, u32[]{:S(2)}) collective-permute-start(bf16[48,8192]{1,0:T(8,128)(2,1)} %collective-permute-done.28.refs_2_), channel_id=1, source_target_pairs={{0,1},{1,0},{2,3},{3,2},{4,5},{5,4},{6,7},{7,6},{8,9},{9,8},{10,11... | collective-permute-start | bytes 2359304 | tf_op jit(solution)/shard_map/ppermute | solution.py:49
  175.6 53.2 %collective-permute-start.35 = (bf16[192,8192]{1,0:T(8,128)(2,1)}, bf16[192,8192]{1,0:T(8,128)(2,1)}, u32[]{:S(2)}, u32[]{:S(2)}) collective-permute-start(bf16[192,8192]{1,0:T(8,128)(2,1)} %get-tuple-element.75), channel_id=1, source_target_pairs={{0,1},{1,0},{2,3},{3,2},{4,5},{5,4},{6,7},{7,6},{8,9},{9,8},{10,11... | collective-permute-start | bytes 9437192 | tf_op jit(solution)/shard_map/ppermute | solution.py:49
  175.6 33.5 %collective-permute-start.30 = (bf16[3,256,512]{2,1,0:T(8,128)(2,1)}, bf16[3,256,512]{2,1,0:T(8,128)(2,1)}, u32[]{:S(2)}, u32[]{:S(2)}) collective-permute-start(bf16[3,256,512]{2,1,0:T(8,128)(2,1)} %get-tuple-element.67), channel_id=1, source_target_pairs={{0,32},{16,48},{32,64},{48,80},{64,96},{80,112},{96,0},{112,16},{1... | collective-permute-start | bytes 2359304 | tf_op jit(solution)/shard_map/ppermute | solution.py:53
  177.6 32.2 %collective-permute-start.31 = (bf16[3,256,512]{2,1,0:T(8,128)(2,1)}, bf16[3,256,512]{2,1,0:T(8,128)(2,1)}, u32[]{:S(2)}, u32[]{:S(2)}) collective-permute-start(bf16[3,256,512]{2,1,0:T(8,128)(2,1)} %get-tuple-element.68), channel_id=1, source_target_pairs={{0,96},{16,112},{32,0},{48,16},{64,32},{80,48},{96,64},{112,80},{1... | collective-permute-start | bytes 2359304 | tf_op jit(solution)/shard_map/ppermute | solution.py:53
  200.1 7.0 %collective-permute-start.32 = (f32[256,128]{1,0:T(8,128)}, f32[256,128]{1,0:T(8,128)S(1)}, u32[]{:S(2)}, u32[]{:S(2)}) collective-permute-start(f32[256,128]{1,0:T(8,128)} %get-tuple-element.69.ratio), channel_id=1, source_target_pairs={{0,32},{16,48},{32,64},{48,80},{64,96},{80,112},{96,0},{112,16},{1... | collective-permute-start | bytes 393224 | tf_op jit(solution)/shard_map/ppermute | solution.py:53
  200.2 7.6 %collective-permute-start.33 = (f32[256,128]{1,0:T(8,128)}, f32[256,128]{1,0:T(8,128)S(1)}, u32[]{:S(2)}, u32[]{:S(2)}) collective-permute-start(f32[256,128]{1,0:T(8,128)} %get-tuple-element.69.ratio), channel_id=1, source_target_pairs={{0,96},{16,112},{32,0},{48,16},{64,32},{80,48},{96,64},{112,80},{1... | collective-permute-start | bytes 393224 | tf_op jit(solution)/shard_map/ppermute | solution.py:53
  207.1 26.1 %collective-permute-start.45 = (bf16[3,256,512]{2,1,0:T(8,128)(2,1)}, bf16[3,256,512]{2,1,0:T(8,128)(2,1)}, u32[]{:S(2)}, u32[]{:S(2)}) collective-permute-start(bf16[3,256,512]{2,1,0:T(8,128)(2,1)} %get-tuple-element.81), channel_id=1, source_target_pairs={{0,16},{16,0},{32,48},{48,32},{64,80},{80,64},{96,112},{112,96},{1... | collective-permute-start | bytes 2359304 | tf_op jit(solution)/shard_map/ppermute | solution.py:57
  207.8 25.1 %collective-permute-start.42 = (f32[256,1]{1,0:T(8,128)}, f32[256,1]{1,0:T(8,128)}, u32[]{:S(2)}, u32[]{:S(2)}) collective-permute-start(f32[256,1]{1,0:T(8,128)} %bitcast.51), channel_id=1, source_target_pairs={{0,16},{16,0},{32,48},{48,32},{64,80},{80,64},{96,112},{112,96},{1... | collective-permute-start | bytes 3080 | tf_op jit(solution)/shard_map/ppermute | solution.py:57
  209.1 62.4 %collective-permute-start.41 = (bf16[3,256,512]{2,1,0:T(8,128)(2,1)}, bf16[3,256,512]{2,1,0:T(8,128)(2,1)}, u32[]{:S(2)}, u32[]{:S(2)}) collective-permute-start(bf16[3,256,512]{2,1,0:T(8,128)(2,1)} %get-tuple-element.78), channel_id=1, source_target_pairs={{0,16},{16,0},{32,48},{48,32},{64,80},{80,64},{96,112},{112,96},{1... | collective-permute-start | bytes 2359304 | tf_op jit(solution)/shard_map/ppermute | solution.py:57
  209.8 61.8 %collective-permute-start.46 = (bf16[3,256,512]{2,1,0:T(8,128)(2,1)}, bf16[3,256,512]{2,1,0:T(8,128)(2,1)}, u32[]{:S(2)}, u32[]{:S(2)}) collective-permute-start(bf16[3,256,512]{2,1,0:T(8,128)(2,1)} %get-tuple-element.82), channel_id=1, source_target_pairs={{0,96},{16,112},{32,0},{48,16},{64,32},{80,48},{96,64},{112,80},{1... | collective-permute-start | bytes 2359304 | tf_op jit(solution)/shard_map/ppermute | solution.py:53
  228.8 21.9 %collective-permute-start.43 = (bf16[3,256,512]{2,1,0:T(8,128)(2,1)}, bf16[3,256,512]{2,1,0:T(8,128)(2,1)S(1)}, u32[]{:S(2)}, u32[]{:S(2)}) collective-permute-start(bf16[3,256,512]{2,1,0:T(8,128)(2,1)} %copy-done.6), channel_id=1, source_target_pairs={{0,32},{16,48},{32,64},{48,80},{64,96},{80,112},{96,0},{112,16},{1... | collective-permute-start | bytes 2359304 | tf_op jit(solution)/shard_map/ppermute | solution.py:53
  232.9 40.9 %collective-permute-start.40 = (bf16[3,256,512]{2,1,0:T(8,128)(2,1)}, bf16[3,256,512]{2,1,0:T(8,128)(2,1)}, u32[]{:S(2)}, u32[]{:S(2)}) collective-permute-start(bf16[3,256,512]{2,1,0:T(8,128)(2,1)} %get-tuple-element.77), channel_id=1, source_target_pairs={{0,32},{16,48},{32,64},{48,80},{64,96},{80,112},{96,0},{112,16},{1... | collective-permute-start | bytes 2359304 | tf_op jit(solution)/shard_map/ppermute | solution.py:53
  233.2 48.7 %collective-permute-start.34 = (bf16[192,8192]{1,0:T(8,128)(2,1)}, bf16[192,8192]{1,0:T(8,128)(2,1)}, u32[]{:S(2)}, u32[]{:S(2)}) collective-permute-start(bf16[192,8192]{1,0:T(8,128)(2,1)} %get-tuple-element.73), channel_id=1, source_target_pairs={{0,1},{1,0},{2,3},{3,2},{4,5},{5,4},{6,7},{7,6},{8,9},{9,8},{10,11... | collective-permute-start | bytes 9437192 | tf_op jit(solution)/shard_map/ppermute | solution.py:49
  250.7 13.8 %collective-permute-start.44 = (bf16[3,256,512]{2,1,0:T(8,128)(2,1)S(1)}, bf16[3,256,512]{2,1,0:T(8,128)(2,1)S(1)}, u32[]{:S(2)}, u32[]{:S(2)}) collective-permute-start(bf16[3,256,512]{2,1,0:T(8,128)(2,1)S(1)} %copy-done.5), channel_id=1, source_target_pairs={{0,96},{16,112},{32,0},{48,16},{64,32},{80,48},{96,64},{112,80},{1... | collective-permute-start | bytes 2359304 | tf_op jit(solution)/shard_map/ppermute | solution.py:53
  264.6 15.7 %collective-permute-start.47 = (bf16[48,8192]{1,0:T(8,128)(2,1)}, bf16[48,8192]{1,0:T(8,128)(2,1)}, u32[]{:S(2)}, u32[]{:S(2)}) collective-permute-start(bf16[48,8192]{1,0:T(8,128)(2,1)} %get-tuple-element.97), channel_id=1, source_target_pairs={{0,6},{1,7},{2,0},{3,1},{4,2},{5,3},{6,4},{7,5},{8,14},{9,15},{10,... | collective-permute-start | bytes 2359304 | tf_op jit(solution)/shard_map/ppermute | solution.py:41
  271.5 38.9 %collective-permute-start.58 = (f32[256,1]{1,0:T(8,128)S(1)}, f32[256,1]{1,0:T(8,128)S(1)}, u32[]{:S(2)}, u32[]{:S(2)}) collective-permute-start(f32[256,1]{1,0:T(8,128)S(1)} %get-tuple-element.99), channel_id=1, source_target_pairs={{0,64},{16,80},{32,96},{48,112},{64,0},{80,16},{96,32},{112,48},{1... | collective-permute-start | bytes 3080 | tf_op jit(solution)/shard_map/ppermute | solution.py:53
  271.6 40.4 %collective-permute-start.57 = (f32[256,1]{1,0:T(8,128)S(1)}, f32[256,1]{1,0:T(8,128)S(1)}, u32[]{:S(2)}, u32[]{:S(2)}) collective-permute-start(f32[256,1]{1,0:T(8,128)S(1)} %get-tuple-element.99), channel_id=1, source_target_pairs={{0,96},{16,112},{32,0},{48,16},{64,32},{80,48},{96,64},{112,80},{1... | collective-permute-start | bytes 3080 | tf_op jit(solution)/shard_map/ppermute | solution.py:53
  278.1 35.9 %collective-permute-start.36 = (bf16[48,8192]{1,0:T(8,128)(2,1)S(1)}, bf16[48,8192]{1,0:T(8,128)(2,1)S(1)}, u32[]{:S(2)}, u32[]{:S(2)}) collective-permute-start(bf16[48,8192]{1,0:T(8,128)(2,1)S(1)} %copy-done.27), channel_id=1, source_target_pairs={{0,2},{1,3},{2,4},{3,5},{4,6},{5,7},{6,0},{7,1},{8,10},{9,11},{10,... | collective-permute-start | bytes 2359304 | tf_op jit(solution)/shard_map/ppermute | solution.py:41
  280.2 28.3 %collective-permute-start.39 = (bf16[48,8192]{1,0:T(8,128)(2,1)S(1)}, bf16[48,8192]{1,0:T(8,128)(2,1)S(1)}, u32[]{:S(2)}, u32[]{:S(2)}) collective-permute-start(bf16[48,8192]{1,0:T(8,128)(2,1)S(1)} %copy-done.28), channel_id=1, source_target_pairs={{0,2},{1,3},{2,4},{3,5},{4,6},{5,7},{6,0},{7,1},{8,10},{9,11},{10,... | collective-permute-start | bytes 2359304 | tf_op jit(solution)/shard_map/ppermute | solution.py:41
  280.2 96.7 %slice-start = ((s8[6291456]{0:T(1024)(128)(4,1)}), s8[4194304]{0:T(1024)(128)(4,1)S(1)}, s32[]{:S(2)}) async-start(s8[6291456]{0:T(1024)(128)(4,1)} %bitcast.49), calls=%async_computation | async-start | bytes 8388608
  282.0 26.7 %collective-permute-start.48 = (bf16[48,8192]{1,0:T(8,128)(2,1)S(1)}, bf16[48,8192]{1,0:T(8,128)(2,1)S(1)}, u32[]{:S(2)}, u32[]{:S(2)}) collective-permute-start(bf16[48,8192]{1,0:T(8,128)(2,1)S(1)} %add_convert_fusion.4), channel_id=1, source_target_pairs={{0,6},{1,7},{2,0},{3,1},{4,2},{5,3},{6,4},{7,5},{8,14},{9,15},{10,... | collective-permute-start | bytes 2359304 | tf_op jit(solution)/shard_map/ppermute | solution.py:41
  285.3 91.7 %slice-start.1 = ((s8[6291456]{0:T(1024)(128)(4,1)}), s8[2097152]{0:T(1024)(128)(4,1)S(1)}, s32[]{:S(2)}) async-start(s8[6291456]{0:T(1024)(128)(4,1)} %bitcast.49), calls=%async_computation.1 | async-start | bytes 4194304
  308.6 32.4 %collective-permute-start.50 = (bf16[3,256,512]{2,1,0:T(8,128)(2,1)S(1)}, bf16[3,256,512]{2,1,0:T(8,128)(2,1)S(1)}, u32[]{:S(2)}, u32[]{:S(2)}) collective-permute-start(bf16[3,256,512]{2,1,0:T(8,128)(2,1)S(1)} %get-tuple-element.93), channel_id=1, source_target_pairs={{0,32},{16,48},{32,64},{48,80},{64,96},{80,112},{96,0},{112,16},{1... | collective-permute-start | bytes 2359304 | tf_op jit(solution)/shard_map/ppermute | solution.py:53
  308.7 34.3 %collective-permute-start.51 = (bf16[3,256,512]{2,1,0:T(8,128)(2,1)S(1)}, bf16[3,256,512]{2,1,0:T(8,128)(2,1)S(1)}, u32[]{:S(2)}, u32[]{:S(2)}) collective-permute-start(bf16[3,256,512]{2,1,0:T(8,128)(2,1)S(1)} %get-tuple-element.91), channel_id=1, source_target_pairs={{0,32},{16,48},{32,64},{48,80},{64,96},{80,112},{96,0},{112,16},{1... | collective-permute-start | bytes 2359304 | tf_op jit(solution)/shard_map/ppermute | solution.py:53
  310.5 32.5 %collective-permute-start.52 = (bf16[3,256,512]{2,1,0:T(8,128)(2,1)S(1)}, bf16[3,256,512]{2,1,0:T(8,128)(2,1)S(1)}, u32[]{:S(2)}, u32[]{:S(2)}) collective-permute-start(bf16[3,256,512]{2,1,0:T(8,128)(2,1)S(1)} %get-tuple-element.90), channel_id=1, source_target_pairs={{0,96},{16,112},{32,0},{48,16},{64,32},{80,48},{96,64},{112,80},{1... | collective-permute-start | bytes 2359304 | tf_op jit(solution)/shard_map/ppermute | solution.py:53
  312.1 32.0 %collective-permute-start.53 = (bf16[3,256,512]{2,1,0:T(8,128)(2,1)S(1)}, bf16[3,256,512]{2,1,0:T(8,128)(2,1)S(1)}, u32[]{:S(2)}, u32[]{:S(2)}) collective-permute-start(bf16[3,256,512]{2,1,0:T(8,128)(2,1)S(1)} %get-tuple-element.92), channel_id=1, source_target_pairs={{0,96},{16,112},{32,0},{48,16},{64,32},{80,48},{96,64},{112,80},{1... | collective-permute-start | bytes 2359304 | tf_op jit(solution)/shard_map/ppermute | solution.py:53
  314.0 27.0 %collective-permute-start.56 = (f32[256,1]{1,0:T(8,128)S(1)}, f32[256,1]{1,0:T(8,128)S(1)}, u32[]{:S(2)}, u32[]{:S(2)}) collective-permute-start(f32[256,1]{1,0:T(8,128)S(1)} %get-tuple-element.99), channel_id=1, source_target_pairs={{0,32},{16,48},{32,64},{48,80},{64,96},{80,112},{96,0},{112,16},{1... | collective-permute-start | bytes 3080 | tf_op jit(solution)/shard_map/ppermute | solution.py:53
  341.0 20.4 %collective-permute-start.54 = (bf16[3,256,512]{2,1,0:T(8,128)(2,1)S(1)}, bf16[3,256,512]{2,1,0:T(8,128)(2,1)S(1)}, u32[]{:S(2)}, u32[]{:S(2)}) collective-permute-start(bf16[3,256,512]{2,1,0:T(8,128)(2,1)S(1)} %copy-done.32), channel_id=1, source_target_pairs={{0,16},{16,0},{32,48},{48,32},{64,80},{80,64},{96,112},{112,96},{1... | collective-permute-start | bytes 2359304 | tf_op jit(solution)/shard_map/ppermute | solution.py:57
  341.0 35.9 %collective-permute-start.55 = (bf16[3,256,512]{2,1,0:T(8,128)(2,1)S(1)}, bf16[3,256,512]{2,1,0:T(8,128)(2,1)S(1)}, u32[]{:S(2)}, u32[]{:S(2)}) collective-permute-start(bf16[3,256,512]{2,1,0:T(8,128)(2,1)S(1)} %copy-done.31), channel_id=1, source_target_pairs={{0,16},{16,0},{32,48},{48,32},{64,80},{80,64},{96,112},{112,96},{1... | collective-permute-start | bytes 2359304 | tf_op jit(solution)/shard_map/ppermute | solution.py:57
  343.0 36.2 %collective-permute-start.38 = (bf16[48,8192]{1,0:T(8,128)(2,1)S(1)}, bf16[48,8192]{1,0:T(8,128)(2,1)S(1)}, u32[]{:S(2)}, u32[]{:S(2)}) collective-permute-start(bf16[48,8192]{1,0:T(8,128)(2,1)S(1)} %slice.97), channel_id=1, source_target_pairs={{0,6},{1,7},{2,0},{3,1},{4,2},{5,3},{6,4},{7,5},{8,14},{9,15},{10,... | collective-permute-start | bytes 2359304 | tf_op jit(solution)/shard_map/ppermute | solution.py:41
  343.0 42.8 %collective-permute-start.49 = (bf16[48,8192]{1,0:T(8,128)(2,1)S(1)}, bf16[48,8192]{1,0:T(8,128)(2,1)S(1)}, u32[]{:S(2)}, u32[]{:S(2)}) collective-permute-start(bf16[48,8192]{1,0:T(8,128)(2,1)S(1)} %get-tuple-element.95), channel_id=1, source_target_pairs={{0,8},{1,9},{2,10},{3,11},{4,12},{5,13},{6,14},{7,15},{8,0},{9,1},... | collective-permute-start | bytes 2359304 | tf_op jit(solution)/shard_map/ppermute | solution.py:45
  344.0 41.8 %collective-permute-start.37 = (bf16[48,8192]{1,0:T(8,128)(2,1)S(1)}, bf16[48,8192]{1,0:T(8,128)(2,1)S(1)}, u32[]{:S(2)}, u32[]{:S(2)}) collective-permute-start(bf16[48,8192]{1,0:T(8,128)(2,1)S(1)} %get-tuple-element.94), channel_id=1, source_target_pairs={{0,2},{1,3},{2,4},{3,5},{4,6},{5,7},{6,0},{7,1},{8,10},{9,11},{10,... | collective-permute-start | bytes 2359304 | tf_op jit(solution)/shard_map/ppermute | solution.py:41
  (30 other events, 521.8 us)

commit v3 on v2

--- a/solution.py
+++ b/solution.py
@@ -17,11 +17,11 @@
 BATCHES = ((0, 1, 2, 3), (4, 5, 6), (7,))
 PIECES = (
     (2, 1, 0), (2, 1, 1), (1, 1, 1), (-1, 1, 0), (2, 0, 0), (2, 0, 1),
-    (1, 1, 0), (-1, 1, 1), (1, 0, 0), (1, 0, 1), (-1, 0, 0), (-1, 0, 1),
+    (1, 1, 0), (-1, 1, 1), (1, 0, 1), (-1, 0, 0), (1, 0, 0), (-1, 0, 1),
     (0, 1, 0), (0, 1, 1), (0, 0, 0), (0, 0, 1),
 )
 EARLY = 4
-ALONE = 4
+ALONE = 6
 
 
 def fsdp_pairs(dx, dy, dc):
@@ -417,11 +417,13 @@
     far_p, moment = lax.optimization_barrier((far_p, moment))
     far_p = to_core(far_p)
     far = bf(f32(far) + f32(far_p))
-    e, f, own_g, own_h, pieces, ratio = gradients_late(target[EARLY:], toks, outs, ggu_t, hid_t, moment)
+    e, f, own_g, own_h, own_l, own_r, pieces, ratio = gradients_late(target[EARLY:], toks, outs, ggu_t, hid_t, moment)
     low, high = to_z(ratio, 1), to_z(ratio, -1)
+    beside = to_y_next(ratio)
     left, right = relay(own_g, own_h, a, b, ratio, low, high)
+    left_1, right_0 = relay(own_l, own_r, c, d, ratio, beside, beside)
     ratio_lanes, ratio = ratio, ratio[:, :1]
-    from_low, from_high, from_next = low[:, :1], high[:, :1], to_y_next(ratio)
+    from_low, from_high, from_next = low[:, :1], high[:, :1], beside[:, :1]
 
     def own(k):
         return f32(pieces[k - EARLY - ALONE]) * ratio[None]
@@ -429,19 +431,14 @@
     def theirs(value, factor):
         return f32(value) * factor[None]
 
+    g, h = to_z(left, 1), to_z(right, -1)
     e, f = to_z(e, 1), to_z(f, -1)
-    g, h = to_z(left, 1), to_z(right, -1)
+    left_1, right_0 = to_z(left_1, 1), to_z(right_0, -1)
     third_y = join(pieces, 12 - EARLY - ALONE, g, h, ratio_lanes)
-    from_next = after(from_next, g, h)
-    third = (
-        bf(own(8) + theirs(e, from_low)),
-        bf(own(9) + theirs(c, from_next)),
-        bf(own(10) + theirs(d, from_next)),
-        bf(own(11) + theirs(f, from_high)),
-    )
+    from_next = after(from_next, left)
+    third = bf(own(10) + theirs(e, from_low)), bf(own(11) + theirs(f, from_high))
     others = (
-        to_z(third[0], 1), to_z(third[1], 1),
-        to_z(third[2], -1), to_z(third[3], -1),
+        to_z(third[0], 1), left_1, right_0, to_z(third[1], -1),
         to_y_next(third_y[0]), to_y_next(third_y[1]),
     )
     total = ratio + from_next
@@ -452,10 +449,12 @@
     near = bf(f32(near) + f32(to_core(near_p)))
     part = [value[i : i + rows] for value in (near, far) for i in range(0, 4 * rows, rows)]
     far_0, far_1 = to_x(part[6], 1), to_x(part[7], -1)
-    up_1, down_0 = to_x(part[5], 1), to_x(part[1], -1)
-    up_0, down_1 = bf(f32(part[2]) + f32(far_0)), bf(f32(part[4]) + f32(far_1))
-    up_0, down_1 = to_x(up_0, 1), to_x(down_1, -1)
-    up_1, down_1 = after(up_1, *third), after(down_1, *third)
+    up_1 = to_x(part[5], 1)
+    down_1 = bf(f32(part[4]) + f32(far_1))
+    down_1 = to_x(down_1, -1)
+    up_0 = bf(f32(part[2]) + f32(far_0))
+    up_0, down_0 = to_x(up_0, 1), to_x(part[1], -1)
+    up_1, down_1 = after(up_1, *third_y), after(down_1, *third_y)
     other = bf(f32(part[3]) + f32(up_1) + f32(down_1))
     other = to_y_half(other)
     grad_tokens = bf(f32(part[0]) + f32(up_0) + f32(down_0) + f32(other))[None]

time: 388 us -> 358 us (0.923)
  waiting for transfers between devices: 202 us -> 161 us
    ppermute x15, waiting for transfers between devices: 59.6 us -> 33.4 us  [to_z(): return lax.ppermute(value, 'lang', lang_pairs(step, 0))]
    ppermute x5, waiting for transfers between devices: 30.9 us -> 6.84 us  [to_y_next(): return lax.ppermute(value, 'lang', lang_pairs(0, 1))]
    ppermute x16, waiting for transfers between devices: 69.2 us -> 83.2 us  [to_x(): return lax.ppermute(value, 'fsdp', fsdp_pairs(step, 0, 0))]
    ppermute x5, waiting for transfers between devices: 37.5 us -> 33.4 us  [to_y_half(): return lax.ppermute(value, 'fsdp', fsdp_pairs(0, 1, 0))]
    unnamed x70 -> x90, local copies, waits for them, and re-layouts: 5.15 us -> 8.85 us
  transfers between devices with their start and end apart: 59 -> 59, of which waited for: 21 -> 20; matrix products, arithmetic and copies ran while one was open for 6% -> 6% of each run, Pallas kernels for 18% -> 20%
where the time goes in v3:
time: 358 us; the launch traced here: 357 us
  waiting for transfers between devices  161 us (45%)
  Pallas kernels  102 us (28%)
  starting transfers between devices  59.4 us (17%)
  other arithmetic  18.4 us (5%)
  local copies, waits for them, and re-layouts  13.8 us (4%)
    ppermute x16, waiting for transfers between devices, to_x(): return lax.ppermute(value, 'fsdp', fsdp_pairs(step, 0, 0))  83.2 us
    pallas_call x3, Pallas kernels, forward(): pl.pallas_call(functools.partial(forward_kernel, n), name='forward', grid...  43.9 us
    ppermute x15, waiting for transfers between devices, to_z(): return lax.ppermute(value, 'lang', lang_pairs(step, 0))  33.4 us
    ppermute x5, waiting for transfers between devices, to_y_half(): return lax.ppermute(value, 'fsdp', fsdp_pairs(0, 1, 0))  33.4 us
    ppermute x16, starting transfers between devices, to_x(): return lax.ppermute(value, 'fsdp', fsdp_pairs(step, 0, 0))  22 us
    ppermute x15, starting transfers between devices, to_z(): return lax.ppermute(value, 'lang', lang_pairs(step, 0))  21.5 us
    pallas_call x1, Pallas kernels, gradients_late(): pl.pallas_call(functools.partial(late_kernel, len(toks), depth), name='la...  19.9 us
    pallas_call x2, Pallas kernels, input_gradient(): pl.pallas_call(functools.partial(input_kernel, len(ggus)), name='input',...  19.7 us
  transfers between devices with their start and end apart: 59, of which 20 were waited for; matrix products, arithmetic and copies ran while one was open for 6% of the time, Pallas kernels for 20%

profile of v3, /device:TPU:0, one launch (start us, length us, event | category | flops | bytes accessed | tf_op | source)
XLA Modules:
  0.0 356.5 jit_solution(15531887084197165477)
XLA Ops:
  0.6 1.7 collective-permute-start
  2.3 3.2 collective-permute-start.2
  5.8 1.6 collective-permute-start.8
  7.5 1.7 collective-permute-start.1
  9.1 12.2 %collective-permute-done.refs_1_ = bf16[48,8192]{1,0:T(8,128)(2,1)S(1)} collective-permute-done((bf16[48,8192]{1,0:T(8,128)(2,1)}, bf16[48,8192]{1,0:T(8,128)(2,1)S(1)}, u32[]{:S(2)}, u32[]{:S(2)}) %collective-permute-start) | collective-permute-done | bytes 786464 | tf_op jit(solution)/shard_map/ppermute | solution.py:41
  21.3 3.1 collective-permute-done.2.refs_3_
  24.4 1.5 collective-permute-start.7
  25.9 14.0 %collective-permute-done.9.refs_11_ = bf16[48,8192]{1,0:T(8,128)(2,1)S(1)} collective-permute-done((bf16[48,8192]{1,0:T(8,128)(2,1)}, bf16[48,8192]{1,0:T(8,128)(2,1)S(1)}, u32[]{:S(2)}, u32[]{:S(2)}) %collective-permute-start.9) | collective-permute-done | bytes 786464 | tf_op jit(solution)/shard_map/ppermute | solution.py:45
  39.9 3.3 collective-permute-start.14
  43.2 1.7 collective-permute-start.15
  45.2 1.5 collective-permute-start.20
  46.7 1.4 collective-permute-start.21
  48.1 13.8 %collective-permute-done.14.refs_0_ = bf16[48,8192]{1,0:T(8,128)(2,1)S(1)} collective-permute-done((bf16[48,8192]{1,0:T(8,128)(2,1)S(1)}, bf16[48,8192]{1,0:T(8,128)(2,1)S(1)}, u32[]{:S(2)}, u32[]{:S(2)}) %collective-permute-start.14) | collective-permute-done | bytes 786464 | tf_op jit(solution)/shard_map/ppermute | solution.py:45
  61.9 1.7 collective-permute-start.22
  63.7 2.8 collective-permute-done.16.refs_2_
  66.6 15.8 %collective-permute-done.20.refs_6_ = bf16[48,8192]{1,0:T(8,128)(2,1)} collective-permute-done((bf16[48,8192]{1,0:T(8,128)(2,1)S(1)}, bf16[48,8192]{1,0:T(8,128)(2,1)}, u32[]{:S(2)}, u32[]{:S(2)}) %collective-permute-start.20) | collective-permute-done | bytes 786464 | tf_op jit(solution)/shard_map/ppermute | solution.py:41
  83.6 1.1 collective-permute-done.6.refs_7_
  84.8 1.0 collective-permute-done.11.refs_13_
  85.9 1.0 collective-permute-done.12.refs_14_
  86.9 1.1 collective-permute-done.13.refs_15_
  88.1 2.2 collective-permute-start.28
  91.9 15.9 %collective-permute-done.26.refs_0_ = bf16[48,8192]{1,0:T(8,128)(2,1)} collective-permute-done((bf16[48,8192]{1,0:T(8,128)(2,1)S(1)}, bf16[48,8192]{1,0:T(8,128)(2,1)}, u32[]{:S(2)}, u32[]{:S(2)}) %collective-permute-start.26) | collective-permute-done | bytes 786464 | tf_op jit(solution)/shard_map/ppermute | solution.py:41
  112.4 17.8 %forward.3 = (bf16[384,512]{1,0:T(8,128)(2,1)}, bf16[384,256]{1,0:T(8,128)(2,1)}, bf16[384,8192]{1,0:T(8,128)(2,1)}, bf16[384,8192]{1,0:T(8,128)(2,1)}) custom-call(bf16[48,8192]{1,0:T(8,128)(2,1)} %bitcast.50, bf16[48,8192]{1,0:T(8,128)(2,1)} %copy-done.20, bf16[48,8192]{1,0:T(8,128)(2,1)} %copy-done.24, bf16[48,8192]{1,0:T(8,128)(2,1)} %copy-done.21, ...), custom_call_target="tpu_custom_call" | custom-call | tf_op jit(solution)/shard_map/forward/pallas_call | solution.py:105
  130.2 15.3 %forward.4 = (bf16[288,512]{1,0:T(8,128)(2,1)}, bf16[288,256]{1,0:T(8,128)(2,1)}, bf16[288,8192]{1,0:T(8,128)(2,1)}, bf16[288,8192]{1,0:T(8,128)(2,1)}) custom-call(bf16[48,8192]{1,0:T(8,128)(2,1)} %copy-done.25, bf16[48,8192]{1,0:T(8,128)(2,1)} %copy-done.27, bf16[48,8192]{1,0:T(8,128)(2,1)} %copy-done.29, bf16[48,8192]{1,0:T(8,128)(2,1)} %copy-done.34, ...), custom_call_target="tpu_custom_call" | custom-call | tf_op jit(solution)/shard_map/forward/pallas_call | solution.py:105
  145.5 10.8 %forward.5 = (bf16[96,512]{1,0:T(8,128)(2,1)}, bf16[96,256]{1,0:T(8,128)(2,1)}, bf16[96,8192]{1,0:T(8,128)(2,1)}, bf16[96,8192]{1,0:T(8,128)(2,1)}) custom-call(bf16[48,8192]{1,0:T(8,128)(2,1)} %collective-permute-done.26.refs_0_, bf16[48,8192]{1,0:T(8,128)(2,1)} %collective-permute-done.27.refs_1_, bf16[48,8192]{1,0:T(8,128)(2,1)} %collective-permute-done.28.refs_2_, ...), custom_call_target="tpu_custom_call" | custom-call | tf_op jit(solution)/shard_map/forward/pallas_call | solution.py:105
  156.3 9.4 %early.1 = (bf16[3,256,512]{2,1,0:T(8,128)(2,1)}, bf16[3,256,512]{2,1,0:T(8,128)(2,1)}, bf16[3,256,512]{2,1,0:T(8,128)(2,1)}, bf16[3,256,512]{2,1,0:T(8,128)(2,1...) custom-call(s32[4]{0:T(128)} %pad_add_fusion.place, ...), custom_call_target="tpu_custom_call" | custom-call | tf_op jit(solution)/shard_map/early/pallas_call | solution.py:313
  165.8 9.9 %input.2 = (bf16[192,8192]{1,0:T(8,128)(2,1)}, bf16[192,8192]{1,0:T(8,128)(2,1)}) custom-call(bf16[288,512]{1,0:T(8,128)(2,1)} %get-tuple-element.66.refs_7_.refs_0_, bf16[96,512]{1,0:T(8,128)(2,1)} %get-tuple-element.59.refs_8_.refs_1_, bf16[8192,256]{1,0:T(8,128)(2,1)} %refs_1_.1, bf16[8192,256]{1,0:T(8,128)(2,1)} %refs_2_.3), custom_call_target="tpu_custom_call" | custom-call | tf_op jit(solution)/shard_map/input/pallas_call | solution.py:143
  175.7 2.0 collective-permute-start.30
  177.6 2.2 collective-permute-start.31
  180.5 19.9 %late.1 = (bf16[3,256,512]{2,1,0:T(8,128)(2,1)}, bf16[3,256,512]{2,1,0:T(8,128)(2,1)}, bf16[3,256,512]{2,1,0:T(8,128)(2,1)}, bf16[3,256,512]{2,1,0:T(8,128)(2,1)...) custom-call(s32[12]{0:T(128)} %stack.133.place, ...), custom_call_target="tpu_custom_call" | custom-call | tf_op jit(solution)/shard_map/late/pallas_call | solution.py:336
  200.5 3.2 collective-permute-start.33
  203.8 3.7 %collective-permute-done.32.low = f32[256,128]{1,0:T(8,128)S(1)} collective-permute-done((f32[256,128]{1,0:T(8,128)}, f32[256,128]{1,0:T(8,128)S(1)}, u32[]{:S(2)}, u32[]{:S(2)}) %collective-permute-start.32) | collective-permute-done | bytes 131104 | tf_op jit(solution)/shard_map/ppermute | solution.py:53
  208.1 2.3 collective-permute-start.52
  210.4 1.1 collective-permute-start.47
  212.4 1.1 copy-done.4
  213.5 1.1 copy-done.5
  214.7 2.0 relay.2
  218.5 9.8 %input.3 = (bf16[192,8192]{1,0:T(8,128)(2,1)}, bf16[192,8192]{1,0:T(8,128)(2,1)}) custom-call(bf16[384,512]{1,0:T(8,128)(2,1)} %get-tuple-element.75.refs_6_.refs_0_, bf16[8192,256]{1,0:T(8,128)(2,1)} %refs_1_.1, bf16[8192,256]{1,0:T(8,128)(2,1)} %refs_2_.3), custom_call_target="tpu_custom_call" | custom-call | tf_op jit(solution)/shard_map/input/pallas_call | solution.py:143
  228.3 1.3 collective-permute-start.48
  229.5 3.9 %add_convert_fusion = bf16[192,8192]{1,0:T(8,128)(2,1)S(1)} fusion(bf16[192,8192]{1,0:T(8,128)(2,1)} %collective-permute-done.35, bf16[192,8192]{1,0:T(8,128)(2,1)} %get-tuple-element.78), kind=kLoop, calls=%fused_computation | loop fusion | flops 6291456 | bytes 9437184 | tf_op jit(solution)/shard_map/convert_element_type | solution.py:363
  233.6 1.5 fusion.5
  235.1 1.1 copy-done.19
  236.3 3.2 collective-permute-start.41
  239.5 6.8 %collective-permute-done.48.b = bf16[3,256,512]{2,1,0:T(8,128)(2,1)S(1)} collective-permute-done((bf16[3,256,512]{2,1,0:T(8,128)(2,1)}, bf16[3,256,512]{2,1,0:T(8,128)(2,1)S(1)}, u32[]{:S(2)}, u32[]{:S(2)}) %collective-permute-start.48) | collective-permute-done | bytes 786464 | tf_op jit(solution)/shard_map/ppermute | solution.py:57
  246.3 2.6 collective-permute-start.42
  249.2 1.8 relay.3
  253.4 1.2 collective-permute-start.58
  254.6 3.6 %fusion.1 = (bf16[3,256,512]{2,1,0:T(8,128)(2,1)}, bf16[3,256,512]{2,1,0:T(8,128)(2,1)}) fusion(bf16[3,256,512]{2,1,0:T(8,128)(2,1)} %collective-permute-done.52, f32[256]{0:T(256)S(1)} %slice_reduce_fusion, bf16[6,3,256,512]{3,2,1,0:T(8,128)(2,1)} %get-tuple-element.80.pieces, f32[256]{0:T(256)S(1)} %get-tuple-element.106, f32[256]{0:T(256)S(1)} %slice_reduce_fusion.1, ...), kind=kLoop, calls=%fused_computation.5 | loop fusion | flops 4718592 | bytes 4721664 | tf_op jit(solution)/shard_map/convert_element_type | solution.py:363
  259.1 1.6 collective-permute-start.57
  260.8 3.5 join.1
  265.2 1.6 add_convert_fusion.4
  266.8 2.5 collective-permute-start.43
  269.3 4.1 %add_convert_fusion.1 = bf16[192,8192]{1,0:T(8,128)(2,1)S(1)} fusion(bf16[192,8192]{1,0:T(8,128)(2,1)} %collective-permute-done.34, bf16[192,8192]{1,0:T(8,128)(2,1)} %get-tuple-element.76), kind=kLoop, calls=%fused_computation.1 | loop fusion | flops 6291456 | bytes 9437184 | tf_op jit(solution)/shard_map/convert_element_type | solution.py:363
  273.3 25.5 %collective-permute-done.39 = bf16[48,8192]{1,0:T(8,128)(2,1)S(1)} collective-permute-done((bf16[48,8192]{1,0:T(8,128)(2,1)}, bf16[48,8192]{1,0:T(8,128)(2,1)S(1)}, u32[]{:S(2)}, u32[]{:S(2)}) %collective-permute-start.39) | collective-permute-done | bytes 786464 | tf_op jit(solution)/shard_map/ppermute | solution.py:41
  299.3 1.8 collective-permute-start.46
  301.1 2.5 collective-permute-start.50
  305.2 1.2 collective-permute-done.56
  307.3 16.0 %collective-permute-done.46.l0 = bf16[3,256,512]{2,1,0:T(8,128)(2,1)S(1)} collective-permute-done((bf16[3,256,512]{2,1,0:T(8,128)(2,1)S(1)}, bf16[3,256,512]{2,1,0:T(8,128)(2,1)S(1)}, u32[]{:S(2)}, u32[]{:S(2)}) %collective-permute-start.46) | collective-permute-done | bytes 786464 | tf_op jit(solution)/shard_map/ppermute | solution.py:53
  324.1 12.5 %collective-permute-done.50.l1 = bf16[3,256,512]{2,1,0:T(8,128)(2,1)S(1)} collective-permute-done((bf16[3,256,512]{2,1,0:T(8,128)(2,1)S(1)}, bf16[3,256,512]{2,1,0:T(8,128)(2,1)S(1)}, u32[]{:S(2)}, u32[]{:S(2)}) %collective-permute-start.50) | collective-permute-done | bytes 786464 | tf_op jit(solution)/shard_map/ppermute | solution.py:53
  336.7 1.5 collective-permute-start.38
  339.8 2.3 last.1
  342.1 10.7 %collective-permute-done.38 = bf16[48,8192]{1,0:T(8,128)(2,1)S(1)} collective-permute-done((bf16[48,8192]{1,0:T(8,128)(2,1)S(1)}, bf16[48,8192]{1,0:T(8,128)(2,1)S(1)}, u32[]{:S(2)}, u32[]{:S(2)}) %collective-permute-start.38) | collective-permute-done | bytes 786464 | tf_op jit(solution)/shard_map/ppermute | solution.py:41
  352.8 2.5 collective-permute-done.44
  355.3 1.3 fusion.4
  (183 shorter events, 22.3 us)
Async XLA Ops:
  0.6 20.7 %collective-permute-start = (bf16[48,8192]{1,0:T(8,128)(2,1)}, bf16[48,8192]{1,0:T(8,128)(2,1)S(1)}, u32[]{:S(2)}, u32[]{:S(2)}) collective-permute-start(bf16[48,8192]{1,0:T(8,128)(2,1)} %bitcast.46), channel_id=1, source_target_pairs={{0,2},{1,3},{2,4},{3,5},{4,6},{5,7},{6,0},{7,1},{8,10},{9,11},{10,... | collective-permute-start | bytes 2359304 | tf_op jit(solution)/shard_map/ppermute | solution.py:41
  2.3 22.1 %collective-permute-start.2 = (bf16[48,8192]{1,0:T(8,128)(2,1)}, bf16[48,8192]{1,0:T(8,128)(2,1)S(1)}, u32[]{:S(2)}, u32[]{:S(2)}) collective-permute-start(bf16[48,8192]{1,0:T(8,128)(2,1)} %bitcast.47), channel_id=1, source_target_pairs={{0,8},{1,9},{2,10},{3,11},{4,12},{5,13},{6,14},{7,15},{8,0},{9,1},... | collective-permute-start | bytes 2359304 | tf_op jit(solution)/shard_map/ppermute | solution.py:45
  5.5 34.4 %collective-permute-start.9 = (bf16[48,8192]{1,0:T(8,128)(2,1)}, bf16[48,8192]{1,0:T(8,128)(2,1)S(1)}, u32[]{:S(2)}, u32[]{:S(2)}) collective-permute-start(bf16[48,8192]{1,0:T(8,128)(2,1)} %bitcast.51), channel_id=1, source_target_pairs={{0,8},{1,9},{2,10},{3,11},{4,12},{5,13},{6,14},{7,15},{8,0},{9,1},... | collective-permute-start | bytes 2359304 | tf_op jit(solution)/shard_map/ppermute | solution.py:45
  5.8 34.1 %collective-permute-start.8 = (bf16[48,8192]{1,0:T(8,128)(2,1)}, bf16[48,8192]{1,0:T(8,128)(2,1)S(1)}, u32[]{:S(2)}, u32[]{:S(2)}) collective-permute-start(bf16[48,8192]{1,0:T(8,128)(2,1)} %bitcast.52), channel_id=1, source_target_pairs={{0,6},{1,7},{2,0},{3,1},{4,2},{5,3},{6,4},{7,5},{8,14},{9,15},{10,... | collective-permute-start | bytes 2359304 | tf_op jit(solution)/shard_map/ppermute | solution.py:41
  7.5 35.7 %collective-permute-start.1 = (bf16[48,8192]{1,0:T(8,128)(2,1)}, bf16[48,8192]{1,0:T(8,128)(2,1)S(1)}, u32[]{:S(2)}, u32[]{:S(2)}) collective-permute-start(bf16[48,8192]{1,0:T(8,128)(2,1)} %bitcast.48), channel_id=1, source_target_pairs={{0,6},{1,7},{2,0},{3,1},{4,2},{5,3},{6,4},{7,5},{8,14},{9,15},{10,... | collective-permute-start | bytes 2359304 | tf_op jit(solution)/shard_map/ppermute | solution.py:41
  21.3 23.6 %collective-permute-start.3 = (bf16[48,8192]{1,0:T(8,128)(2,1)}, bf16[48,8192]{1,0:T(8,128)(2,1)S(1)}, u32[]{:S(2)}, u32[]{:S(2)}) collective-permute-start(bf16[48,8192]{1,0:T(8,128)(2,1)} %bitcast.49), channel_id=1, source_target_pairs={{0,1},{1,0},{2,3},{3,2},{4,5},{5,4},{6,7},{7,6},{8,9},{9,8},{10,11... | collective-permute-start | bytes 2359304 | tf_op jit(solution)/shard_map/ppermute | solution.py:49
  24.4 58.6 %copy-start.21 = (bf16[48,8192]{1,0:T(8,128)(2,1)}, bf16[48,8192]{1,0:T(8,128)(2,1)S(1)}, u32[]{:S(2)}) copy-start(bf16[48,8192]{1,0:T(8,128)(2,1)S(1)} %collective-permute-done.2.refs_3_) | copy-start | bytes 2359300
  24.4 20.8 %collective-permute-start.7 = (bf16[48,8192]{1,0:T(8,128)(2,1)}, bf16[48,8192]{1,0:T(8,128)(2,1)S(1)}, u32[]{:S(2)}, u32[]{:S(2)}) collective-permute-start(bf16[48,8192]{1,0:T(8,128)(2,1)} %bitcast.53), channel_id=1, source_target_pairs={{0,2},{1,3},{2,4},{3,5},{4,6},{5,7},{6,0},{7,1},{8,10},{9,11},{10,... | collective-permute-start | bytes 2359304 | tf_op jit(solution)/shard_map/ppermute | solution.py:41
  39.9 6.8 %collective-permute-start.10 = (bf16[48,8192]{1,0:T(8,128)(2,1)}, bf16[48,8192]{1,0:T(8,128)(2,1)S(1)}, u32[]{:S(2)}, u32[]{:S(2)}) collective-permute-start(bf16[48,8192]{1,0:T(8,128)(2,1)} %bitcast.54), channel_id=1, source_target_pairs={{0,1},{1,0},{2,3},{3,2},{4,5},{5,4},{6,7},{7,6},{8,9},{9,8},{10,11... | collective-permute-start | bytes 2359304 | tf_op jit(solution)/shard_map/ppermute | solution.py:49
  39.9 48.2 %copy-start.23 = (bf16[48,8192]{1,0:T(8,128)(2,1)}, bf16[48,8192]{1,0:T(8,128)(2,1)S(1)}, u32[]{:S(2)}) copy-start(bf16[48,8192]{1,0:T(8,128)(2,1)S(1)} %collective-permute-done.8.refs_10_) | copy-start | bytes 2359300
  39.9 22.0 %collective-permute-start.14 = (bf16[48,8192]{1,0:T(8,128)(2,1)S(1)}, bf16[48,8192]{1,0:T(8,128)(2,1)S(1)}, u32[]{:S(2)}, u32[]{:S(2)}) collective-permute-start(bf16[48,8192]{1,0:T(8,128)(2,1)S(1)} %collective-permute-done.refs_1_), channel_id=1, source_target_pairs={{0,8},{1,9},{2,10},{3,11},{4,12},{5,13},{6,14},{7,15},{8,0},{9,1},... | collective-permute-start | bytes 2359304 | tf_op jit(solution)/shard_map/ppermute | solution.py:45
  43.2 47.1 %copy-start.24 = (bf16[48,8192]{1,0:T(8,128)(2,1)}, bf16[48,8192]{1,0:T(8,128)(2,1)S(1)}, u32[]{:S(2)}) copy-start(bf16[48,8192]{1,0:T(8,128)(2,1)S(1)} %collective-permute-done.1.refs_2_) | copy-start | bytes 2359300
  43.2 20.4 %collective-permute-start.15 = (bf16[48,8192]{1,0:T(8,128)(2,1)S(1)}, bf16[48,8192]{1,0:T(8,128)(2,1)S(1)}, u32[]{:S(2)}, u32[]{:S(2)}) collective-permute-start(bf16[48,8192]{1,0:T(8,128)(2,1)S(1)} %collective-permute-done.2.refs_3_), channel_id=1, source_target_pairs={{0,6},{1,7},{2,0},{3,1},{4,2},{5,3},{6,4},{7,5},{8,14},{9,15},{10,... | collective-permute-start | bytes 2359304 | tf_op jit(solution)/shard_map/ppermute | solution.py:41
  44.9 21.6 %collective-permute-start.16 = (bf16[48,8192]{1,0:T(8,128)(2,1)S(1)}, bf16[48,8192]{1,0:T(8,128)(2,1)S(1)}, u32[]{:S(2)}, u32[]{:S(2)}) collective-permute-start(bf16[48,8192]{1,0:T(8,128)(2,1)S(1)} %collective-permute-done.refs_1_), channel_id=1, source_target_pairs={{0,2},{1,3},{2,4},{3,5},{4,6},{5,7},{6,0},{7,1},{8,10},{9,11},{10,... | collective-permute-start | bytes 2359304 | tf_op jit(solution)/shard_map/ppermute | solution.py:41
  45.2 37.2 %collective-permute-start.20 = (bf16[48,8192]{1,0:T(8,128)(2,1)S(1)}, bf16[48,8192]{1,0:T(8,128)(2,1)}, u32[]{:S(2)}, u32[]{:S(2)}) collective-permute-start(bf16[48,8192]{1,0:T(8,128)(2,1)S(1)} %collective-permute-done.9.refs_11_), channel_id=1, source_target_pairs={{0,2},{1,3},{2,4},{3,5},{4,6},{5,7},{6,0},{7,1},{8,10},{9,11},{10,... | collective-permute-start | bytes 2359304 | tf_op jit(solution)/shard_map/ppermute | solution.py:41
  46.7 35.7 %collective-permute-start.21 = (bf16[48,8192]{1,0:T(8,128)(2,1)S(1)}, bf16[48,8192]{1,0:T(8,128)(2,1)}, u32[]{:S(2)}, u32[]{:S(2)}) collective-permute-start(bf16[48,8192]{1,0:T(8,128)(2,1)S(1)} %collective-permute-done.8.refs_10_), channel_id=1, source_target_pairs={{0,8},{1,9},{2,10},{3,11},{4,12},{5,13},{6,14},{7,15},{8,0},{9,1},... | collective-permute-start | bytes 2359304 | tf_op jit(solution)/shard_map/ppermute | solution.py:45
  61.9 21.0 %collective-permute-start.22 = (bf16[48,8192]{1,0:T(8,128)(2,1)S(1)}, bf16[48,8192]{1,0:T(8,128)(2,1)}, u32[]{:S(2)}, u32[]{:S(2)}) collective-permute-start(bf16[48,8192]{1,0:T(8,128)(2,1)S(1)} %collective-permute-done.8.refs_10_), channel_id=1, source_target_pairs={{0,6},{1,7},{2,0},{3,1},{4,2},{5,3},{6,4},{7,5},{8,14},{9,15},{10,... | collective-permute-start | bytes 2359304 | tf_op jit(solution)/shard_map/ppermute | solution.py:41
  63.6 19.4 %collective-permute-start.4 = (bf16[48,8192]{1,0:T(8,128)(2,1)S(1)}, bf16[48,8192]{1,0:T(8,128)(2,1)S(1)}, u32[]{:S(2)}, u32[]{:S(2)}) collective-permute-start(bf16[48,8192]{1,0:T(8,128)(2,1)S(1)} %collective-permute-done.refs_1_), channel_id=1, source_target_pairs={{0,1},{1,0},{2,3},{3,2},{4,5},{5,4},{6,7},{7,6},{8,9},{9,8},{10,11... | collective-permute-start | bytes 2359304 | tf_op jit(solution)/shard_map/ppermute | solution.py:49
  66.5 17.0 %collective-permute-start.5 = (bf16[48,8192]{1,0:T(8,128)(2,1)S(1)}, bf16[48,8192]{1,0:T(8,128)(2,1)S(1)}, u32[]{:S(2)}, u32[]{:S(2)}) collective-permute-start(bf16[48,8192]{1,0:T(8,128)(2,1)S(1)} %collective-permute-done.1.refs_2_), channel_id=1, source_target_pairs={{0,1},{1,0},{2,3},{3,2},{4,5},{5,4},{6,7},{7,6},{8,9},{9,8},{10,11... | collective-permute-start | bytes 2359304 | tf_op jit(solution)/shard_map/ppermute | solution.py:49
  82.4 2.3 collective-permute-start.6
  82.4 3.4 collective-permute-start.11
  82.9 4.0 %collective-permute-start.12 = (bf16[48,8192]{1,0:T(8,128)(2,1)S(1)}, bf16[48,8192]{1,0:T(8,128)(2,1)S(1)}, u32[]{:S(2)}, u32[]{:S(2)}) collective-permute-start(bf16[48,8192]{1,0:T(8,128)(2,1)S(1)} %collective-permute-done.8.refs_10_), channel_id=1, source_target_pairs={{0,1},{1,0},{2,3},{3,2},{4,5},{5,4},{6,7},{7,6},{8,9},{9,8},{10,11... | collective-permute-start | bytes 2359304 | tf_op jit(solution)/shard_map/ppermute | solution.py:49
  83.0 5.0 %collective-permute-start.13 = (bf16[48,8192]{1,0:T(8,128)(2,1)S(1)}, bf16[48,8192]{1,0:T(8,128)(2,1)S(1)}, u32[]{:S(2)}, u32[]{:S(2)}) collective-permute-start(bf16[48,8192]{1,0:T(8,128)(2,1)S(1)} %collective-permute-done.9.refs_11_), channel_id=1, source_target_pairs={{0,1},{1,0},{2,3},{3,2},{4,5},{5,4},{6,7},{7,6},{8,9},{9,8},{10,11... | collective-permute-start | bytes 2359304 | tf_op jit(solution)/shard_map/ppermute | solution.py:49
  83.5 7.7 %collective-permute-start.17 = (bf16[48,8192]{1,0:T(8,128)(2,1)S(1)}, bf16[48,8192]{1,0:T(8,128)(2,1)S(1)}, u32[]{:S(2)}, u32[]{:S(2)}) collective-permute-start(bf16[48,8192]{1,0:T(8,128)(2,1)S(1)} %collective-permute-done.14.refs_0_), channel_id=1, source_target_pairs={{0,1},{1,0},{2,3},{3,2},{4,5},{5,4},{6,7},{7,6},{8,9},{9,8},{10,11... | collective-permute-start | bytes 2359304 | tf_op jit(solution)/shard_map/ppermute | solution.py:49
  84.7 6.6 %collective-permute-start.18 = (bf16[48,8192]{1,0:T(8,128)(2,1)S(1)}, bf16[48,8192]{1,0:T(8,128)(2,1)}, u32[]{:S(2)}, u32[]{:S(2)}) collective-permute-start(bf16[48,8192]{1,0:T(8,128)(2,1)S(1)} %collective-permute-done.15.refs_1_), channel_id=1, source_target_pairs={{0,1},{1,0},{2,3},{3,2},{4,5},{5,4},{6,7},{7,6},{8,9},{9,8},{10,11... | collective-permute-start | bytes 2359304 | tf_op jit(solution)/shard_map/ppermute | solution.py:49
  85.8 6.0 %collective-permute-start.19 = (bf16[48,8192]{1,0:T(8,128)(2,1)S(1)}, bf16[48,8192]{1,0:T(8,128)(2,1)}, u32[]{:S(2)}, u32[]{:S(2)}) collective-permute-start(bf16[48,8192]{1,0:T(8,128)(2,1)S(1)} %collective-permute-done.16.refs_2_), channel_id=1, source_target_pairs={{0,1},{1,0},{2,3},{3,2},{4,5},{5,4},{6,7},{7,6},{8,9},{9,8},{10,11... | collective-permute-start | bytes 2359304 | tf_op jit(solution)/shard_map/ppermute | solution.py:49
  86.9 20.9 %collective-permute-start.26 = (bf16[48,8192]{1,0:T(8,128)(2,1)S(1)}, bf16[48,8192]{1,0:T(8,128)(2,1)}, u32[]{:S(2)}, u32[]{:S(2)}) collective-permute-start(bf16[48,8192]{1,0:T(8,128)(2,1)S(1)} %collective-permute-done.14.refs_0_), channel_id=1, source_target_pairs={{0,2},{1,3},{2,4},{3,5},{4,6},{5,7},{6,0},{7,1},{8,10},{9,11},{10,... | collective-permute-start | bytes 2359304 | tf_op jit(solution)/shard_map/ppermute | solution.py:41
  88.1 19.9 %collective-permute-start.28 = (bf16[48,8192]{1,0:T(8,128)(2,1)}, bf16[48,8192]{1,0:T(8,128)(2,1)}, u32[]{:S(2)}, u32[]{:S(2)}) collective-permute-start(bf16[48,8192]{1,0:T(8,128)(2,1)} %collective-permute-done.21.refs_7_), channel_id=1, source_target_pairs={{0,6},{1,7},{2,0},{3,1},{4,2},{5,3},{6,4},{7,5},{8,14},{9,15},{10,... | collective-permute-start | bytes 2359304 | tf_op jit(solution)/shard_map/ppermute | solution.py:41
  91.2 39.0 %collective-permute-start.24 = (bf16[48,8192]{1,0:T(8,128)(2,1)}, bf16[48,8192]{1,0:T(8,128)(2,1)}, u32[]{:S(2)}, u32[]{:S(2)}) collective-permute-start(bf16[48,8192]{1,0:T(8,128)(2,1)} %collective-permute-done.21.refs_7_), channel_id=1, source_target_pairs={{0,1},{1,0},{2,3},{3,2},{4,5},{5,4},{6,7},{7,6},{8,9},{9,8},{10,11... | collective-permute-start | bytes 2359304 | tf_op jit(solution)/shard_map/ppermute | solution.py:49
  91.3 38.9 %collective-permute-start.23 = (bf16[48,8192]{1,0:T(8,128)(2,1)}, bf16[48,8192]{1,0:T(8,128)(2,1)}, u32[]{:S(2)}, u32[]{:S(2)}) collective-permute-start(bf16[48,8192]{1,0:T(8,128)(2,1)} %collective-permute-done.20.refs_6_), channel_id=1, source_target_pairs={{0,1},{1,0},{2,3},{3,2},{4,5},{5,4},{6,7},{7,6},{8,9},{9,8},{10,11... | collective-permute-start | bytes 2359304 | tf_op jit(solution)/shard_map/ppermute | solution.py:49
  91.8 38.4 %collective-permute-start.25 = (bf16[48,8192]{1,0:T(8,128)(2,1)}, bf16[48,8192]{1,0:T(8,128)(2,1)}, u32[]{:S(2)}, u32[]{:S(2)}) collective-permute-start(bf16[48,8192]{1,0:T(8,128)(2,1)} %collective-permute-done.22.refs_8_), channel_id=1, source_target_pairs={{0,1},{1,0},{2,3},{3,2},{4,5},{5,4},{6,7},{7,6},{8,9},{9,8},{10,11... | collective-permute-start | bytes 2359304 | tf_op jit(solution)/shard_map/ppermute | solution.py:49
  107.8 37.7 %collective-permute-start.27 = (bf16[48,8192]{1,0:T(8,128)(2,1)}, bf16[48,8192]{1,0:T(8,128)(2,1)}, u32[]{:S(2)}, u32[]{:S(2)}) collective-permute-start(bf16[48,8192]{1,0:T(8,128)(2,1)} %collective-permute-done.26.refs_0_), channel_id=1, source_target_pairs={{0,1},{1,0},{2,3},{3,2},{4,5},{5,4},{6,7},{7,6},{8,9},{9,8},{10,11... | collective-permute-start | bytes 2359304 | tf_op jit(solution)/shard_map/ppermute | solution.py:49
  108.0 37.6 %collective-permute-start.29 = (bf16[48,8192]{1,0:T(8,128)(2,1)}, bf16[48,8192]{1,0:T(8,128)(2,1)}, u32[]{:S(2)}, u32[]{:S(2)}) collective-permute-start(bf16[48,8192]{1,0:T(8,128)(2,1)} %collective-permute-done.28.refs_2_), channel_id=1, source_target_pairs={{0,1},{1,0},{2,3},{3,2},{4,5},{5,4},{6,7},{7,6},{8,9},{9,8},{10,11... | collective-permute-start | bytes 2359304 | tf_op jit(solution)/shard_map/ppermute | solution.py:49
  175.6 52.6 %collective-permute-start.35 = (bf16[192,8192]{1,0:T(8,128)(2,1)}, bf16[192,8192]{1,0:T(8,128)(2,1)}, u32[]{:S(2)}, u32[]{:S(2)}) collective-permute-start(bf16[192,8192]{1,0:T(8,128)(2,1)} %get-tuple-element.79), channel_id=1, source_target_pairs={{0,1},{1,0},{2,3},{3,2},{4,5},{5,4},{6,7},{7,6},{8,9},{9,8},{10,11... | collective-permute-start | bytes 9437192 | tf_op jit(solution)/shard_map/ppermute | solution.py:49
  175.7 34.7 %collective-permute-start.30 = (bf16[3,256,512]{2,1,0:T(8,128)(2,1)}, bf16[3,256,512]{2,1,0:T(8,128)(2,1)}, u32[]{:S(2)}, u32[]{:S(2)}) collective-permute-start(bf16[3,256,512]{2,1,0:T(8,128)(2,1)} %get-tuple-element.71), channel_id=1, source_target_pairs={{0,32},{16,48},{32,64},{48,80},{64,96},{80,112},{96,0},{112,16},{1... | collective-permute-start | bytes 2359304 | tf_op jit(solution)/shard_map/ppermute | solution.py:53
  177.6 32.8 %collective-permute-start.31 = (bf16[3,256,512]{2,1,0:T(8,128)(2,1)}, bf16[3,256,512]{2,1,0:T(8,128)(2,1)}, u32[]{:S(2)}, u32[]{:S(2)}) collective-permute-start(bf16[3,256,512]{2,1,0:T(8,128)(2,1)} %get-tuple-element.72), channel_id=1, source_target_pairs={{0,96},{16,112},{32,0},{48,16},{64,32},{80,48},{96,64},{112,80},{1... | collective-permute-start | bytes 2359304 | tf_op jit(solution)/shard_map/ppermute | solution.py:53
  200.5 7.0 %collective-permute-start.32 = (f32[256,128]{1,0:T(8,128)}, f32[256,128]{1,0:T(8,128)S(1)}, u32[]{:S(2)}, u32[]{:S(2)}) collective-permute-start(f32[256,128]{1,0:T(8,128)} %get-tuple-element.73.ratio), channel_id=1, source_target_pairs={{0,32},{16,48},{32,64},{48,80},{64,96},{80,112},{96,0},{112,16},{1... | collective-permute-start | bytes 393224 | tf_op jit(solution)/shard_map/ppermute | solution.py:53
  200.5 7.6 %collective-permute-start.33 = (f32[256,128]{1,0:T(8,128)}, f32[256,128]{1,0:T(8,128)S(1)}, u32[]{:S(2)}, u32[]{:S(2)}) collective-permute-start(f32[256,128]{1,0:T(8,128)} %get-tuple-element.73.ratio), channel_id=1, source_target_pairs={{0,96},{16,112},{32,0},{48,16},{64,32},{80,48},{96,64},{112,80},{1... | collective-permute-start | bytes 393224 | tf_op jit(solution)/shard_map/ppermute | solution.py:53
  207.4 26.0 %collective-permute-start.49 = (f32[256,128]{1,0:T(8,128)}, f32[256,128]{1,0:T(8,128)S(1)}, u32[]{:S(2)}, u32[]{:S(2)}) collective-permute-start(f32[256,128]{1,0:T(8,128)} %get-tuple-element.73.ratio), channel_id=1, source_target_pairs={{0,16},{16,0},{32,48},{48,32},{64,80},{80,64},{96,112},{112,96},{1... | collective-permute-start | bytes 393224 | tf_op jit(solution)/shard_map/ppermute | solution.py:57
  208.1 28.1 %collective-permute-start.52 = (bf16[3,256,512]{2,1,0:T(8,128)(2,1)}, bf16[3,256,512]{2,1,0:T(8,128)(2,1)}, u32[]{:S(2)}, u32[]{:S(2)}) collective-permute-start(bf16[3,256,512]{2,1,0:T(8,128)(2,1)} %get-tuple-element.93), channel_id=1, source_target_pairs={{0,96},{16,112},{32,0},{48,16},{64,32},{80,48},{96,64},{112,80},{1... | collective-permute-start | bytes 2359304 | tf_op jit(solution)/shard_map/ppermute | solution.py:53
  210.4 43.0 %collective-permute-start.45 = (bf16[3,256,512]{2,1,0:T(8,128)(2,1)}, bf16[3,256,512]{2,1,0:T(8,128)(2,1)}, u32[]{:S(2)}, u32[]{:S(2)}) collective-permute-start(bf16[3,256,512]{2,1,0:T(8,128)(2,1)} %get-tuple-element.86), channel_id=1, source_target_pairs={{0,32},{16,48},{32,64},{48,80},{64,96},{80,112},{96,0},{112,16},{1... | collective-permute-start | bytes 2359304 | tf_op jit(solution)/shard_map/ppermute | solution.py:53
  210.4 25.8 %collective-permute-start.47 = (bf16[3,256,512]{2,1,0:T(8,128)(2,1)}, bf16[3,256,512]{2,1,0:T(8,128)(2,1)}, u32[]{:S(2)}, u32[]{:S(2)}) collective-permute-start(bf16[3,256,512]{2,1,0:T(8,128)(2,1)} %get-tuple-element.89), channel_id=1, source_target_pairs={{0,16},{16,0},{32,48},{48,32},{64,80},{80,64},{96,112},{112,96},{1... | collective-permute-start | bytes 2359304 | tf_op jit(solution)/shard_map/ppermute | solution.py:57
  228.3 18.1 %collective-permute-start.48 = (bf16[3,256,512]{2,1,0:T(8,128)(2,1)}, bf16[3,256,512]{2,1,0:T(8,128)(2,1)S(1)}, u32[]{:S(2)}, u32[]{:S(2)}) collective-permute-start(bf16[3,256,512]{2,1,0:T(8,128)(2,1)} %get-tuple-element.90), channel_id=1, source_target_pairs={{0,16},{16,0},{32,48},{48,32},{64,80},{80,64},{96,112},{112,96},{1... | collective-permute-start | bytes 2359304 | tf_op jit(solution)/shard_map/ppermute | solution.py:57
  233.5 33.2 %collective-permute-start.34 = (bf16[192,8192]{1,0:T(8,128)(2,1)}, bf16[192,8192]{1,0:T(8,128)(2,1)}, u32[]{:S(2)}, u32[]{:S(2)}) collective-permute-start(bf16[192,8192]{1,0:T(8,128)(2,1)} %get-tuple-element.77), channel_id=1, source_target_pairs={{0,1},{1,0},{2,3},{3,2},{4,5},{5,4},{6,7},{7,6},{8,9},{9,8},{10,11... | collective-permute-start | bytes 9437192 | tf_op jit(solution)/shard_map/ppermute | solution.py:49
  236.2 22.0 %collective-permute-start.40 = (bf16[3,256,512]{2,1,0:T(8,128)(2,1)S(1)}, bf16[3,256,512]{2,1,0:T(8,128)(2,1)S(1)}, u32[]{:S(2)}, u32[]{:S(2)}) collective-permute-start(bf16[3,256,512]{2,1,0:T(8,128)(2,1)S(1)} %copy-done.18), channel_id=1, source_target_pairs={{0,32},{16,48},{32,64},{48,80},{64,96},{80,112},{96,0},{112,16},{1... | collective-permute-start | bytes 2359304 | tf_op jit(solution)/shard_map/ppermute | solution.py:53
  236.3 24.5 %collective-permute-start.41 = (bf16[3,256,512]{2,1,0:T(8,128)(2,1)S(1)}, bf16[3,256,512]{2,1,0:T(8,128)(2,1)}, u32[]{:S(2)}, u32[]{:S(2)}) collective-permute-start(bf16[3,256,512]{2,1,0:T(8,128)(2,1)S(1)} %copy-done.16), channel_id=1, source_target_pairs={{0,96},{16,112},{32,0},{48,16},{64,32},{80,48},{96,64},{112,80},{1... | collective-permute-start | bytes 2359304 | tf_op jit(solution)/shard_map/ppermute | solution.py:53
  246.3 18.0 %collective-permute-start.42 = (bf16[48,8192]{1,0:T(8,128)(2,1)}, bf16[48,8192]{1,0:T(8,128)(2,1)}, u32[]{:S(2)}, u32[]{:S(2)}) collective-permute-start(bf16[48,8192]{1,0:T(8,128)(2,1)} %get-tuple-element.103), channel_id=1, source_target_pairs={{0,6},{1,7},{2,0},{3,1},{4,2},{5,3},{6,4},{7,5},{8,14},{9,15},{10,... | collective-permute-start | bytes 2359304 | tf_op jit(solution)/shard_map/ppermute | solution.py:41
  253.4 47.7 %collective-permute-start.58 = (f32[256,1]{1,0:T(8,128)S(1)}, f32[256,1]{1,0:T(8,128)S(1)}, u32[]{:S(2)}, u32[]{:S(2)}) collective-permute-start(f32[256,1]{1,0:T(8,128)S(1)} %get-tuple-element.105), channel_id=1, source_target_pairs={{0,64},{16,80},{32,96},{48,112},{64,0},{80,16},{96,32},{112,48},{1... | collective-permute-start | bytes 3080 | tf_op jit(solution)/shard_map/ppermute | solution.py:53
  259.1 44.5 %collective-permute-start.57 = (f32[256,1]{1,0:T(8,128)S(1)}, f32[256,1]{1,0:T(8,128)}, u32[]{:S(2)}, u32[]{:S(2)}) collective-permute-start(f32[256,1]{1,0:T(8,128)S(1)} %get-tuple-element.105), channel_id=1, source_target_pairs={{0,96},{16,112},{32,0},{48,16},{64,32},{80,48},{96,64},{112,80},{1... | collective-permute-start | bytes 3080 | tf_op jit(solution)/shard_map/ppermute | solution.py:53
  264.3 40.1 %collective-permute-start.36 = (bf16[48,8192]{1,0:T(8,128)(2,1)}, bf16[48,8192]{1,0:T(8,128)(2,1)S(1)}, u32[]{:S(2)}, u32[]{:S(2)}) collective-permute-start(bf16[48,8192]{1,0:T(8,128)(2,1)} %get-tuple-element.102), channel_id=1, source_target_pairs={{0,2},{1,3},{2,4},{3,5},{4,6},{5,7},{6,0},{7,1},{8,10},{9,11},{10,... | collective-permute-start | bytes 2359304 | tf_op jit(solution)/shard_map/ppermute | solution.py:41
  264.3 34.5 %collective-permute-start.39 = (bf16[48,8192]{1,0:T(8,128)(2,1)}, bf16[48,8192]{1,0:T(8,128)(2,1)S(1)}, u32[]{:S(2)}, u32[]{:S(2)}) collective-permute-start(bf16[48,8192]{1,0:T(8,128)(2,1)} %get-tuple-element.104), channel_id=1, source_target_pairs={{0,2},{1,3},{2,4},{3,5},{4,6},{5,7},{6,0},{7,1},{8,10},{9,11},{10,... | collective-permute-start | bytes 2359304 | tf_op jit(solution)/shard_map/ppermute | solution.py:41
  266.8 32.5 %collective-permute-start.43 = (bf16[48,8192]{1,0:T(8,128)(2,1)S(1)}, bf16[48,8192]{1,0:T(8,128)(2,1)S(1)}, u32[]{:S(2)}, u32[]{:S(2)}) collective-permute-start(bf16[48,8192]{1,0:T(8,128)(2,1)S(1)} %add_convert_fusion.4), channel_id=1, source_target_pairs={{0,6},{1,7},{2,0},{3,1},{4,2},{5,3},{6,4},{7,5},{8,14},{9,15},{10,... | collective-permute-start | bytes 2359304 | tf_op jit(solution)/shard_map/ppermute | solution.py:41
  269.2 70.5 %slice-start = ((s8[4718592]{0:T(1024)(128)(4,1)}), s8[4194304]{0:T(1024)(128)(4,1)S(1)}, s32[]{:S(2)}) async-start(s8[4718592]{0:T(1024)(128)(4,1)} %bitcast.43), calls=%async_computation | async-start | bytes 8388608
  269.2 70.5 %slice-start.1 = ((s8[4718592]{0:T(1024)(128)(4,1)}), s8[524288]{0:T(1024)(128)(4,1)S(1)}, s32[]{:S(2)}) async-start(s8[4718592]{0:T(1024)(128)(4,1)} %bitcast.43), calls=%async_computation.1 | async-start | bytes 1048576
  298.8 7.6 %collective-permute-start.56 = (f32[256,1]{1,0:T(8,128)S(1)}, f32[256,1]{1,0:T(8,128)S(1)}, u32[]{:S(2)}, u32[]{:S(2)}) collective-permute-start(f32[256,1]{1,0:T(8,128)S(1)} %get-tuple-element.105), channel_id=1, source_target_pairs={{0,32},{16,48},{32,64},{48,80},{64,96},{80,112},{96,0},{112,16},{1... | collective-permute-start | bytes 3080 | tf_op jit(solution)/shard_map/ppermute | solution.py:53
  299.3 24.0 %collective-permute-start.46 = (bf16[3,256,512]{2,1,0:T(8,128)(2,1)S(1)}, bf16[3,256,512]{2,1,0:T(8,128)(2,1)S(1)}, u32[]{:S(2)}, u32[]{:S(2)}) collective-permute-start(bf16[3,256,512]{2,1,0:T(8,128)(2,1)S(1)} %copy-done.39), channel_id=1, source_target_pairs={{0,32},{16,48},{32,64},{48,80},{64,96},{80,112},{96,0},{112,16},{1... | collective-permute-start | bytes 2359304 | tf_op jit(solution)/shard_map/ppermute | solution.py:53
  301.1 35.6 %collective-permute-start.50 = (bf16[3,256,512]{2,1,0:T(8,128)(2,1)S(1)}, bf16[3,256,512]{2,1,0:T(8,128)(2,1)S(1)}, u32[]{:S(2)}, u32[]{:S(2)}) collective-permute-start(bf16[3,256,512]{2,1,0:T(8,128)(2,1)S(1)} %copy-done.14), channel_id=1, source_target_pairs={{0,32},{16,48},{32,64},{48,80},{64,96},{80,112},{96,0},{112,16},{1... | collective-permute-start | bytes 2359304 | tf_op jit(solution)/shard_map/ppermute | solution.py:53
  303.6 34.6 %collective-permute-start.51 = (bf16[3,256,512]{2,1,0:T(8,128)(2,1)S(1)}, bf16[3,256,512]{2,1,0:T(8,128)(2,1)S(1)}, u32[]{:S(2)}, u32[]{:S(2)}) collective-permute-start(bf16[3,256,512]{2,1,0:T(8,128)(2,1)S(1)} %copy-done.12), channel_id=1, source_target_pairs={{0,96},{16,112},{32,0},{48,16},{64,32},{80,48},{96,64},{112,80},{1... | collective-permute-start | bytes 2359304 | tf_op jit(solution)/shard_map/ppermute | solution.py:53
  304.4 33.8 %collective-permute-start.53 = (bf16[3,256,512]{2,1,0:T(8,128)(2,1)S(1)}, bf16[3,256,512]{2,1,0:T(8,128)(2,1)S(1)}, u32[]{:S(2)}, u32[]{:S(2)}) collective-permute-start(bf16[3,256,512]{2,1,0:T(8,128)(2,1)S(1)} %copy-done.38), channel_id=1, source_target_pairs={{0,96},{16,112},{32,0},{48,16},{64,32},{80,48},{96,64},{112,80},{1... | collective-permute-start | bytes 2359304 | tf_op jit(solution)/shard_map/ppermute | solution.py:53
  306.4 33.3 %collective-permute-start.54 = (bf16[3,256,512]{2,1,0:T(8,128)(2,1)S(1)}, bf16[3,256,512]{2,1,0:T(8,128)(2,1)S(1)}, u32[]{:S(2)}, u32[]{:S(2)}) collective-permute-start(bf16[3,256,512]{2,1,0:T(8,128)(2,1)S(1)} %copy-done.42), channel_id=1, source_target_pairs={{0,16},{16,0},{32,48},{48,32},{64,80},{80,64},{96,112},{112,96},{1... | collective-permute-start | bytes 2359304 | tf_op jit(solution)/shard_map/ppermute | solution.py:57
  323.3 16.5 %collective-permute-start.55 = (bf16[3,256,512]{2,1,0:T(8,128)(2,1)S(1)}, bf16[3,256,512]{2,1,0:T(8,128)(2,1)S(1)}, u32[]{:S(2)}, u32[]{:S(2)}) collective-permute-start(bf16[3,256,512]{2,1,0:T(8,128)(2,1)S(1)} %copy-done.41), channel_id=1, source_target_pairs={{0,16},{16,0},{32,48},{48,32},{64,80},{80,64},{96,112},{112,96},{1... | collective-permute-start | bytes 2359304 | tf_op jit(solution)/shard_map/ppermute | solution.py:57
  336.7 16.1 %collective-permute-start.38 = (bf16[48,8192]{1,0:T(8,128)(2,1)S(1)}, bf16[48,8192]{1,0:T(8,128)(2,1)S(1)}, u32[]{:S(2)}, u32[]{:S(2)}) collective-permute-start(bf16[48,8192]{1,0:T(8,128)(2,1)S(1)} %slice.93), channel_id=1, source_target_pairs={{0,6},{1,7},{2,0},{3,1},{4,2},{5,3},{6,4},{7,5},{8,14},{9,15},{10,... | collective-permute-start | bytes 2359304 | tf_op jit(solution)/shard_map/ppermute | solution.py:41
  338.1 17.1 %collective-permute-start.44 = (bf16[48,8192]{1,0:T(8,128)(2,1)S(1)}, bf16[48,8192]{1,0:T(8,128)(2,1)S(1)}, u32[]{:S(2)}, u32[]{:S(2)}) collective-permute-start(bf16[48,8192]{1,0:T(8,128)(2,1)S(1)} %get-tuple-element.101), channel_id=1, source_target_pairs={{0,8},{1,9},{2,10},{3,11},{4,12},{5,13},{6,14},{7,15},{8,0},{9,1},... | collective-permute-start | bytes 2359304 | tf_op jit(solution)/shard_map/ppermute | solution.py:45
  338.1 17.1 %collective-permute-start.37 = (bf16[48,8192]{1,0:T(8,128)(2,1)S(1)}, bf16[48,8192]{1,0:T(8,128)(2,1)S(1)}, u32[]{:S(2)}, u32[]{:S(2)}) collective-permute-start(bf16[48,8192]{1,0:T(8,128)(2,1)S(1)} %get-tuple-element.100), channel_id=1, source_target_pairs={{0,2},{1,3},{2,4},{3,5},{4,6},{5,7},{6,0},{7,1},{8,10},{9,11},{10,... | collective-permute-start | bytes 2359304 | tf_op jit(solution)/shard_map/ppermute | solution.py:41
  (40 other events, 680.8 us)

commit v4 on v3

--- a/solution.py
+++ b/solution.py
@@ -170,7 +170,7 @@
         in_specs=whole,
         out_specs=whole[:2],
         out_shape=[jax.ShapeDtypeStruct(arrays[0].shape, jnp.bfloat16)] * 2,
-        compiler_params=pltpu.CompilerParams(vmem_limit_bytes=VMEM_SMALL),
+        compiler_params=pltpu.CompilerParams(vmem_limit_bytes=VMEM),
         interpret=INTERPRET,
     )(*arrays)
 
@@ -192,7 +192,7 @@
         in_specs=[pl.BlockSpec((2, 3, hid, block), lambda k: (first // 2, 0, 0, 0))] + whole,
         out_specs=whole[:2],
         out_shape=[jax.ShapeDtypeStruct(a.shape, jnp.bfloat16)] * 2,
-        compiler_params=pltpu.CompilerParams(vmem_limit_bytes=VMEM),
+        compiler_params=pltpu.CompilerParams(vmem_limit_bytes=VMEM_SMALL),
         interpret=INTERPRET,
     )(pieces, a, b, ratio)
 
@@ -410,6 +410,9 @@
         outs.append(out)
         ggus.append(ggu)
         hids.append(hidden)
+    near, near_p = input_gradient(ggus[:1], w_gate, w_up)
+    near_p = to_core(near_p)
+
     *first, ggu_t, hid_t, moment = gradients_early(target[:EARLY], toks, outs, ggus, hids)
     a, b = to_z(first[0], 1), to_z(first[1], -1)
     c, d = to_y_next(first[2]), to_y_next(first[3])
@@ -445,8 +448,8 @@
     total = total + to_z(total, 1) + to_z(total, -1) + to_z(total, 2)
     grad_gate, grad_up, grad_down = last_sum(pieces, others, ratio, total)
 
-    near, near_p = input_gradient([after(ggus[0], left)], w_gate, w_up)
-    near = bf(f32(near) + f32(to_core(near_p)))
+    near, near_p = after(near, *third_y), after(near_p, *third_y)
+    near = bf(f32(near) + f32(near_p))
     part = [value[i : i + rows] for value in (near, far) for i in range(0, 4 * rows, rows)]
     far_0, far_1 = to_x(part[6], 1), to_x(part[7], -1)
     up_1 = to_x(part[5], 1)

time: 358 us -> 372 us (1.039)
  starting transfers between devices: 59.4 us -> 69.9 us
  waiting for transfers between devices: 161 us -> 171 us
  local copies, waits for them, and re-layouts: 13.8 us -> 8.87 us
    ppermute x5, waiting for transfers between devices: 6.84 us -> 20.1 us  [to_y_next(): return lax.ppermute(value, 'lang', lang_pairs(0, 1))]
    unnamed x90 -> x64, local copies, waits for them, and re-layouts: 8.85 us -> 3.02 us
    ppermute x5, starting transfers between devices: 8.15 us -> 13.4 us  [to_y_half(): return lax.ppermute(value, 'fsdp', fsdp_pairs(0, 1, 0))]
    ppermute x18, waiting for transfers between devices: 4.18 us -> 0.05 us  [to_core(): return lax.ppermute(value, 'fsdp', fsdp_pairs(0, 0, 1))]
  transfers between devices with their start and end apart: 59 -> 59, of which waited for: 20 -> 22; matrix products, arithmetic and copies ran while one was open for 6% -> 5% of each run, Pallas kernels for 20% -> 20%
where the time goes in v4:
time: 372 us; the launch traced here: 370 us
  waiting for transfers between devices  171 us (46%)
  Pallas kernels  104 us (28%)
  starting transfers between devices  69.9 us (19%)
  other arithmetic  14.9 us (4%)
  local copies, waits for them, and re-layouts  8.87 us (2%)
    ppermute x16, waiting for transfers between devices, to_x(): return lax.ppermute(value, 'fsdp', fsdp_pairs(step, 0, 0))  83 us
    pallas_call x3, Pallas kernels, forward(): pl.pallas_call(functools.partial(forward_kernel, n), name='forward', grid...  43.9 us
    ppermute x5, waiting for transfers between devices, to_y_half(): return lax.ppermute(value, 'fsdp', fsdp_pairs(0, 1, 0))  35.7 us
    ppermute x15, waiting for transfers between devices, to_z(): return lax.ppermute(value, 'lang', lang_pairs(step, 0))  32.1 us
    ppermute x16, starting transfers between devices, to_x(): return lax.ppermute(value, 'fsdp', fsdp_pairs(step, 0, 0))  23.9 us
    ppermute x15, starting transfers between devices, to_z(): return lax.ppermute(value, 'lang', lang_pairs(step, 0))  22.8 us
    ppermute x5, waiting for transfers between devices, to_y_next(): return lax.ppermute(value, 'lang', lang_pairs(0, 1))  20.1 us
    pallas_call x1, Pallas kernels, gradients_late(): pl.pallas_call(functools.partial(late_kernel, len(toks), depth), name='la...  19.9 us
  transfers between devices with their start and end apart: 59, of which 22 were waited for; matrix products, arithmetic and copies ran while one was open for 5% of the time, Pallas kernels for 20%

profile of v4, /device:TPU:0, one launch (start us, length us, event | category | flops | bytes accessed | tf_op | source)
XLA Modules:
  0.0 370.4 jit_solution(13228099502924235997)
XLA Ops:
  0.7 3.4 collective-permute-start.2
  4.1 2.8 collective-permute-start.1
  7.3 15.6 %collective-permute-done.2.refs_3_ = bf16[48,8192]{1,0:T(8,128)(2,1)S(1)} collective-permute-done((bf16[48,8192]{1,0:T(8,128)(2,1)}, bf16[48,8192]{1,0:T(8,128)(2,1)S(1)}, u32[]{:S(2)}, u32[]{:S(2)}) %collective-permute-start.2) | collective-permute-done | bytes 786464 | tf_op jit(solution)/shard_map/ppermute | solution.py:45
  22.9 2.9 collective-permute-start.8
  25.8 1.8 collective-permute-done.refs_1_
  27.6 1.5 collective-permute-start.15
  29.2 10.1 %collective-permute-done.9.refs_11_ = bf16[48,8192]{1,0:T(8,128)(2,1)S(1)} collective-permute-done((bf16[48,8192]{1,0:T(8,128)(2,1)}, bf16[48,8192]{1,0:T(8,128)(2,1)S(1)}, u32[]{:S(2)}, u32[]{:S(2)}) %collective-permute-start.9) | collective-permute-done | bytes 786464 | tf_op jit(solution)/shard_map/ppermute | solution.py:45
  39.3 4.8 %collective-permute-done.8.refs_10_ = bf16[48,8192]{1,0:T(8,128)(2,1)S(1)} collective-permute-done((bf16[48,8192]{1,0:T(8,128)(2,1)}, bf16[48,8192]{1,0:T(8,128)(2,1)S(1)}, u32[]{:S(2)}, u32[]{:S(2)}) %collective-permute-start.8) | collective-permute-done | bytes 786464 | tf_op jit(solution)/shard_map/ppermute | solution.py:41
  46.1 3.2 collective-permute-start.14
  49.3 9.5 %collective-permute-done.15.refs_1_ = bf16[48,8192]{1,0:T(8,128)(2,1)S(1)} collective-permute-done((bf16[48,8192]{1,0:T(8,128)(2,1)S(1)}, bf16[48,8192]{1,0:T(8,128)(2,1)S(1)}, u32[]{:S(2)}, u32[]{:S(2)}) %collective-permute-start.15) | collective-permute-done | bytes 786464 | tf_op jit(solution)/shard_map/ppermute | solution.py:41
  58.9 1.3 collective-permute-start.20
  60.4 1.8 collective-permute-done.16.refs_2_
  62.3 1.4 collective-permute-start.22
  64.2 3.2 collective-permute-start.21
  67.5 13.4 %collective-permute-done.20.refs_6_ = bf16[48,8192]{1,0:T(8,128)(2,1)} collective-permute-done((bf16[48,8192]{1,0:T(8,128)(2,1)S(1)}, bf16[48,8192]{1,0:T(8,128)(2,1)}, u32[]{:S(2)}, u32[]{:S(2)}) %collective-permute-start.20) | collective-permute-done | bytes 786464 | tf_op jit(solution)/shard_map/ppermute | solution.py:41
  81.6 2.5 collective-permute-done.21.refs_7_
  84.3 3.3 collective-permute-start.28
  89.1 13.8 %collective-permute-done.26.refs_0_ = bf16[48,8192]{1,0:T(8,128)(2,1)} collective-permute-done((bf16[48,8192]{1,0:T(8,128)(2,1)S(1)}, bf16[48,8192]{1,0:T(8,128)(2,1)}, u32[]{:S(2)}, u32[]{:S(2)}) %collective-permute-start.26) | collective-permute-done | bytes 786464 | tf_op jit(solution)/shard_map/ppermute | solution.py:41
  103.4 1.9 collective-permute-done.28.refs_2_
  109.1 17.8 %forward.3 = (bf16[384,512]{1,0:T(8,128)(2,1)}, bf16[384,256]{1,0:T(8,128)(2,1)}, bf16[384,8192]{1,0:T(8,128)(2,1)}, bf16[384,8192]{1,0:T(8,128)(2,1)}) custom-call(bf16[48,8192]{1,0:T(8,128)(2,1)} %bitcast.50, bf16[48,8192]{1,0:T(8,128)(2,1)} %copy-done.9, bf16[48,8192]{1,0:T(8,128)(2,1)} %copy-done.8, bf16[48,8192]{1,0:T(8,128)(2,1)} %copy-done.7, ...), custom_call_target="tpu_custom_call" | custom-call | tf_op jit(solution)/shard_map/forward/pallas_call | solution.py:105
  126.9 15.3 %forward.4 = (bf16[288,512]{1,0:T(8,128)(2,1)}, bf16[288,256]{1,0:T(8,128)(2,1)}, bf16[288,8192]{1,0:T(8,128)(2,1)}, bf16[288,8192]{1,0:T(8,128)(2,1)}) custom-call(bf16[48,8192]{1,0:T(8,128)(2,1)} %copy-done.16, bf16[48,8192]{1,0:T(8,128)(2,1)} %copy-done.11, bf16[48,8192]{1,0:T(8,128)(2,1)} %copy-done.15, ...), custom_call_target="tpu_custom_call" | custom-call | tf_op jit(solution)/shard_map/forward/pallas_call | solution.py:105
  142.2 10.8 %forward.5 = (bf16[96,512]{1,0:T(8,128)(2,1)}, bf16[96,256]{1,0:T(8,128)(2,1)}, bf16[96,8192]{1,0:T(8,128)(2,1)}, bf16[96,8192]{1,0:T(8,128)(2,1)}) custom-call(bf16[48,8192]{1,0:T(8,128)(2,1)} %collective-permute-done.26.refs_0_, bf16[48,8192]{1,0:T(8,128)(2,1)} %collective-permute-done.27.refs_1_, bf16[48,8192]{1,0:T(8,128)(2,1)} %collective-permute-done.28.refs_2_, ...), custom_call_target="tpu_custom_call" | custom-call | tf_op jit(solution)/shard_map/forward/pallas_call | solution.py:105
  153.0 9.4 %early.1 = (bf16[3,256,512]{2,1,0:T(8,128)(2,1)}, bf16[3,256,512]{2,1,0:T(8,128)(2,1)}, bf16[3,256,512]{2,1,0:T(8,128)(2,1)}, bf16[3,256,512]{2,1,0:T(8,128)(2,1...) custom-call(s32[4]{0:T(128)} %pad_add_fusion.place, ...), custom_call_target="tpu_custom_call" | custom-call | tf_op jit(solution)/shard_map/early/pallas_call | solution.py:313
  162.4 9.8 %input.3 = (bf16[192,8192]{1,0:T(8,128)(2,1)}, bf16[192,8192]{1,0:T(8,128)(2,1)}) custom-call(bf16[288,512]{1,0:T(8,128)(2,1)} %get-tuple-element.68.refs_7_.refs_0_, bf16[96,512]{1,0:T(8,128)(2,1)} %get-tuple-element.61.refs_8_.refs_1_, bf16[8192,256]{1,0:T(8,128)(2,1)} %refs_2_.3, bf16[8192,256]{1,0:T(8,128)(2,1)} %refs_3_.1), custom_call_target="tpu_custom_call" | custom-call | tf_op jit(solution)/shard_map/input/pallas_call | solution.py:143
  172.7 1.9 collective-permute-start.30
  174.6 2.1 collective-permute-start.31
  177.5 19.9 %late.1 = (bf16[3,256,512]{2,1,0:T(8,128)(2,1)}, bf16[3,256,512]{2,1,0:T(8,128)(2,1)}, bf16[3,256,512]{2,1,0:T(8,128)(2,1)}, bf16[3,256,512]{2,1,0:T(8,128)(2,1)...) custom-call(s32[12]{0:T(128)} %stack.133.place, ...), custom_call_target="tpu_custom_call" | custom-call | tf_op jit(solution)/shard_map/late/pallas_call | solution.py:336
  197.4 2.1 collective-permute-start.33
  199.5 9.8 %input.2 = (bf16[192,8192]{1,0:T(8,128)(2,1)}, bf16[192,8192]{1,0:T(8,128)(2,1)}) custom-call(bf16[384,512]{1,0:T(8,128)(2,1)} %get-tuple-element.52.refs_0_.refs_6_, bf16[8192,256]{1,0:T(8,128)(2,1)} %refs_2_.3, bf16[8192,256]{1,0:T(8,128)(2,1)} %refs_3_.1), custom_call_target="tpu_custom_call" | custom-call | tf_op jit(solution)/shard_map/input/pallas_call | solution.py:143
  209.9 1.6 collective-permute-start.49
  212.0 1.6 collective-permute-start.48
  213.5 3.5 relay.2
  217.1 3.9 %add_convert_fusion = bf16[192,8192]{1,0:T(8,128)(2,1)S(1)} fusion(bf16[192,8192]{1,0:T(8,128)(2,1)} %collective-permute-done.37, bf16[192,8192]{1,0:T(8,128)(2,1)} %get-tuple-element.84), kind=kLoop, calls=%fused_computation | loop fusion | flops 6291456 | bytes 9437184 | tf_op jit(solution)/shard_map/convert_element_type | solution.py:363
  221.0 3.3 collective-permute-start.52
  224.3 1.5 fusion.5
  225.9 7.4 %collective-permute-done.47.a = bf16[3,256,512]{2,1,0:T(8,128)(2,1)} collective-permute-done((bf16[3,256,512]{2,1,0:T(8,128)(2,1)}, bf16[3,256,512]{2,1,0:T(8,128)(2,1)}, u32[]{:S(2)}, u32[]{:S(2)}) %collective-permute-start.47) | collective-permute-done | bytes 786464 | tf_op jit(solution)/shard_map/ppermute | solution.py:57
  233.3 3.2 collective-permute-start.35
  236.5 12.7 %collective-permute-done.48.b = bf16[3,256,512]{2,1,0:T(8,128)(2,1)} collective-permute-done((bf16[3,256,512]{2,1,0:T(8,128)(2,1)}, bf16[3,256,512]{2,1,0:T(8,128)(2,1)}, u32[]{:S(2)}, u32[]{:S(2)}) %collective-permute-start.48) | collective-permute-done | bytes 786464 | tf_op jit(solution)/shard_map/ppermute | solution.py:57
  249.2 3.7 collective-permute-start.42
  254.0 3.5 relay.3
  257.6 4.8 %collective-permute-start.58 = (f32[256,1]{1,0:T(8,128)S(1)}, f32[256,1]{1,0:T(8,128)S(1)}, u32[]{:S(2)}, u32[]{:S(2)}) collective-permute-start(f32[256,1]{1,0:T(8,128)S(1)} %get-tuple-element.107), channel_id=1, source_target_pairs={{0,64},{16,80},{32,96},{48,112},{64,0},{80,16},{96,32},{112,48},{1... | collective-permute-start | bytes 3080 | tf_op jit(solution)/shard_map/ppermute | solution.py:53
  262.4 2.6 fusion.1
  265.1 5.1 %collective-permute-done.34.a = bf16[3,256,512]{2,1,0:T(8,128)(2,1)} collective-permute-done((bf16[3,256,512]{2,1,0:T(8,128)(2,1)}, bf16[3,256,512]{2,1,0:T(8,128)(2,1)}, u32[]{:S(2)}, u32[]{:S(2)}) %collective-permute-start.34) | collective-permute-done | bytes 786464 | tf_op jit(solution)/shard_map/ppermute | solution.py:53
  270.2 2.3 copy-done
  272.5 2.3 join.1
  275.8 1.6 collective-permute-start.41
  277.5 1.7 add_convert_fusion.4
  279.2 1.7 collective-permute-start.43
  280.9 3.0 add_convert_fusion.1
  283.9 27.2 %collective-permute-done.41 = bf16[48,8192]{1,0:T(8,128)(2,1)S(1)} collective-permute-done((bf16[48,8192]{1,0:T(8,128)(2,1)S(1)}, bf16[48,8192]{1,0:T(8,128)(2,1)S(1)}, u32[]{:S(2)}, u32[]{:S(2)}) %collective-permute-start.41) | collective-permute-done | bytes 786464 | tf_op jit(solution)/shard_map/ppermute | solution.py:41
  311.5 2.9 collective-permute-start.51
  314.4 1.9 collective-permute-start.53
  316.9 1.7 collective-permute-done.56
  318.7 1.6 collective-permute-start.54
  320.3 15.3 %collective-permute-done.50.l1 = bf16[3,256,512]{2,1,0:T(8,128)(2,1)S(1)} collective-permute-done((bf16[3,256,512]{2,1,0:T(8,128)(2,1)S(1)}, bf16[3,256,512]{2,1,0:T(8,128)(2,1)S(1)}, u32[]{:S(2)}, u32[]{:S(2)}) %collective-permute-start.50) | collective-permute-done | bytes 786464 | tf_op jit(solution)/shard_map/ppermute | solution.py:53
  335.5 1.6 collective-permute-start.55
  337.1 1.7 collective-permute-start.40
  338.9 6.5 %collective-permute-done.53.r1 = bf16[3,256,512]{2,1,0:T(8,128)(2,1)S(1)} collective-permute-done((bf16[3,256,512]{2,1,0:T(8,128)(2,1)S(1)}, bf16[3,256,512]{2,1,0:T(8,128)(2,1)S(1)}, u32[]{:S(2)}, u32[]{:S(2)}) %collective-permute-start.53) | collective-permute-done | bytes 786464 | tf_op jit(solution)/shard_map/ppermute | solution.py:53
  345.4 3.4 collective-permute-done.46.l0
  348.8 3.2 collective-permute-start.44
  352.1 2.3 last.1
  354.3 7.9 %collective-permute-done.39 = bf16[48,8192]{1,0:T(8,128)(2,1)S(1)} collective-permute-done((bf16[48,8192]{1,0:T(8,128)(2,1)S(1)}, bf16[48,8192]{1,0:T(8,128)(2,1)S(1)}, u32[]{:S(2)}, u32[]{:S(2)}) %collective-permute-start.39) | collective-permute-done | bytes 786464 | tf_op jit(solution)/shard_map/ppermute | solution.py:41
  362.2 6.9 %collective-permute-done.44 = bf16[48,8192]{1,0:T(8,128)(2,1)S(1)} collective-permute-done((bf16[48,8192]{1,0:T(8,128)(2,1)S(1)}, bf16[48,8192]{1,0:T(8,128)(2,1)S(1)}, u32[]{:S(2)}, u32[]{:S(2)}) %collective-permute-start.44) | collective-permute-done | bytes 786464 | tf_op jit(solution)/shard_map/ppermute | solution.py:45
  369.1 1.3 fusion.4
  (157 shorter events, 15.7 us)
Async XLA Ops:
  0.6 6.2 %collective-permute-start.3 = (bf16[48,8192]{1,0:T(8,128)(2,1)}, bf16[48,8192]{1,0:T(8,128)(2,1)}, u32[]{:S(2)}, u32[]{:S(2)}) collective-permute-start(bf16[48,8192]{1,0:T(8,128)(2,1)} %bitcast.46), channel_id=1, source_target_pairs={{0,1},{1,0},{2,3},{3,2},{4,5},{5,4},{6,7},{7,6},{8,9},{9,8},{10,11... | collective-permute-start | bytes 2359304 | tf_op jit(solution)/shard_map/ppermute | solution.py:49
  0.7 22.2 %collective-permute-start.2 = (bf16[48,8192]{1,0:T(8,128)(2,1)}, bf16[48,8192]{1,0:T(8,128)(2,1)S(1)}, u32[]{:S(2)}, u32[]{:S(2)}) collective-permute-start(bf16[48,8192]{1,0:T(8,128)(2,1)} %bitcast.47), channel_id=1, source_target_pairs={{0,8},{1,9},{2,10},{3,11},{4,12},{5,13},{6,14},{7,15},{8,0},{9,1},... | collective-permute-start | bytes 2359304 | tf_op jit(solution)/shard_map/ppermute | solution.py:45
  4.1 21.7 %collective-permute-start.1 = (bf16[48,8192]{1,0:T(8,128)(2,1)}, bf16[48,8192]{1,0:T(8,128)(2,1)S(1)}, u32[]{:S(2)}, u32[]{:S(2)}) collective-permute-start(bf16[48,8192]{1,0:T(8,128)(2,1)} %bitcast.48), channel_id=1, source_target_pairs={{0,6},{1,7},{2,0},{3,1},{4,2},{5,3},{6,4},{7,5},{8,14},{9,15},{10,... | collective-permute-start | bytes 2359304 | tf_op jit(solution)/shard_map/ppermute | solution.py:41
  6.9 20.7 %collective-permute-start = (bf16[48,8192]{1,0:T(8,128)(2,1)}, bf16[48,8192]{1,0:T(8,128)(2,1)S(1)}, u32[]{:S(2)}, u32[]{:S(2)}) collective-permute-start(bf16[48,8192]{1,0:T(8,128)(2,1)} %bitcast.49), channel_id=1, source_target_pairs={{0,2},{1,3},{2,4},{3,5},{4,6},{5,7},{6,0},{7,1},{8,10},{9,11},{10,... | collective-permute-start | bytes 2359304 | tf_op jit(solution)/shard_map/ppermute | solution.py:41
  6.9 22.2 %collective-permute-start.10 = (bf16[48,8192]{1,0:T(8,128)(2,1)}, bf16[48,8192]{1,0:T(8,128)(2,1)S(1)}, u32[]{:S(2)}, u32[]{:S(2)}) collective-permute-start(bf16[48,8192]{1,0:T(8,128)(2,1)} %bitcast.51), channel_id=1, source_target_pairs={{0,1},{1,0},{2,3},{3,2},{4,5},{5,4},{6,7},{7,6},{8,9},{9,8},{10,11... | collective-permute-start | bytes 2359304 | tf_op jit(solution)/shard_map/ppermute | solution.py:49
  6.9 32.4 %collective-permute-start.9 = (bf16[48,8192]{1,0:T(8,128)(2,1)}, bf16[48,8192]{1,0:T(8,128)(2,1)S(1)}, u32[]{:S(2)}, u32[]{:S(2)}) collective-permute-start(bf16[48,8192]{1,0:T(8,128)(2,1)} %bitcast.52), channel_id=1, source_target_pairs={{0,8},{1,9},{2,10},{3,11},{4,12},{5,13},{6,14},{7,15},{8,0},{9,1},... | collective-permute-start | bytes 2359304 | tf_op jit(solution)/shard_map/ppermute | solution.py:45
  22.9 21.1 %collective-permute-start.8 = (bf16[48,8192]{1,0:T(8,128)(2,1)}, bf16[48,8192]{1,0:T(8,128)(2,1)S(1)}, u32[]{:S(2)}, u32[]{:S(2)}) collective-permute-start(bf16[48,8192]{1,0:T(8,128)(2,1)} %bitcast.53), channel_id=1, source_target_pairs={{0,6},{1,7},{2,0},{3,1},{4,2},{5,3},{6,4},{7,5},{8,14},{9,15},{10,... | collective-permute-start | bytes 2359304 | tf_op jit(solution)/shard_map/ppermute | solution.py:41
  25.8 20.3 %collective-permute-start.7 = (bf16[48,8192]{1,0:T(8,128)(2,1)}, bf16[48,8192]{1,0:T(8,128)(2,1)S(1)}, u32[]{:S(2)}, u32[]{:S(2)}) collective-permute-start(bf16[48,8192]{1,0:T(8,128)(2,1)} %bitcast.54), channel_id=1, source_target_pairs={{0,2},{1,3},{2,4},{3,5},{4,6},{5,7},{6,0},{7,1},{8,10},{9,11},{10,... | collective-permute-start | bytes 2359304 | tf_op jit(solution)/shard_map/ppermute | solution.py:41
  27.6 31.2 %collective-permute-start.15 = (bf16[48,8192]{1,0:T(8,128)(2,1)S(1)}, bf16[48,8192]{1,0:T(8,128)(2,1)S(1)}, u32[]{:S(2)}, u32[]{:S(2)}) collective-permute-start(bf16[48,8192]{1,0:T(8,128)(2,1)S(1)} %collective-permute-done.2.refs_3_), channel_id=1, source_target_pairs={{0,6},{1,7},{2,0},{3,1},{4,2},{5,3},{6,4},{7,5},{8,14},{9,15},{10,... | collective-permute-start | bytes 2359304 | tf_op jit(solution)/shard_map/ppermute | solution.py:41
  29.1 38.4 %copy-start.10 = (bf16[48,8192]{1,0:T(8,128)(2,1)}, bf16[48,8192]{1,0:T(8,128)(2,1)S(1)}, u32[]{:S(2)}) copy-start(bf16[48,8192]{1,0:T(8,128)(2,1)S(1)} %collective-permute-done.10.refs_12_) | copy-start | bytes 2359300
  29.1 29.8 %collective-permute-start.6 = (bf16[48,8192]{1,0:T(8,128)(2,1)S(1)}, bf16[48,8192]{1,0:T(8,128)(2,1)S(1)}, u32[]{:S(2)}, u32[]{:S(2)}) collective-permute-start(bf16[48,8192]{1,0:T(8,128)(2,1)S(1)} %collective-permute-done.2.refs_3_), channel_id=1, source_target_pairs={{0,1},{1,0},{2,3},{3,2},{4,5},{5,4},{6,7},{7,6},{8,9},{9,8},{10,11... | collective-permute-start | bytes 2359304 | tf_op jit(solution)/shard_map/ppermute | solution.py:49
  39.3 42.2 %copy-start.12 = (bf16[48,8192]{1,0:T(8,128)(2,1)}, bf16[48,8192]{1,0:T(8,128)(2,1)S(1)}, u32[]{:S(2)}) copy-start(bf16[48,8192]{1,0:T(8,128)(2,1)S(1)} %collective-permute-done.9.refs_11_) | copy-start | bytes 2359300
  39.3 20.9 %collective-permute-start.5 = (bf16[48,8192]{1,0:T(8,128)(2,1)S(1)}, bf16[48,8192]{1,0:T(8,128)(2,1)S(1)}, u32[]{:S(2)}, u32[]{:S(2)}) collective-permute-start(bf16[48,8192]{1,0:T(8,128)(2,1)S(1)} %collective-permute-done.1.refs_2_), channel_id=1, source_target_pairs={{0,1},{1,0},{2,3},{3,2},{4,5},{5,4},{6,7},{7,6},{8,9},{9,8},{10,11... | collective-permute-start | bytes 2359304 | tf_op jit(solution)/shard_map/ppermute | solution.py:49
  44.1 18.2 %collective-permute-start.16 = (bf16[48,8192]{1,0:T(8,128)(2,1)S(1)}, bf16[48,8192]{1,0:T(8,128)(2,1)S(1)}, u32[]{:S(2)}, u32[]{:S(2)}) collective-permute-start(bf16[48,8192]{1,0:T(8,128)(2,1)S(1)} %collective-permute-done.refs_1_), channel_id=1, source_target_pairs={{0,2},{1,3},{2,4},{3,5},{4,6},{5,7},{6,0},{7,1},{8,10},{9,11},{10,... | collective-permute-start | bytes 2359304 | tf_op jit(solution)/shard_map/ppermute | solution.py:41
  46.1 38.0 %copy-start.14 = (bf16[48,8192]{1,0:T(8,128)(2,1)}, bf16[48,8192]{1,0:T(8,128)(2,1)S(1)}, u32[]{:S(2)}) copy-start(bf16[48,8192]{1,0:T(8,128)(2,1)S(1)} %collective-permute-done.7.refs_9_) | copy-start | bytes 2359300
  46.1 18.1 %collective-permute-start.14 = (bf16[48,8192]{1,0:T(8,128)(2,1)S(1)}, bf16[48,8192]{1,0:T(8,128)(2,1)S(1)}, u32[]{:S(2)}, u32[]{:S(2)}) collective-permute-start(bf16[48,8192]{1,0:T(8,128)(2,1)S(1)} %collective-permute-done.refs_1_), channel_id=1, source_target_pairs={{0,8},{1,9},{2,10},{3,11},{4,12},{5,13},{6,14},{7,15},{8,0},{9,1},... | collective-permute-start | bytes 2359304 | tf_op jit(solution)/shard_map/ppermute | solution.py:45
  58.8 8.6 %collective-permute-start.4 = (bf16[48,8192]{1,0:T(8,128)(2,1)S(1)}, bf16[48,8192]{1,0:T(8,128)(2,1)S(1)}, u32[]{:S(2)}, u32[]{:S(2)}) collective-permute-start(bf16[48,8192]{1,0:T(8,128)(2,1)S(1)} %collective-permute-done.refs_1_), channel_id=1, source_target_pairs={{0,1},{1,0},{2,3},{3,2},{4,5},{5,4},{6,7},{7,6},{8,9},{9,8},{10,11... | collective-permute-start | bytes 2359304 | tf_op jit(solution)/shard_map/ppermute | solution.py:49
  58.9 22.1 %collective-permute-start.20 = (bf16[48,8192]{1,0:T(8,128)(2,1)S(1)}, bf16[48,8192]{1,0:T(8,128)(2,1)}, u32[]{:S(2)}, u32[]{:S(2)}) collective-permute-start(bf16[48,8192]{1,0:T(8,128)(2,1)S(1)} %collective-permute-done.9.refs_11_), channel_id=1, source_target_pairs={{0,2},{1,3},{2,4},{3,5},{4,6},{5,7},{6,0},{7,1},{8,10},{9,11},{10,... | collective-permute-start | bytes 2359304 | tf_op jit(solution)/shard_map/ppermute | solution.py:41
  60.2 20.8 %collective-permute-start.13 = (bf16[48,8192]{1,0:T(8,128)(2,1)S(1)}, bf16[48,8192]{1,0:T(8,128)(2,1)S(1)}, u32[]{:S(2)}, u32[]{:S(2)}) collective-permute-start(bf16[48,8192]{1,0:T(8,128)(2,1)S(1)} %collective-permute-done.9.refs_11_), channel_id=1, source_target_pairs={{0,1},{1,0},{2,3},{3,2},{4,5},{5,4},{6,7},{7,6},{8,9},{9,8},{10,11... | collective-permute-start | bytes 2359304 | tf_op jit(solution)/shard_map/ppermute | solution.py:49
  62.3 19.3 %collective-permute-start.22 = (bf16[48,8192]{1,0:T(8,128)(2,1)S(1)}, bf16[48,8192]{1,0:T(8,128)(2,1)}, u32[]{:S(2)}, u32[]{:S(2)}) collective-permute-start(bf16[48,8192]{1,0:T(8,128)(2,1)S(1)} %collective-permute-done.8.refs_10_), channel_id=1, source_target_pairs={{0,6},{1,7},{2,0},{3,1},{4,2},{5,3},{6,4},{7,5},{8,14},{9,15},{10,... | collective-permute-start | bytes 2359304 | tf_op jit(solution)/shard_map/ppermute | solution.py:41
  64.2 19.9 %collective-permute-start.21 = (bf16[48,8192]{1,0:T(8,128)(2,1)S(1)}, bf16[48,8192]{1,0:T(8,128)(2,1)}, u32[]{:S(2)}, u32[]{:S(2)}) collective-permute-start(bf16[48,8192]{1,0:T(8,128)(2,1)S(1)} %collective-permute-done.8.refs_10_), channel_id=1, source_target_pairs={{0,8},{1,9},{2,10},{3,11},{4,12},{5,13},{6,14},{7,15},{8,0},{9,1},... | collective-permute-start | bytes 2359304 | tf_op jit(solution)/shard_map/ppermute | solution.py:45
  67.4 16.7 %collective-permute-start.12 = (bf16[48,8192]{1,0:T(8,128)(2,1)S(1)}, bf16[48,8192]{1,0:T(8,128)(2,1)S(1)}, u32[]{:S(2)}, u32[]{:S(2)}) collective-permute-start(bf16[48,8192]{1,0:T(8,128)(2,1)S(1)} %collective-permute-done.8.refs_10_), channel_id=1, source_target_pairs={{0,1},{1,0},{2,3},{3,2},{4,5},{5,4},{6,7},{7,6},{8,9},{9,8},{10,11... | collective-permute-start | bytes 2359304 | tf_op jit(solution)/shard_map/ppermute | solution.py:49
  80.9 3.3 collective-permute-start.11
  81.0 7.5 %collective-permute-start.18 = (bf16[48,8192]{1,0:T(8,128)(2,1)S(1)}, bf16[48,8192]{1,0:T(8,128)(2,1)S(1)}, u32[]{:S(2)}, u32[]{:S(2)}) collective-permute-start(bf16[48,8192]{1,0:T(8,128)(2,1)S(1)} %collective-permute-done.15.refs_1_), channel_id=1, source_target_pairs={{0,1},{1,0},{2,3},{3,2},{4,5},{5,4},{6,7},{7,6},{8,9},{9,8},{10,11... | collective-permute-start | bytes 2359304 | tf_op jit(solution)/shard_map/ppermute | solution.py:49
  81.5 7.2 %collective-permute-start.19 = (bf16[48,8192]{1,0:T(8,128)(2,1)S(1)}, bf16[48,8192]{1,0:T(8,128)(2,1)}, u32[]{:S(2)}, u32[]{:S(2)}) collective-permute-start(bf16[48,8192]{1,0:T(8,128)(2,1)S(1)} %collective-permute-done.16.refs_2_), channel_id=1, source_target_pairs={{0,1},{1,0},{2,3},{3,2},{4,5},{5,4},{6,7},{7,6},{8,9},{9,8},{10,11... | collective-permute-start | bytes 2359304 | tf_op jit(solution)/shard_map/ppermute | solution.py:49
  84.1 18.8 %collective-permute-start.26 = (bf16[48,8192]{1,0:T(8,128)(2,1)S(1)}, bf16[48,8192]{1,0:T(8,128)(2,1)}, u32[]{:S(2)}, u32[]{:S(2)}) collective-permute-start(bf16[48,8192]{1,0:T(8,128)(2,1)S(1)} %collective-permute-done.14.refs_0_), channel_id=1, source_target_pairs={{0,2},{1,3},{2,4},{3,5},{4,6},{5,7},{6,0},{7,1},{8,10},{9,11},{10,... | collective-permute-start | bytes 2359304 | tf_op jit(solution)/shard_map/ppermute | solution.py:41
  84.1 18.7 %collective-permute-start.17 = (bf16[48,8192]{1,0:T(8,128)(2,1)S(1)}, bf16[48,8192]{1,0:T(8,128)(2,1)}, u32[]{:S(2)}, u32[]{:S(2)}) collective-permute-start(bf16[48,8192]{1,0:T(8,128)(2,1)S(1)} %collective-permute-done.14.refs_0_), channel_id=1, source_target_pairs={{0,1},{1,0},{2,3},{3,2},{4,5},{5,4},{6,7},{7,6},{8,9},{9,8},{10,11... | collective-permute-start | bytes 2359304 | tf_op jit(solution)/shard_map/ppermute | solution.py:49
  84.3 21.0 %collective-permute-start.28 = (bf16[48,8192]{1,0:T(8,128)(2,1)}, bf16[48,8192]{1,0:T(8,128)(2,1)}, u32[]{:S(2)}, u32[]{:S(2)}) collective-permute-start(bf16[48,8192]{1,0:T(8,128)(2,1)} %collective-permute-done.21.refs_7_), channel_id=1, source_target_pairs={{0,6},{1,7},{2,0},{3,1},{4,2},{5,3},{6,4},{7,5},{8,14},{9,15},{10,... | collective-permute-start | bytes 2359304 | tf_op jit(solution)/shard_map/ppermute | solution.py:41
  88.5 38.4 %collective-permute-start.24 = (bf16[48,8192]{1,0:T(8,128)(2,1)}, bf16[48,8192]{1,0:T(8,128)(2,1)}, u32[]{:S(2)}, u32[]{:S(2)}) collective-permute-start(bf16[48,8192]{1,0:T(8,128)(2,1)} %collective-permute-done.21.refs_7_), channel_id=1, source_target_pairs={{0,1},{1,0},{2,3},{3,2},{4,5},{5,4},{6,7},{7,6},{8,9},{9,8},{10,11... | collective-permute-start | bytes 2359304 | tf_op jit(solution)/shard_map/ppermute | solution.py:49
  88.8 38.1 %collective-permute-start.23 = (bf16[48,8192]{1,0:T(8,128)(2,1)}, bf16[48,8192]{1,0:T(8,128)(2,1)}, u32[]{:S(2)}, u32[]{:S(2)}) collective-permute-start(bf16[48,8192]{1,0:T(8,128)(2,1)} %collective-permute-done.20.refs_6_), channel_id=1, source_target_pairs={{0,1},{1,0},{2,3},{3,2},{4,5},{5,4},{6,7},{7,6},{8,9},{9,8},{10,11... | collective-permute-start | bytes 2359304 | tf_op jit(solution)/shard_map/ppermute | solution.py:49
  102.9 24.0 %collective-permute-start.25 = (bf16[48,8192]{1,0:T(8,128)(2,1)}, bf16[48,8192]{1,0:T(8,128)(2,1)}, u32[]{:S(2)}, u32[]{:S(2)}) collective-permute-start(bf16[48,8192]{1,0:T(8,128)(2,1)} %collective-permute-done.22.refs_8_), channel_id=1, source_target_pairs={{0,1},{1,0},{2,3},{3,2},{4,5},{5,4},{6,7},{7,6},{8,9},{9,8},{10,11... | collective-permute-start | bytes 2359304 | tf_op jit(solution)/shard_map/ppermute | solution.py:49
  102.9 39.3 %collective-permute-start.27 = (bf16[48,8192]{1,0:T(8,128)(2,1)}, bf16[48,8192]{1,0:T(8,128)(2,1)}, u32[]{:S(2)}, u32[]{:S(2)}) collective-permute-start(bf16[48,8192]{1,0:T(8,128)(2,1)} %collective-permute-done.26.refs_0_), channel_id=1, source_target_pairs={{0,1},{1,0},{2,3},{3,2},{4,5},{5,4},{6,7},{7,6},{8,9},{9,8},{10,11... | collective-permute-start | bytes 2359304 | tf_op jit(solution)/shard_map/ppermute | solution.py:49
  105.3 36.9 %collective-permute-start.29 = (bf16[48,8192]{1,0:T(8,128)(2,1)}, bf16[48,8192]{1,0:T(8,128)(2,1)}, u32[]{:S(2)}, u32[]{:S(2)}) collective-permute-start(bf16[48,8192]{1,0:T(8,128)(2,1)} %collective-permute-done.28.refs_2_), channel_id=1, source_target_pairs={{0,1},{1,0},{2,3},{3,2},{4,5},{5,4},{6,7},{7,6},{8,9},{9,8},{10,11... | collective-permute-start | bytes 2359304 | tf_op jit(solution)/shard_map/ppermute | solution.py:49
  172.2 44.8 %collective-permute-start.37 = (bf16[192,8192]{1,0:T(8,128)(2,1)}, bf16[192,8192]{1,0:T(8,128)(2,1)}, u32[]{:S(2)}, u32[]{:S(2)}) collective-permute-start(bf16[192,8192]{1,0:T(8,128)(2,1)} %get-tuple-element.85), channel_id=1, source_target_pairs={{0,1},{1,0},{2,3},{3,2},{4,5},{5,4},{6,7},{7,6},{8,9},{9,8},{10,11... | collective-permute-start | bytes 9437192 | tf_op jit(solution)/shard_map/ppermute | solution.py:49
  172.7 38.8 %collective-permute-start.30 = (bf16[3,256,512]{2,1,0:T(8,128)(2,1)}, bf16[3,256,512]{2,1,0:T(8,128)(2,1)}, u32[]{:S(2)}, u32[]{:S(2)}) collective-permute-start(bf16[3,256,512]{2,1,0:T(8,128)(2,1)} %get-tuple-element.74), channel_id=1, source_target_pairs={{0,32},{16,48},{32,64},{48,80},{64,96},{80,112},{96,0},{112,16},{1... | collective-permute-start | bytes 2359304 | tf_op jit(solution)/shard_map/ppermute | solution.py:53
  174.6 37.3 %collective-permute-start.31 = (bf16[3,256,512]{2,1,0:T(8,128)(2,1)}, bf16[3,256,512]{2,1,0:T(8,128)(2,1)}, u32[]{:S(2)}, u32[]{:S(2)}) collective-permute-start(bf16[3,256,512]{2,1,0:T(8,128)(2,1)} %get-tuple-element.75), channel_id=1, source_target_pairs={{0,96},{16,112},{32,0},{48,16},{64,32},{80,48},{96,64},{112,80},{1... | collective-permute-start | bytes 2359304 | tf_op jit(solution)/shard_map/ppermute | solution.py:53
  197.4 11.9 %collective-permute-start.33 = (f32[256,128]{1,0:T(8,128)}, f32[256,128]{1,0:T(8,128)S(1)}, u32[]{:S(2)}, u32[]{:S(2)}) collective-permute-start(f32[256,128]{1,0:T(8,128)} %get-tuple-element.76.ratio), channel_id=1, source_target_pairs={{0,96},{16,112},{32,0},{48,16},{64,32},{80,48},{96,64},{112,80},{1... | collective-permute-start | bytes 393224 | tf_op jit(solution)/shard_map/ppermute | solution.py:53
  199.5 10.4 %collective-permute-start.32 = (f32[256,128]{1,0:T(8,128)}, f32[256,128]{1,0:T(8,128)}, u32[]{:S(2)}, u32[]{:S(2)}) collective-permute-start(f32[256,128]{1,0:T(8,128)} %get-tuple-element.76.ratio), channel_id=1, source_target_pairs={{0,32},{16,48},{32,64},{48,80},{64,96},{80,112},{96,0},{112,16},{1... | collective-permute-start | bytes 393224 | tf_op jit(solution)/shard_map/ppermute | solution.py:53
  209.3 65.5 %collective-permute-start.36 = (bf16[192,8192]{1,0:T(8,128)(2,1)}, bf16[192,8192]{1,0:T(8,128)(2,1)}, u32[]{:S(2)}, u32[]{:S(2)}) collective-permute-start(bf16[192,8192]{1,0:T(8,128)(2,1)} %get-tuple-element.82), channel_id=1, source_target_pairs={{0,1},{1,0},{2,3},{3,2},{4,5},{5,4},{6,7},{7,6},{8,9},{9,8},{10,11... | collective-permute-start | bytes 9437192 | tf_op jit(solution)/shard_map/ppermute | solution.py:49
  209.9 11.1 %collective-permute-start.49 = (f32[256,128]{1,0:T(8,128)S(1)}, f32[256,128]{1,0:T(8,128)S(1)}, u32[]{:S(2)}, u32[]{:S(2)}) collective-permute-start(f32[256,128]{1,0:T(8,128)S(1)} %copy-done.1), channel_id=1, source_target_pairs={{0,16},{16,0},{32,48},{48,32},{64,80},{80,64},{96,112},{112,96},{1... | collective-permute-start | bytes 393224 | tf_op jit(solution)/shard_map/ppermute | solution.py:57
  211.5 21.7 %collective-permute-start.47 = (bf16[3,256,512]{2,1,0:T(8,128)(2,1)}, bf16[3,256,512]{2,1,0:T(8,128)(2,1)}, u32[]{:S(2)}, u32[]{:S(2)}) collective-permute-start(bf16[3,256,512]{2,1,0:T(8,128)(2,1)} %get-tuple-element.91), channel_id=1, source_target_pairs={{0,16},{16,0},{32,48},{48,32},{64,80},{80,64},{96,112},{112,96},{1... | collective-permute-start | bytes 2359304 | tf_op jit(solution)/shard_map/ppermute | solution.py:57
  212.0 37.2 %collective-permute-start.48 = (bf16[3,256,512]{2,1,0:T(8,128)(2,1)}, bf16[3,256,512]{2,1,0:T(8,128)(2,1)}, u32[]{:S(2)}, u32[]{:S(2)}) collective-permute-start(bf16[3,256,512]{2,1,0:T(8,128)(2,1)} %get-tuple-element.92), channel_id=1, source_target_pairs={{0,16},{16,0},{32,48},{48,32},{64,80},{80,64},{96,112},{112,96},{1... | collective-permute-start | bytes 2359304 | tf_op jit(solution)/shard_map/ppermute | solution.py:57
  217.1 32.1 %collective-permute-start.45 = (bf16[3,256,512]{2,1,0:T(8,128)(2,1)}, bf16[3,256,512]{2,1,0:T(8,128)(2,1)}, u32[]{:S(2)}, u32[]{:S(2)}) collective-permute-start(bf16[3,256,512]{2,1,0:T(8,128)(2,1)} %get-tuple-element.88), channel_id=1, source_target_pairs={{0,32},{16,48},{32,64},{48,80},{64,96},{80,112},{96,0},{112,16},{1... | collective-permute-start | bytes 2359304 | tf_op jit(solution)/shard_map/ppermute | solution.py:53
  221.0 36.6 %collective-permute-start.52 = (bf16[3,256,512]{2,1,0:T(8,128)(2,1)}, bf16[3,256,512]{2,1,0:T(8,128)(2,1)}, u32[]{:S(2)}, u32[]{:S(2)}) collective-permute-start(bf16[3,256,512]{2,1,0:T(8,128)(2,1)} %get-tuple-element.95), channel_id=1, source_target_pairs={{0,96},{16,112},{32,0},{48,16},{64,32},{80,48},{96,64},{112,80},{1... | collective-permute-start | bytes 2359304 | tf_op jit(solution)/shard_map/ppermute | solution.py:53
  233.3 31.7 %collective-permute-start.35 = (bf16[3,256,512]{2,1,0:T(8,128)(2,1)}, bf16[3,256,512]{2,1,0:T(8,128)(2,1)}, u32[]{:S(2)}, u32[]{:S(2)}) collective-permute-start(bf16[3,256,512]{2,1,0:T(8,128)(2,1)} %get-tuple-element.78), channel_id=1, source_target_pairs={{0,96},{16,112},{32,0},{48,16},{64,32},{80,48},{96,64},{112,80},{1... | collective-permute-start | bytes 2359304 | tf_op jit(solution)/shard_map/ppermute | solution.py:53
  249.2 21.0 %collective-permute-start.34 = (bf16[3,256,512]{2,1,0:T(8,128)(2,1)}, bf16[3,256,512]{2,1,0:T(8,128)(2,1)}, u32[]{:S(2)}, u32[]{:S(2)}) collective-permute-start(bf16[3,256,512]{2,1,0:T(8,128)(2,1)} %get-tuple-element.77), channel_id=1, source_target_pairs={{0,32},{16,48},{32,64},{48,80},{64,96},{80,112},{96,0},{112,16},{1... | collective-permute-start | bytes 2359304 | tf_op jit(solution)/shard_map/ppermute | solution.py:53
  249.2 28.3 %collective-permute-start.42 = (bf16[48,8192]{1,0:T(8,128)(2,1)}, bf16[48,8192]{1,0:T(8,128)(2,1)}, u32[]{:S(2)}, u32[]{:S(2)}) collective-permute-start(bf16[48,8192]{1,0:T(8,128)(2,1)} %get-tuple-element.105), channel_id=1, source_target_pairs={{0,6},{1,7},{2,0},{3,1},{4,2},{5,3},{6,4},{7,5},{8,14},{9,15},{10,... | collective-permute-start | bytes 2359304 | tf_op jit(solution)/shard_map/ppermute | solution.py:41
  257.6 53.9 %collective-permute-start.58 = (f32[256,1]{1,0:T(8,128)S(1)}, f32[256,1]{1,0:T(8,128)S(1)}, u32[]{:S(2)}, u32[]{:S(2)}) collective-permute-start(f32[256,1]{1,0:T(8,128)S(1)} %get-tuple-element.107), channel_id=1, source_target_pairs={{0,64},{16,80},{32,96},{48,112},{64,0},{80,16},{96,32},{112,48},{1... | collective-permute-start | bytes 3080 | tf_op jit(solution)/shard_map/ppermute | solution.py:53
  265.0 49.5 %collective-permute-start.57 = (f32[256,1]{1,0:T(8,128)S(1)}, f32[256,1]{1,0:T(8,128)S(1)}, u32[]{:S(2)}, u32[]{:S(2)}) collective-permute-start(f32[256,1]{1,0:T(8,128)S(1)} %get-tuple-element.107), channel_id=1, source_target_pairs={{0,96},{16,112},{32,0},{48,16},{64,32},{80,48},{96,64},{112,80},{1... | collective-permute-start | bytes 3080 | tf_op jit(solution)/shard_map/ppermute | solution.py:53
  274.8 41.6 %collective-permute-start.38 = (bf16[48,8192]{1,0:T(8,128)(2,1)S(1)}, bf16[48,8192]{1,0:T(8,128)(2,1)S(1)}, u32[]{:S(2)}, u32[]{:S(2)}) collective-permute-start(bf16[48,8192]{1,0:T(8,128)(2,1)S(1)} %copy-done.24), channel_id=1, source_target_pairs={{0,2},{1,3},{2,4},{3,5},{4,6},{5,7},{6,0},{7,1},{8,10},{9,11},{10,... | collective-permute-start | bytes 2359304 | tf_op jit(solution)/shard_map/ppermute | solution.py:41
  275.8 35.3 %collective-permute-start.41 = (bf16[48,8192]{1,0:T(8,128)(2,1)S(1)}, bf16[48,8192]{1,0:T(8,128)(2,1)S(1)}, u32[]{:S(2)}, u32[]{:S(2)}) collective-permute-start(bf16[48,8192]{1,0:T(8,128)(2,1)S(1)} %copy-done.25), channel_id=1, source_target_pairs={{0,2},{1,3},{2,4},{3,5},{4,6},{5,7},{6,0},{7,1},{8,10},{9,11},{10,... | collective-permute-start | bytes 2359304 | tf_op jit(solution)/shard_map/ppermute | solution.py:41
  277.5 74.5 %slice-start = ((s8[4718592]{0:T(1024)(128)(4,1)}), s8[4194304]{0:T(1024)(128)(4,1)S(1)}, s32[]{:S(2)}) async-start(s8[4718592]{0:T(1024)(128)(4,1)} %bitcast.43), calls=%async_computation | async-start | bytes 8388608
  279.2 72.8 %slice-start.1 = ((s8[4718592]{0:T(1024)(128)(4,1)}), s8[524288]{0:T(1024)(128)(4,1)S(1)}, s32[]{:S(2)}) async-start(s8[4718592]{0:T(1024)(128)(4,1)} %bitcast.43), calls=%async_computation.1 | async-start | bytes 1048576
  279.2 31.9 %collective-permute-start.43 = (bf16[48,8192]{1,0:T(8,128)(2,1)S(1)}, bf16[48,8192]{1,0:T(8,128)(2,1)S(1)}, u32[]{:S(2)}, u32[]{:S(2)}) collective-permute-start(bf16[48,8192]{1,0:T(8,128)(2,1)S(1)} %add_convert_fusion.4), channel_id=1, source_target_pairs={{0,6},{1,7},{2,0},{3,1},{4,2},{5,3},{6,4},{7,5},{8,14},{9,15},{10,... | collective-permute-start | bytes 2359304 | tf_op jit(solution)/shard_map/ppermute | solution.py:41
  311.1 7.6 %collective-permute-start.56 = (f32[256,1]{1,0:T(8,128)S(1)}, f32[256,1]{1,0:T(8,128)S(1)}, u32[]{:S(2)}, u32[]{:S(2)}) collective-permute-start(f32[256,1]{1,0:T(8,128)S(1)} %get-tuple-element.107), channel_id=1, source_target_pairs={{0,32},{16,48},{32,64},{48,80},{64,96},{80,112},{96,0},{112,16},{1... | collective-permute-start | bytes 3080 | tf_op jit(solution)/shard_map/ppermute | solution.py:53
  311.1 24.4 %collective-permute-start.50 = (bf16[3,256,512]{2,1,0:T(8,128)(2,1)S(1)}, bf16[3,256,512]{2,1,0:T(8,128)(2,1)S(1)}, u32[]{:S(2)}, u32[]{:S(2)}) collective-permute-start(bf16[3,256,512]{2,1,0:T(8,128)(2,1)S(1)} %copy-done.29), channel_id=1, source_target_pairs={{0,32},{16,48},{32,64},{48,80},{64,96},{80,112},{96,0},{112,16},{1... | collective-permute-start | bytes 2359304 | tf_op jit(solution)/shard_map/ppermute | solution.py:53
  311.5 25.6 %collective-permute-start.51 = (bf16[3,256,512]{2,1,0:T(8,128)(2,1)S(1)}, bf16[3,256,512]{2,1,0:T(8,128)(2,1)S(1)}, u32[]{:S(2)}, u32[]{:S(2)}) collective-permute-start(bf16[3,256,512]{2,1,0:T(8,128)(2,1)S(1)} %copy-done.28), channel_id=1, source_target_pairs={{0,96},{16,112},{32,0},{48,16},{64,32},{80,48},{96,64},{112,80},{1... | collective-permute-start | bytes 2359304 | tf_op jit(solution)/shard_map/ppermute | solution.py:53
  314.4 30.9 %collective-permute-start.53 = (bf16[3,256,512]{2,1,0:T(8,128)(2,1)S(1)}, bf16[3,256,512]{2,1,0:T(8,128)(2,1)S(1)}, u32[]{:S(2)}, u32[]{:S(2)}) collective-permute-start(bf16[3,256,512]{2,1,0:T(8,128)(2,1)S(1)} %get-tuple-element.100), channel_id=1, source_target_pairs={{0,96},{16,112},{32,0},{48,16},{64,32},{80,48},{96,64},{112,80},{1... | collective-permute-start | bytes 2359304 | tf_op jit(solution)/shard_map/ppermute | solution.py:53
  316.4 32.4 %collective-permute-start.46 = (bf16[3,256,512]{2,1,0:T(8,128)(2,1)S(1)}, bf16[3,256,512]{2,1,0:T(8,128)(2,1)S(1)}, u32[]{:S(2)}, u32[]{:S(2)}) collective-permute-start(bf16[3,256,512]{2,1,0:T(8,128)(2,1)S(1)} %get-tuple-element.101), channel_id=1, source_target_pairs={{0,32},{16,48},{32,64},{48,80},{64,96},{80,112},{96,0},{112,16},{1... | collective-permute-start | bytes 2359304 | tf_op jit(solution)/shard_map/ppermute | solution.py:53
  318.7 33.3 %collective-permute-start.54 = (bf16[3,256,512]{2,1,0:T(8,128)(2,1)S(1)}, bf16[3,256,512]{2,1,0:T(8,128)(2,1)S(1)}, u32[]{:S(2)}, u32[]{:S(2)}) collective-permute-start(bf16[3,256,512]{2,1,0:T(8,128)(2,1)S(1)} %get-tuple-element.79), channel_id=1, source_target_pairs={{0,16},{16,0},{32,48},{48,32},{64,80},{80,64},{96,112},{112,96},{1... | collective-permute-start | bytes 2359304 | tf_op jit(solution)/shard_map/ppermute | solution.py:57
  335.5 16.5 %collective-permute-start.55 = (bf16[3,256,512]{2,1,0:T(8,128)(2,1)S(1)}, bf16[3,256,512]{2,1,0:T(8,128)(2,1)S(1)}, u32[]{:S(2)}, u32[]{:S(2)}) collective-permute-start(bf16[3,256,512]{2,1,0:T(8,128)(2,1)S(1)} %get-tuple-element.80), channel_id=1, source_target_pairs={{0,16},{16,0},{32,48},{48,32},{64,80},{80,64},{96,112},{112,96},{1... | collective-permute-start | bytes 2359304 | tf_op jit(solution)/shard_map/ppermute | solution.py:57
  337.1 17.2 %collective-permute-start.40 = (bf16[48,8192]{1,0:T(8,128)(2,1)S(1)}, bf16[48,8192]{1,0:T(8,128)(2,1)S(1)}, u32[]{:S(2)}, u32[]{:S(2)}) collective-permute-start(bf16[48,8192]{1,0:T(8,128)(2,1)S(1)} %slice.93), channel_id=1, source_target_pairs={{0,6},{1,7},{2,0},{3,1},{4,2},{5,3},{6,4},{7,5},{8,14},{9,15},{10,... | collective-permute-start | bytes 2359304 | tf_op jit(solution)/shard_map/ppermute | solution.py:41
  345.4 16.9 %collective-permute-start.39 = (bf16[48,8192]{1,0:T(8,128)(2,1)S(1)}, bf16[48,8192]{1,0:T(8,128)(2,1)S(1)}, u32[]{:S(2)}, u32[]{:S(2)}) collective-permute-start(bf16[48,8192]{1,0:T(8,128)(2,1)S(1)} %get-tuple-element.102), channel_id=1, source_target_pairs={{0,2},{1,3},{2,4},{3,5},{4,6},{5,7},{6,0},{7,1},{8,10},{9,11},{10,... | collective-permute-start | bytes 2359304 | tf_op jit(solution)/shard_map/ppermute | solution.py:41
  348.8 20.3 %collective-permute-start.44 = (bf16[48,8192]{1,0:T(8,128)(2,1)S(1)}, bf16[48,8192]{1,0:T(8,128)(2,1)S(1)}, u32[]{:S(2)}, u32[]{:S(2)}) collective-permute-start(bf16[48,8192]{1,0:T(8,128)(2,1)S(1)} %get-tuple-element.103), channel_id=1, source_target_pairs={{0,8},{1,9},{2,10},{3,11},{4,12},{5,13},{6,14},{7,15},{8,0},{9,1},... | collective-permute-start | bytes 2359304 | tf_op jit(solution)/shard_map/ppermute | solution.py:45
  (27 other events, 494.3 us)

commit v5 on v4

--- a/solution.py
+++ b/solution.py
@@ -266,10 +266,8 @@
 
     @pl.when(step == 0)
     def _():
-        ggu = jnp.concatenate([r[...] for r in ggus], axis=0).astype(jnp.float32)
-        ggu_t[...] = ggu.T.astype(ggu_t.dtype)
-        hidden = jnp.concatenate([r[...] for r in hids], axis=0).astype(jnp.float32)
-        hid_t[...] = hidden.T.astype(hid_t.dtype)
+        ggu_t[...] = jnp.concatenate([r[...] for r in ggus], axis=0).T
+        hid_t[...] = jnp.concatenate([r[...] for r in hids], axis=0).T
         moment[...] = jnp.zeros_like(moment)
 
     gradient_step(ggu_t, hid_t, toks, outs, functools.partial(to_one, step, alone, None), moment)
@@ -417,7 +415,6 @@
     a, b = to_z(first[0], 1), to_z(first[1], -1)
     c, d = to_y_next(first[2]), to_y_next(first[3])
     far, far_p = input_gradient([after(ggus[1], moment), ggus[2]], w_gate, w_up)
-    far_p, moment = lax.optimization_barrier((far_p, moment))
     far_p = to_core(far_p)
     far = bf(f32(far) + f32(far_p))
     e, f, own_g, own_h, own_l, own_r, pieces, ratio = gradients_late(target[EARLY:], toks, outs, ggu_t, hid_t, moment)

time: 372 us -> 368 us (0.989)
  starting transfers between devices: 69.9 us -> 62.5 us
    ppermute x5, waiting for transfers between devices: 35.7 us -> 30.6 us  [to_y_half(): return lax.ppermute(value, 'fsdp', fsdp_pairs(0, 1, 0))]
    ppermute x15, waiting for transfers between devices: 32.1 us -> 36.8 us  [to_z(): return lax.ppermute(value, 'lang', lang_pairs(step, 0))]
    ppermute x16, waiting for transfers between devices: 83 us -> 86.9 us  [to_x(): return lax.ppermute(value, 'fsdp', fsdp_pairs(step, 0, 0))]
  transfers between devices with their start and end apart: 59 -> 59, of which waited for: 22 -> 23; matrix products, arithmetic and copies ran while one was open for 5% -> 5% of each run, Pallas kernels for 20% -> 20%
where the time goes in v5:
time: 368 us; the launch traced here: 366 us
  waiting for transfers between devices  174 us (47%)
  Pallas kernels  104 us (28%)
  starting transfers between devices  62.5 us (17%)
  other arithmetic  14.9 us (4%)
  local copies, waits for them, and re-layouts  8.73 us (2%)
    ppermute x16, waiting for transfers between devices, to_x(): return lax.ppermute(value, 'fsdp', fsdp_pairs(step, 0, 0))  86.9 us
    pallas_call x3, Pallas kernels, forward(): pl.pallas_call(functools.partial(forward_kernel, n), name='forward', grid...  43.8 us
    ppermute x15, waiting for transfers between devices, to_z(): return lax.ppermute(value, 'lang', lang_pairs(step, 0))  36.8 us
    ppermute x5, waiting for transfers between devices, to_y_half(): return lax.ppermute(value, 'fsdp', fsdp_pairs(0, 1, 0))  30.6 us
    ppermute x16, starting transfers between devices, to_x(): return lax.ppermute(value, 'fsdp', fsdp_pairs(step, 0, 0))  21.8 us
    ppermute x5, waiting for transfers between devices, to_y_next(): return lax.ppermute(value, 'lang', lang_pairs(0, 1))  20.2 us
    ppermute x15, starting transfers between devices, to_z(): return lax.ppermute(value, 'lang', lang_pairs(step, 0))  20 us
    pallas_call x1, Pallas kernels, gradients_late(): pl.pallas_call(functools.partial(late_kernel, len(toks), depth), name='la...  19.9 us
  transfers between devices with their start and end apart: 59, of which 23 were waited for; matrix products, arithmetic and copies ran while one was open for 5% of the time, Pallas kernels for 20%

profile of v5, /device:TPU:0, one launch (start us, length us, event | category | flops | bytes accessed | tf_op | source)
XLA Modules:
  0.0 366.3 jit_solution(6369597978653108714)
XLA Ops:
  0.7 3.4 collective-permute-start.2
  4.1 2.8 collective-permute-start.1
  7.3 15.6 %collective-permute-done.2.refs_3_ = bf16[48,8192]{1,0:T(8,128)(2,1)S(1)} collective-permute-done((bf16[48,8192]{1,0:T(8,128)(2,1)}, bf16[48,8192]{1,0:T(8,128)(2,1)S(1)}, u32[]{:S(2)}, u32[]{:S(2)}) %collective-permute-start.2) | collective-permute-done | bytes 786464 | tf_op jit(solution)/shard_map/ppermute | solution.py:45
  22.9 2.9 collective-permute-start.8
  25.8 1.8 collective-permute-done.refs_1_
  27.6 1.5 collective-permute-start.15
  29.2 10.1 %collective-permute-done.9.refs_11_ = bf16[48,8192]{1,0:T(8,128)(2,1)S(1)} collective-permute-done((bf16[48,8192]{1,0:T(8,128)(2,1)}, bf16[48,8192]{1,0:T(8,128)(2,1)S(1)}, u32[]{:S(2)}, u32[]{:S(2)}) %collective-permute-start.9) | collective-permute-done | bytes 786464 | tf_op jit(solution)/shard_map/ppermute | solution.py:45
  39.3 4.8 %collective-permute-done.8.refs_10_ = bf16[48,8192]{1,0:T(8,128)(2,1)S(1)} collective-permute-done((bf16[48,8192]{1,0:T(8,128)(2,1)}, bf16[48,8192]{1,0:T(8,128)(2,1)S(1)}, u32[]{:S(2)}, u32[]{:S(2)}) %collective-permute-start.8) | collective-permute-done | bytes 786464 | tf_op jit(solution)/shard_map/ppermute | solution.py:41
  44.1 1.1 collective-permute-start.16
  45.2 1.0 collective-permute-done.7.refs_9_
  46.1 3.2 collective-permute-start.14
  49.3 9.5 %collective-permute-done.15.refs_1_ = bf16[48,8192]{1,0:T(8,128)(2,1)S(1)} collective-permute-done((bf16[48,8192]{1,0:T(8,128)(2,1)S(1)}, bf16[48,8192]{1,0:T(8,128)(2,1)S(1)}, u32[]{:S(2)}, u32[]{:S(2)}) %collective-permute-start.15) | collective-permute-done | bytes 786464 | tf_op jit(solution)/shard_map/ppermute | solution.py:41
  58.9 1.3 collective-permute-start.20
  60.4 1.8 collective-permute-done.16.refs_2_
  62.3 1.4 collective-permute-start.22
  64.2 3.2 collective-permute-start.21
  67.5 13.4 %collective-permute-done.20.refs_6_ = bf16[48,8192]{1,0:T(8,128)(2,1)} collective-permute-done((bf16[48,8192]{1,0:T(8,128)(2,1)S(1)}, bf16[48,8192]{1,0:T(8,128)(2,1)}, u32[]{:S(2)}, u32[]{:S(2)}) %collective-permute-start.20) | collective-permute-done | bytes 786464 | tf_op jit(solution)/shard_map/ppermute | solution.py:41
  81.6 2.5 collective-permute-done.21.refs_7_
  84.3 3.3 collective-permute-start.28
  89.1 13.8 %collective-permute-done.26.refs_0_ = bf16[48,8192]{1,0:T(8,128)(2,1)} collective-permute-done((bf16[48,8192]{1,0:T(8,128)(2,1)S(1)}, bf16[48,8192]{1,0:T(8,128)(2,1)}, u32[]{:S(2)}, u32[]{:S(2)}) %collective-permute-start.26) | collective-permute-done | bytes 786464 | tf_op jit(solution)/shard_map/ppermute | solution.py:41
  103.4 1.9 collective-permute-done.28.refs_2_
  109.0 17.8 %forward.3 = (bf16[384,512]{1,0:T(8,128)(2,1)}, bf16[384,256]{1,0:T(8,128)(2,1)}, bf16[384,8192]{1,0:T(8,128)(2,1)}, bf16[384,8192]{1,0:T(8,128)(2,1)}) custom-call(bf16[48,8192]{1,0:T(8,128)(2,1)} %bitcast.50, bf16[48,8192]{1,0:T(8,128)(2,1)} %copy-done.9, bf16[48,8192]{1,0:T(8,128)(2,1)} %copy-done.8, bf16[48,8192]{1,0:T(8,128)(2,1)} %copy-done.7, ...), custom_call_target="tpu_custom_call" | custom-call | tf_op jit(solution)/shard_map/forward/pallas_call | solution.py:105
  126.8 15.3 %forward.4 = (bf16[288,512]{1,0:T(8,128)(2,1)}, bf16[288,256]{1,0:T(8,128)(2,1)}, bf16[288,8192]{1,0:T(8,128)(2,1)}, bf16[288,8192]{1,0:T(8,128)(2,1)}) custom-call(bf16[48,8192]{1,0:T(8,128)(2,1)} %copy-done.16, bf16[48,8192]{1,0:T(8,128)(2,1)} %copy-done.11, bf16[48,8192]{1,0:T(8,128)(2,1)} %copy-done.15, ...), custom_call_target="tpu_custom_call" | custom-call | tf_op jit(solution)/shard_map/forward/pallas_call | solution.py:105
  142.1 10.8 %forward.5 = (bf16[96,512]{1,0:T(8,128)(2,1)}, bf16[96,256]{1,0:T(8,128)(2,1)}, bf16[96,8192]{1,0:T(8,128)(2,1)}, bf16[96,8192]{1,0:T(8,128)(2,1)}) custom-call(bf16[48,8192]{1,0:T(8,128)(2,1)} %collective-permute-done.26.refs_0_, bf16[48,8192]{1,0:T(8,128)(2,1)} %collective-permute-done.27.refs_1_, bf16[48,8192]{1,0:T(8,128)(2,1)} %collective-permute-done.28.refs_2_, ...), custom_call_target="tpu_custom_call" | custom-call | tf_op jit(solution)/shard_map/forward/pallas_call | solution.py:105
  152.9 9.4 %early.1 = (bf16[3,256,512]{2,1,0:T(8,128)(2,1)}, bf16[3,256,512]{2,1,0:T(8,128)(2,1)}, bf16[3,256,512]{2,1,0:T(8,128)(2,1)}, bf16[3,256,512]{2,1,0:T(8,128)(2,1...) custom-call(s32[4]{0:T(128)} %pad_add_fusion.place, ...), custom_call_target="tpu_custom_call" | custom-call | tf_op jit(solution)/shard_map/early/pallas_call | solution.py:311
  162.3 9.8 %input.3 = (bf16[192,8192]{1,0:T(8,128)(2,1)}, bf16[192,8192]{1,0:T(8,128)(2,1)}) custom-call(bf16[288,512]{1,0:T(8,128)(2,1)} %get-tuple-element.79.refs_7_.refs_0_, bf16[96,512]{1,0:T(8,128)(2,1)} %get-tuple-element.59.refs_8_.refs_1_, bf16[8192,256]{1,0:T(8,128)(2,1)} %refs_2_.3, bf16[8192,256]{1,0:T(8,128)(2,1)} %refs_3_.1), custom_call_target="tpu_custom_call" | custom-call | tf_op jit(solution)/shard_map/input/pallas_call | solution.py:143
  172.6 1.9 collective-permute-start.30
  174.5 2.1 collective-permute-start.31
  177.3 19.9 %late.1 = (bf16[3,256,512]{2,1,0:T(8,128)(2,1)}, bf16[3,256,512]{2,1,0:T(8,128)(2,1)}, bf16[3,256,512]{2,1,0:T(8,128)(2,1)}, bf16[3,256,512]{2,1,0:T(8,128)(2,1)...) custom-call(s32[12]{0:T(128)} %stack.133.place, ...), custom_call_target="tpu_custom_call" | custom-call | tf_op jit(solution)/shard_map/late/pallas_call | solution.py:334
  197.2 2.1 collective-permute-start.33
  199.3 9.8 %input.2 = (bf16[192,8192]{1,0:T(8,128)(2,1)}, bf16[192,8192]{1,0:T(8,128)(2,1)}) custom-call(bf16[384,512]{1,0:T(8,128)(2,1)} %get-tuple-element.50.refs_0_.refs_6_, bf16[8192,256]{1,0:T(8,128)(2,1)} %refs_2_.3, bf16[8192,256]{1,0:T(8,128)(2,1)} %refs_3_.1), custom_call_target="tpu_custom_call" | custom-call | tf_op jit(solution)/shard_map/input/pallas_call | solution.py:143
  209.8 1.6 collective-permute-start.49
  211.4 3.3 collective-permute-start.52
  214.7 3.5 relay.2
  218.6 4.0 %add_convert_fusion = bf16[192,8192]{1,0:T(8,128)(2,1)S(1)} fusion(bf16[192,8192]{1,0:T(8,128)(2,1)} %collective-permute-done.37, bf16[192,8192]{1,0:T(8,128)(2,1)} %get-tuple-element.80), kind=kLoop, calls=%fused_computation | loop fusion | flops 6291456 | bytes 9437184 | tf_op jit(solution)/shard_map/convert_element_type | solution.py:361
  222.7 1.6 collective-permute-start.48
  224.3 1.4 fusion.5
  225.8 6.6 %collective-permute-done.45 = bf16[3,256,512]{2,1,0:T(8,128)(2,1)} collective-permute-done((bf16[3,256,512]{2,1,0:T(8,128)(2,1)}, bf16[3,256,512]{2,1,0:T(8,128)(2,1)}, u32[]{:S(2)}, u32[]{:S(2)}) %collective-permute-start.45) | collective-permute-done | bytes 786464 | tf_op jit(solution)/shard_map/ppermute | solution.py:53
  232.4 1.7 collective-permute-start.35
  234.1 4.8 %collective-permute-done.47.a = bf16[3,256,512]{2,1,0:T(8,128)(2,1)} collective-permute-done((bf16[3,256,512]{2,1,0:T(8,128)(2,1)}, bf16[3,256,512]{2,1,0:T(8,128)(2,1)}, u32[]{:S(2)}, u32[]{:S(2)}) %collective-permute-start.47) | collective-permute-done | bytes 786464 | tf_op jit(solution)/shard_map/ppermute | solution.py:57
  238.9 15.3 %collective-permute-done.48.b = bf16[3,256,512]{2,1,0:T(8,128)(2,1)} collective-permute-done((bf16[3,256,512]{2,1,0:T(8,128)(2,1)S(1)}, bf16[3,256,512]{2,1,0:T(8,128)(2,1)}, u32[]{:S(2)}, u32[]{:S(2)}) %collective-permute-start.48) | collective-permute-done | bytes 786464 | tf_op jit(solution)/shard_map/ppermute | solution.py:57
  254.3 3.7 %collective-permute-start.42 = (bf16[48,8192]{1,0:T(8,128)(2,1)}, bf16[48,8192]{1,0:T(8,128)(2,1)}, u32[]{:S(2)}, u32[]{:S(2)}) collective-permute-start(bf16[48,8192]{1,0:T(8,128)(2,1)} %get-tuple-element.101), channel_id=1, source_target_pairs={{0,6},{1,7},{2,0},{3,1},{4,2},{5,3},{6,4},{7,5},{8,14},{9,15},{10,... | collective-permute-start | bytes 2359304 | tf_op jit(solution)/shard_map/ppermute | solution.py:41
  258.1 1.0 slice_reduce_fusion.1
  259.1 3.5 relay.3
  262.7 1.5 collective-permute-start.58
  264.2 2.6 fusion.1
  267.2 2.3 copy-done
  269.5 2.3 join.1
  272.0 1.9 collective-permute-done.42
  273.9 1.7 add_convert_fusion.4
  275.6 3.8 %collective-permute-start.43 = (bf16[48,8192]{1,0:T(8,128)(2,1)S(1)}, bf16[48,8192]{1,0:T(8,128)(2,1)S(1)}, u32[]{:S(2)}, u32[]{:S(2)}) collective-permute-start(bf16[48,8192]{1,0:T(8,128)(2,1)S(1)} %add_convert_fusion.4), channel_id=1, source_target_pairs={{0,6},{1,7},{2,0},{3,1},{4,2},{5,3},{6,4},{7,5},{8,14},{9,15},{10,... | collective-permute-start | bytes 2359304 | tf_op jit(solution)/shard_map/ppermute | solution.py:41
  279.4 3.0 add_convert_fusion.1
  282.4 24.8 %collective-permute-done.41 = bf16[48,8192]{1,0:T(8,128)(2,1)S(1)} collective-permute-done((bf16[48,8192]{1,0:T(8,128)(2,1)S(1)}, bf16[48,8192]{1,0:T(8,128)(2,1)S(1)}, u32[]{:S(2)}, u32[]{:S(2)}) %collective-permute-start.41) | collective-permute-done | bytes 786464 | tf_op jit(solution)/shard_map/ppermute | solution.py:41
  307.1 1.7 collective-permute-start.56
  308.9 1.5 collective-permute-start.53
  311.8 2.4 collective-permute-start.51
  315.2 14.1 %collective-permute-done.53.r1 = bf16[3,256,512]{2,1,0:T(8,128)(2,1)S(1)} collective-permute-done((bf16[3,256,512]{2,1,0:T(8,128)(2,1)S(1)}, bf16[3,256,512]{2,1,0:T(8,128)(2,1)S(1)}, u32[]{:S(2)}, u32[]{:S(2)}) %collective-permute-start.53) | collective-permute-done | bytes 786464 | tf_op jit(solution)/shard_map/ppermute | solution.py:53
  329.7 2.3 collective-permute-done.46.l0
  332.0 13.6 %collective-permute-done.50.l1 = bf16[3,256,512]{2,1,0:T(8,128)(2,1)S(1)} collective-permute-done((bf16[3,256,512]{2,1,0:T(8,128)(2,1)S(1)}, bf16[3,256,512]{2,1,0:T(8,128)(2,1)S(1)}, u32[]{:S(2)}, u32[]{:S(2)}) %collective-permute-start.50) | collective-permute-done | bytes 786464 | tf_op jit(solution)/shard_map/ppermute | solution.py:53
  345.7 2.9 collective-permute-start.44
  348.6 2.3 last.1
  350.9 12.3 %collective-permute-done.39 = bf16[48,8192]{1,0:T(8,128)(2,1)S(1)} collective-permute-done((bf16[48,8192]{1,0:T(8,128)(2,1)S(1)}, bf16[48,8192]{1,0:T(8,128)(2,1)S(1)}, u32[]{:S(2)}, u32[]{:S(2)}) %collective-permute-start.39) | collective-permute-done | bytes 786464 | tf_op jit(solution)/shard_map/ppermute | solution.py:41
  363.2 1.8 collective-permute-done.44
  365.0 1.3 fusion.4
  (159 shorter events, 13.8 us)
Async XLA Ops:
  0.6 6.2 %collective-permute-start.3 = (bf16[48,8192]{1,0:T(8,128)(2,1)}, bf16[48,8192]{1,0:T(8,128)(2,1)}, u32[]{:S(2)}, u32[]{:S(2)}) collective-permute-start(bf16[48,8192]{1,0:T(8,128)(2,1)} %bitcast.46), channel_id=1, source_target_pairs={{0,1},{1,0},{2,3},{3,2},{4,5},{5,4},{6,7},{7,6},{8,9},{9,8},{10,11... | collective-permute-start | bytes 2359304 | tf_op jit(solution)/shard_map/ppermute | solution.py:49
  0.7 22.2 %collective-permute-start.2 = (bf16[48,8192]{1,0:T(8,128)(2,1)}, bf16[48,8192]{1,0:T(8,128)(2,1)S(1)}, u32[]{:S(2)}, u32[]{:S(2)}) collective-permute-start(bf16[48,8192]{1,0:T(8,128)(2,1)} %bitcast.47), channel_id=1, source_target_pairs={{0,8},{1,9},{2,10},{3,11},{4,12},{5,13},{6,14},{7,15},{8,0},{9,1},... | collective-permute-start | bytes 2359304 | tf_op jit(solution)/shard_map/ppermute | solution.py:45
  4.1 21.7 %collective-permute-start.1 = (bf16[48,8192]{1,0:T(8,128)(2,1)}, bf16[48,8192]{1,0:T(8,128)(2,1)S(1)}, u32[]{:S(2)}, u32[]{:S(2)}) collective-permute-start(bf16[48,8192]{1,0:T(8,128)(2,1)} %bitcast.48), channel_id=1, source_target_pairs={{0,6},{1,7},{2,0},{3,1},{4,2},{5,3},{6,4},{7,5},{8,14},{9,15},{10,... | collective-permute-start | bytes 2359304 | tf_op jit(solution)/shard_map/ppermute | solution.py:41
  6.9 20.7 %collective-permute-start = (bf16[48,8192]{1,0:T(8,128)(2,1)}, bf16[48,8192]{1,0:T(8,128)(2,1)S(1)}, u32[]{:S(2)}, u32[]{:S(2)}) collective-permute-start(bf16[48,8192]{1,0:T(8,128)(2,1)} %bitcast.49), channel_id=1, source_target_pairs={{0,2},{1,3},{2,4},{3,5},{4,6},{5,7},{6,0},{7,1},{8,10},{9,11},{10,... | collective-permute-start | bytes 2359304 | tf_op jit(solution)/shard_map/ppermute | solution.py:41
  6.9 22.2 %collective-permute-start.10 = (bf16[48,8192]{1,0:T(8,128)(2,1)}, bf16[48,8192]{1,0:T(8,128)(2,1)S(1)}, u32[]{:S(2)}, u32[]{:S(2)}) collective-permute-start(bf16[48,8192]{1,0:T(8,128)(2,1)} %bitcast.51), channel_id=1, source_target_pairs={{0,1},{1,0},{2,3},{3,2},{4,5},{5,4},{6,7},{7,6},{8,9},{9,8},{10,11... | collective-permute-start | bytes 2359304 | tf_op jit(solution)/shard_map/ppermute | solution.py:49
  6.9 32.4 %collective-permute-start.9 = (bf16[48,8192]{1,0:T(8,128)(2,1)}, bf16[48,8192]{1,0:T(8,128)(2,1)S(1)}, u32[]{:S(2)}, u32[]{:S(2)}) collective-permute-start(bf16[48,8192]{1,0:T(8,128)(2,1)} %bitcast.52), channel_id=1, source_target_pairs={{0,8},{1,9},{2,10},{3,11},{4,12},{5,13},{6,14},{7,15},{8,0},{9,1},... | collective-permute-start | bytes 2359304 | tf_op jit(solution)/shard_map/ppermute | solution.py:45
  22.9 21.1 %collective-permute-start.8 = (bf16[48,8192]{1,0:T(8,128)(2,1)}, bf16[48,8192]{1,0:T(8,128)(2,1)S(1)}, u32[]{:S(2)}, u32[]{:S(2)}) collective-permute-start(bf16[48,8192]{1,0:T(8,128)(2,1)} %bitcast.53), channel_id=1, source_target_pairs={{0,6},{1,7},{2,0},{3,1},{4,2},{5,3},{6,4},{7,5},{8,14},{9,15},{10,... | collective-permute-start | bytes 2359304 | tf_op jit(solution)/shard_map/ppermute | solution.py:41
  25.8 20.3 %collective-permute-start.7 = (bf16[48,8192]{1,0:T(8,128)(2,1)}, bf16[48,8192]{1,0:T(8,128)(2,1)S(1)}, u32[]{:S(2)}, u32[]{:S(2)}) collective-permute-start(bf16[48,8192]{1,0:T(8,128)(2,1)} %bitcast.54), channel_id=1, source_target_pairs={{0,2},{1,3},{2,4},{3,5},{4,6},{5,7},{6,0},{7,1},{8,10},{9,11},{10,... | collective-permute-start | bytes 2359304 | tf_op jit(solution)/shard_map/ppermute | solution.py:41
  27.6 31.2 %collective-permute-start.15 = (bf16[48,8192]{1,0:T(8,128)(2,1)S(1)}, bf16[48,8192]{1,0:T(8,128)(2,1)S(1)}, u32[]{:S(2)}, u32[]{:S(2)}) collective-permute-start(bf16[48,8192]{1,0:T(8,128)(2,1)S(1)} %collective-permute-done.2.refs_3_), channel_id=1, source_target_pairs={{0,6},{1,7},{2,0},{3,1},{4,2},{5,3},{6,4},{7,5},{8,14},{9,15},{10,... | collective-permute-start | bytes 2359304 | tf_op jit(solution)/shard_map/ppermute | solution.py:41
  29.1 38.4 %copy-start.10 = (bf16[48,8192]{1,0:T(8,128)(2,1)}, bf16[48,8192]{1,0:T(8,128)(2,1)S(1)}, u32[]{:S(2)}) copy-start(bf16[48,8192]{1,0:T(8,128)(2,1)S(1)} %collective-permute-done.10.refs_12_) | copy-start | bytes 2359300
  29.1 29.8 %collective-permute-start.6 = (bf16[48,8192]{1,0:T(8,128)(2,1)S(1)}, bf16[48,8192]{1,0:T(8,128)(2,1)S(1)}, u32[]{:S(2)}, u32[]{:S(2)}) collective-permute-start(bf16[48,8192]{1,0:T(8,128)(2,1)S(1)} %collective-permute-done.2.refs_3_), channel_id=1, source_target_pairs={{0,1},{1,0},{2,3},{3,2},{4,5},{5,4},{6,7},{7,6},{8,9},{9,8},{10,11... | collective-permute-start | bytes 2359304 | tf_op jit(solution)/shard_map/ppermute | solution.py:49
  39.3 42.2 %copy-start.12 = (bf16[48,8192]{1,0:T(8,128)(2,1)}, bf16[48,8192]{1,0:T(8,128)(2,1)S(1)}, u32[]{:S(2)}) copy-start(bf16[48,8192]{1,0:T(8,128)(2,1)S(1)} %collective-permute-done.9.refs_11_) | copy-start | bytes 2359300
  39.3 20.9 %collective-permute-start.5 = (bf16[48,8192]{1,0:T(8,128)(2,1)S(1)}, bf16[48,8192]{1,0:T(8,128)(2,1)S(1)}, u32[]{:S(2)}, u32[]{:S(2)}) collective-permute-start(bf16[48,8192]{1,0:T(8,128)(2,1)S(1)} %collective-permute-done.1.refs_2_), channel_id=1, source_target_pairs={{0,1},{1,0},{2,3},{3,2},{4,5},{5,4},{6,7},{7,6},{8,9},{9,8},{10,11... | collective-permute-start | bytes 2359304 | tf_op jit(solution)/shard_map/ppermute | solution.py:49
  44.1 18.2 %collective-permute-start.16 = (bf16[48,8192]{1,0:T(8,128)(2,1)S(1)}, bf16[48,8192]{1,0:T(8,128)(2,1)S(1)}, u32[]{:S(2)}, u32[]{:S(2)}) collective-permute-start(bf16[48,8192]{1,0:T(8,128)(2,1)S(1)} %collective-permute-done.refs_1_), channel_id=1, source_target_pairs={{0,2},{1,3},{2,4},{3,5},{4,6},{5,7},{6,0},{7,1},{8,10},{9,11},{10,... | collective-permute-start | bytes 2359304 | tf_op jit(solution)/shard_map/ppermute | solution.py:41
  46.1 38.0 %copy-start.14 = (bf16[48,8192]{1,0:T(8,128)(2,1)}, bf16[48,8192]{1,0:T(8,128)(2,1)S(1)}, u32[]{:S(2)}) copy-start(bf16[48,8192]{1,0:T(8,128)(2,1)S(1)} %collective-permute-done.7.refs_9_) | copy-start | bytes 2359300
  46.1 18.1 %collective-permute-start.14 = (bf16[48,8192]{1,0:T(8,128)(2,1)S(1)}, bf16[48,8192]{1,0:T(8,128)(2,1)S(1)}, u32[]{:S(2)}, u32[]{:S(2)}) collective-permute-start(bf16[48,8192]{1,0:T(8,128)(2,1)S(1)} %collective-permute-done.refs_1_), channel_id=1, source_target_pairs={{0,8},{1,9},{2,10},{3,11},{4,12},{5,13},{6,14},{7,15},{8,0},{9,1},... | collective-permute-start | bytes 2359304 | tf_op jit(solution)/shard_map/ppermute | solution.py:45
  58.8 8.6 %collective-permute-start.4 = (bf16[48,8192]{1,0:T(8,128)(2,1)S(1)}, bf16[48,8192]{1,0:T(8,128)(2,1)S(1)}, u32[]{:S(2)}, u32[]{:S(2)}) collective-permute-start(bf16[48,8192]{1,0:T(8,128)(2,1)S(1)} %collective-permute-done.refs_1_), channel_id=1, source_target_pairs={{0,1},{1,0},{2,3},{3,2},{4,5},{5,4},{6,7},{7,6},{8,9},{9,8},{10,11... | collective-permute-start | bytes 2359304 | tf_op jit(solution)/shard_map/ppermute | solution.py:49
  58.9 22.1 %collective-permute-start.20 = (bf16[48,8192]{1,0:T(8,128)(2,1)S(1)}, bf16[48,8192]{1,0:T(8,128)(2,1)}, u32[]{:S(2)}, u32[]{:S(2)}) collective-permute-start(bf16[48,8192]{1,0:T(8,128)(2,1)S(1)} %collective-permute-done.9.refs_11_), channel_id=1, source_target_pairs={{0,2},{1,3},{2,4},{3,5},{4,6},{5,7},{6,0},{7,1},{8,10},{9,11},{10,... | collective-permute-start | bytes 2359304 | tf_op jit(solution)/shard_map/ppermute | solution.py:41
  60.2 20.8 %collective-permute-start.13 = (bf16[48,8192]{1,0:T(8,128)(2,1)S(1)}, bf16[48,8192]{1,0:T(8,128)(2,1)S(1)}, u32[]{:S(2)}, u32[]{:S(2)}) collective-permute-start(bf16[48,8192]{1,0:T(8,128)(2,1)S(1)} %collective-permute-done.9.refs_11_), channel_id=1, source_target_pairs={{0,1},{1,0},{2,3},{3,2},{4,5},{5,4},{6,7},{7,6},{8,9},{9,8},{10,11... | collective-permute-start | bytes 2359304 | tf_op jit(solution)/shard_map/ppermute | solution.py:49
  62.3 19.3 %collective-permute-start.22 = (bf16[48,8192]{1,0:T(8,128)(2,1)S(1)}, bf16[48,8192]{1,0:T(8,128)(2,1)}, u32[]{:S(2)}, u32[]{:S(2)}) collective-permute-start(bf16[48,8192]{1,0:T(8,128)(2,1)S(1)} %collective-permute-done.8.refs_10_), channel_id=1, source_target_pairs={{0,6},{1,7},{2,0},{3,1},{4,2},{5,3},{6,4},{7,5},{8,14},{9,15},{10,... | collective-permute-start | bytes 2359304 | tf_op jit(solution)/shard_map/ppermute | solution.py:41
  64.2 19.9 %collective-permute-start.21 = (bf16[48,8192]{1,0:T(8,128)(2,1)S(1)}, bf16[48,8192]{1,0:T(8,128)(2,1)}, u32[]{:S(2)}, u32[]{:S(2)}) collective-permute-start(bf16[48,8192]{1,0:T(8,128)(2,1)S(1)} %collective-permute-done.8.refs_10_), channel_id=1, source_target_pairs={{0,8},{1,9},{2,10},{3,11},{4,12},{5,13},{6,14},{7,15},{8,0},{9,1},... | collective-permute-start | bytes 2359304 | tf_op jit(solution)/shard_map/ppermute | solution.py:45
  67.4 16.7 %collective-permute-start.12 = (bf16[48,8192]{1,0:T(8,128)(2,1)S(1)}, bf16[48,8192]{1,0:T(8,128)(2,1)S(1)}, u32[]{:S(2)}, u32[]{:S(2)}) collective-permute-start(bf16[48,8192]{1,0:T(8,128)(2,1)S(1)} %collective-permute-done.8.refs_10_), channel_id=1, source_target_pairs={{0,1},{1,0},{2,3},{3,2},{4,5},{5,4},{6,7},{7,6},{8,9},{9,8},{10,11... | collective-permute-start | bytes 2359304 | tf_op jit(solution)/shard_map/ppermute | solution.py:49
  80.9 3.3 collective-permute-start.11
  81.0 7.5 %collective-permute-start.18 = (bf16[48,8192]{1,0:T(8,128)(2,1)S(1)}, bf16[48,8192]{1,0:T(8,128)(2,1)S(1)}, u32[]{:S(2)}, u32[]{:S(2)}) collective-permute-start(bf16[48,8192]{1,0:T(8,128)(2,1)S(1)} %collective-permute-done.15.refs_1_), channel_id=1, source_target_pairs={{0,1},{1,0},{2,3},{3,2},{4,5},{5,4},{6,7},{7,6},{8,9},{9,8},{10,11... | collective-permute-start | bytes 2359304 | tf_op jit(solution)/shard_map/ppermute | solution.py:49
  81.5 7.2 %collective-permute-start.19 = (bf16[48,8192]{1,0:T(8,128)(2,1)S(1)}, bf16[48,8192]{1,0:T(8,128)(2,1)}, u32[]{:S(2)}, u32[]{:S(2)}) collective-permute-start(bf16[48,8192]{1,0:T(8,128)(2,1)S(1)} %collective-permute-done.16.refs_2_), channel_id=1, source_target_pairs={{0,1},{1,0},{2,3},{3,2},{4,5},{5,4},{6,7},{7,6},{8,9},{9,8},{10,11... | collective-permute-start | bytes 2359304 | tf_op jit(solution)/shard_map/ppermute | solution.py:49
  84.1 18.8 %collective-permute-start.26 = (bf16[48,8192]{1,0:T(8,128)(2,1)S(1)}, bf16[48,8192]{1,0:T(8,128)(2,1)}, u32[]{:S(2)}, u32[]{:S(2)}) collective-permute-start(bf16[48,8192]{1,0:T(8,128)(2,1)S(1)} %collective-permute-done.14.refs_0_), channel_id=1, source_target_pairs={{0,2},{1,3},{2,4},{3,5},{4,6},{5,7},{6,0},{7,1},{8,10},{9,11},{10,... | collective-permute-start | bytes 2359304 | tf_op jit(solution)/shard_map/ppermute | solution.py:41
  84.1 18.7 %collective-permute-start.17 = (bf16[48,8192]{1,0:T(8,128)(2,1)S(1)}, bf16[48,8192]{1,0:T(8,128)(2,1)}, u32[]{:S(2)}, u32[]{:S(2)}) collective-permute-start(bf16[48,8192]{1,0:T(8,128)(2,1)S(1)} %collective-permute-done.14.refs_0_), channel_id=1, source_target_pairs={{0,1},{1,0},{2,3},{3,2},{4,5},{5,4},{6,7},{7,6},{8,9},{9,8},{10,11... | collective-permute-start | bytes 2359304 | tf_op jit(solution)/shard_map/ppermute | solution.py:49
  84.3 21.0 %collective-permute-start.28 = (bf16[48,8192]{1,0:T(8,128)(2,1)}, bf16[48,8192]{1,0:T(8,128)(2,1)}, u32[]{:S(2)}, u32[]{:S(2)}) collective-permute-start(bf16[48,8192]{1,0:T(8,128)(2,1)} %collective-permute-done.21.refs_7_), channel_id=1, source_target_pairs={{0,6},{1,7},{2,0},{3,1},{4,2},{5,3},{6,4},{7,5},{8,14},{9,15},{10,... | collective-permute-start | bytes 2359304 | tf_op jit(solution)/shard_map/ppermute | solution.py:41
  88.5 38.3 %collective-permute-start.24 = (bf16[48,8192]{1,0:T(8,128)(2,1)}, bf16[48,8192]{1,0:T(8,128)(2,1)}, u32[]{:S(2)}, u32[]{:S(2)}) collective-permute-start(bf16[48,8192]{1,0:T(8,128)(2,1)} %collective-permute-done.21.refs_7_), channel_id=1, source_target_pairs={{0,1},{1,0},{2,3},{3,2},{4,5},{5,4},{6,7},{7,6},{8,9},{9,8},{10,11... | collective-permute-start | bytes 2359304 | tf_op jit(solution)/shard_map/ppermute | solution.py:49
  88.8 38.0 %collective-permute-start.23 = (bf16[48,8192]{1,0:T(8,128)(2,1)}, bf16[48,8192]{1,0:T(8,128)(2,1)}, u32[]{:S(2)}, u32[]{:S(2)}) collective-permute-start(bf16[48,8192]{1,0:T(8,128)(2,1)} %collective-permute-done.20.refs_6_), channel_id=1, source_target_pairs={{0,1},{1,0},{2,3},{3,2},{4,5},{5,4},{6,7},{7,6},{8,9},{9,8},{10,11... | collective-permute-start | bytes 2359304 | tf_op jit(solution)/shard_map/ppermute | solution.py:49
  102.9 23.9 %collective-permute-start.25 = (bf16[48,8192]{1,0:T(8,128)(2,1)}, bf16[48,8192]{1,0:T(8,128)(2,1)}, u32[]{:S(2)}, u32[]{:S(2)}) collective-permute-start(bf16[48,8192]{1,0:T(8,128)(2,1)} %collective-permute-done.22.refs_8_), channel_id=1, source_target_pairs={{0,1},{1,0},{2,3},{3,2},{4,5},{5,4},{6,7},{7,6},{8,9},{9,8},{10,11... | collective-permute-start | bytes 2359304 | tf_op jit(solution)/shard_map/ppermute | solution.py:49
  102.9 39.2 %collective-permute-start.27 = (bf16[48,8192]{1,0:T(8,128)(2,1)}, bf16[48,8192]{1,0:T(8,128)(2,1)}, u32[]{:S(2)}, u32[]{:S(2)}) collective-permute-start(bf16[48,8192]{1,0:T(8,128)(2,1)} %collective-permute-done.26.refs_0_), channel_id=1, source_target_pairs={{0,1},{1,0},{2,3},{3,2},{4,5},{5,4},{6,7},{7,6},{8,9},{9,8},{10,11... | collective-permute-start | bytes 2359304 | tf_op jit(solution)/shard_map/ppermute | solution.py:49
  105.3 36.8 %collective-permute-start.29 = (bf16[48,8192]{1,0:T(8,128)(2,1)}, bf16[48,8192]{1,0:T(8,128)(2,1)}, u32[]{:S(2)}, u32[]{:S(2)}) collective-permute-start(bf16[48,8192]{1,0:T(8,128)(2,1)} %collective-permute-done.28.refs_2_), channel_id=1, source_target_pairs={{0,1},{1,0},{2,3},{3,2},{4,5},{5,4},{6,7},{7,6},{8,9},{9,8},{10,11... | collective-permute-start | bytes 2359304 | tf_op jit(solution)/shard_map/ppermute | solution.py:49
  172.1 46.1 %collective-permute-start.37 = (bf16[192,8192]{1,0:T(8,128)(2,1)}, bf16[192,8192]{1,0:T(8,128)(2,1)}, u32[]{:S(2)}, u32[]{:S(2)}) collective-permute-start(bf16[192,8192]{1,0:T(8,128)(2,1)} %get-tuple-element.81), channel_id=1, source_target_pairs={{0,1},{1,0},{2,3},{3,2},{4,5},{5,4},{6,7},{7,6},{8,9},{9,8},{10,11... | collective-permute-start | bytes 9437192 | tf_op jit(solution)/shard_map/ppermute | solution.py:49
  172.6 38.8 %collective-permute-start.30 = (bf16[3,256,512]{2,1,0:T(8,128)(2,1)}, bf16[3,256,512]{2,1,0:T(8,128)(2,1)}, u32[]{:S(2)}, u32[]{:S(2)}) collective-permute-start(bf16[3,256,512]{2,1,0:T(8,128)(2,1)} %get-tuple-element.69), channel_id=1, source_target_pairs={{0,32},{16,48},{32,64},{48,80},{64,96},{80,112},{96,0},{112,16},{1... | collective-permute-start | bytes 2359304 | tf_op jit(solution)/shard_map/ppermute | solution.py:53
  174.5 36.9 %collective-permute-start.31 = (bf16[3,256,512]{2,1,0:T(8,128)(2,1)}, bf16[3,256,512]{2,1,0:T(8,128)(2,1)}, u32[]{:S(2)}, u32[]{:S(2)}) collective-permute-start(bf16[3,256,512]{2,1,0:T(8,128)(2,1)} %get-tuple-element.70), channel_id=1, source_target_pairs={{0,96},{16,112},{32,0},{48,16},{64,32},{80,48},{96,64},{112,80},{1... | collective-permute-start | bytes 2359304 | tf_op jit(solution)/shard_map/ppermute | solution.py:53
  197.2 11.9 %collective-permute-start.33 = (f32[256,128]{1,0:T(8,128)}, f32[256,128]{1,0:T(8,128)S(1)}, u32[]{:S(2)}, u32[]{:S(2)}) collective-permute-start(f32[256,128]{1,0:T(8,128)} %get-tuple-element.71.ratio), channel_id=1, source_target_pairs={{0,96},{16,112},{32,0},{48,16},{64,32},{80,48},{96,64},{112,80},{1... | collective-permute-start | bytes 393224 | tf_op jit(solution)/shard_map/ppermute | solution.py:53
  199.3 10.5 %collective-permute-start.32 = (f32[256,128]{1,0:T(8,128)}, f32[256,128]{1,0:T(8,128)}, u32[]{:S(2)}, u32[]{:S(2)}) collective-permute-start(f32[256,128]{1,0:T(8,128)} %get-tuple-element.71.ratio), channel_id=1, source_target_pairs={{0,32},{16,48},{32,64},{48,80},{64,96},{80,112},{96,0},{112,16},{1... | collective-permute-start | bytes 393224 | tf_op jit(solution)/shard_map/ppermute | solution.py:53
  209.2 62.6 %collective-permute-start.36 = (bf16[192,8192]{1,0:T(8,128)(2,1)}, bf16[192,8192]{1,0:T(8,128)(2,1)}, u32[]{:S(2)}, u32[]{:S(2)}) collective-permute-start(bf16[192,8192]{1,0:T(8,128)(2,1)} %get-tuple-element.77), channel_id=1, source_target_pairs={{0,1},{1,0},{2,3},{3,2},{4,5},{5,4},{6,7},{7,6},{8,9},{9,8},{10,11... | collective-permute-start | bytes 9437192 | tf_op jit(solution)/shard_map/ppermute | solution.py:49
  209.8 12.8 %collective-permute-start.49 = (f32[256,128]{1,0:T(8,128)S(1)}, f32[256,128]{1,0:T(8,128)S(1)}, u32[]{:S(2)}, u32[]{:S(2)}) collective-permute-start(f32[256,128]{1,0:T(8,128)S(1)} %copy-done.1), channel_id=1, source_target_pairs={{0,16},{16,0},{32,48},{48,32},{64,80},{80,64},{96,112},{112,96},{1... | collective-permute-start | bytes 393224 | tf_op jit(solution)/shard_map/ppermute | solution.py:57
  211.4 21.0 %collective-permute-start.45 = (bf16[3,256,512]{2,1,0:T(8,128)(2,1)}, bf16[3,256,512]{2,1,0:T(8,128)(2,1)}, u32[]{:S(2)}, u32[]{:S(2)}) collective-permute-start(bf16[3,256,512]{2,1,0:T(8,128)(2,1)} %get-tuple-element.84), channel_id=1, source_target_pairs={{0,32},{16,48},{32,64},{48,80},{64,96},{80,112},{96,0},{112,16},{1... | collective-permute-start | bytes 2359304 | tf_op jit(solution)/shard_map/ppermute | solution.py:53
  211.4 51.3 %collective-permute-start.52 = (bf16[3,256,512]{2,1,0:T(8,128)(2,1)}, bf16[3,256,512]{2,1,0:T(8,128)(2,1)}, u32[]{:S(2)}, u32[]{:S(2)}) collective-permute-start(bf16[3,256,512]{2,1,0:T(8,128)(2,1)} %get-tuple-element.91), channel_id=1, source_target_pairs={{0,96},{16,112},{32,0},{48,16},{64,32},{80,48},{96,64},{112,80},{1... | collective-permute-start | bytes 2359304 | tf_op jit(solution)/shard_map/ppermute | solution.py:53
  218.2 20.7 %collective-permute-start.47 = (bf16[3,256,512]{2,1,0:T(8,128)(2,1)}, bf16[3,256,512]{2,1,0:T(8,128)(2,1)}, u32[]{:S(2)}, u32[]{:S(2)}) collective-permute-start(bf16[3,256,512]{2,1,0:T(8,128)(2,1)} %get-tuple-element.87), channel_id=1, source_target_pairs={{0,16},{16,0},{32,48},{48,32},{64,80},{80,64},{96,112},{112,96},{1... | collective-permute-start | bytes 2359304 | tf_op jit(solution)/shard_map/ppermute | solution.py:57
  222.7 31.6 %collective-permute-start.48 = (bf16[3,256,512]{2,1,0:T(8,128)(2,1)S(1)}, bf16[3,256,512]{2,1,0:T(8,128)(2,1)}, u32[]{:S(2)}, u32[]{:S(2)}) collective-permute-start(bf16[3,256,512]{2,1,0:T(8,128)(2,1)S(1)} %copy-done.28), channel_id=1, source_target_pairs={{0,16},{16,0},{32,48},{48,32},{64,80},{80,64},{96,112},{112,96},{1... | collective-permute-start | bytes 2359304 | tf_op jit(solution)/shard_map/ppermute | solution.py:57
  232.4 34.4 %collective-permute-start.35 = (bf16[3,256,512]{2,1,0:T(8,128)(2,1)}, bf16[3,256,512]{2,1,0:T(8,128)(2,1)}, u32[]{:S(2)}, u32[]{:S(2)}) collective-permute-start(bf16[3,256,512]{2,1,0:T(8,128)(2,1)} %get-tuple-element.73), channel_id=1, source_target_pairs={{0,96},{16,112},{32,0},{48,16},{64,32},{80,48},{96,64},{112,80},{1... | collective-permute-start | bytes 2359304 | tf_op jit(solution)/shard_map/ppermute | solution.py:53
  238.9 28.2 %collective-permute-start.34 = (bf16[3,256,512]{2,1,0:T(8,128)(2,1)}, bf16[3,256,512]{2,1,0:T(8,128)(2,1)}, u32[]{:S(2)}, u32[]{:S(2)}) collective-permute-start(bf16[3,256,512]{2,1,0:T(8,128)(2,1)} %get-tuple-element.72), channel_id=1, source_target_pairs={{0,32},{16,48},{32,64},{48,80},{64,96},{80,112},{96,0},{112,16},{1... | collective-permute-start | bytes 2359304 | tf_op jit(solution)/shard_map/ppermute | solution.py:53
  254.3 19.6 %collective-permute-start.42 = (bf16[48,8192]{1,0:T(8,128)(2,1)}, bf16[48,8192]{1,0:T(8,128)(2,1)}, u32[]{:S(2)}, u32[]{:S(2)}) collective-permute-start(bf16[48,8192]{1,0:T(8,128)(2,1)} %get-tuple-element.101), channel_id=1, source_target_pairs={{0,6},{1,7},{2,0},{3,1},{4,2},{5,3},{6,4},{7,5},{8,14},{9,15},{10,... | collective-permute-start | bytes 2359304 | tf_op jit(solution)/shard_map/ppermute | solution.py:41
  262.7 47.7 %collective-permute-start.58 = (f32[256,1]{1,0:T(8,128)S(1)}, f32[256,1]{1,0:T(8,128)S(1)}, u32[]{:S(2)}, u32[]{:S(2)}) collective-permute-start(f32[256,1]{1,0:T(8,128)S(1)} %get-tuple-element.103), channel_id=1, source_target_pairs={{0,64},{16,80},{32,96},{48,112},{64,0},{80,16},{96,32},{112,48},{1... | collective-permute-start | bytes 3080 | tf_op jit(solution)/shard_map/ppermute | solution.py:53
  266.8 44.1 %collective-permute-start.57 = (f32[256,1]{1,0:T(8,128)S(1)}, f32[256,1]{1,0:T(8,128)S(1)}, u32[]{:S(2)}, u32[]{:S(2)}) collective-permute-start(f32[256,1]{1,0:T(8,128)S(1)} %get-tuple-element.103), channel_id=1, source_target_pairs={{0,96},{16,112},{32,0},{48,16},{64,32},{80,48},{96,64},{112,80},{1... | collective-permute-start | bytes 3080 | tf_op jit(solution)/shard_map/ppermute | solution.py:53
  271.8 40.0 %collective-permute-start.38 = (bf16[48,8192]{1,0:T(8,128)(2,1)S(1)}, bf16[48,8192]{1,0:T(8,128)(2,1)S(1)}, u32[]{:S(2)}, u32[]{:S(2)}) collective-permute-start(bf16[48,8192]{1,0:T(8,128)(2,1)S(1)} %copy-done.24), channel_id=1, source_target_pairs={{0,2},{1,3},{2,4},{3,5},{4,6},{5,7},{6,0},{7,1},{8,10},{9,11},{10,... | collective-permute-start | bytes 2359304 | tf_op jit(solution)/shard_map/ppermute | solution.py:41
  271.9 35.3 %collective-permute-start.41 = (bf16[48,8192]{1,0:T(8,128)(2,1)S(1)}, bf16[48,8192]{1,0:T(8,128)(2,1)S(1)}, u32[]{:S(2)}, u32[]{:S(2)}) collective-permute-start(bf16[48,8192]{1,0:T(8,128)(2,1)S(1)} %copy-done.25), channel_id=1, source_target_pairs={{0,2},{1,3},{2,4},{3,5},{4,6},{5,7},{6,0},{7,1},{8,10},{9,11},{10,... | collective-permute-start | bytes 2359304 | tf_op jit(solution)/shard_map/ppermute | solution.py:41
  273.9 74.8 %slice-start = ((s8[4718592]{0:T(1024)(128)(4,1)}), s8[4194304]{0:T(1024)(128)(4,1)S(1)}, s32[]{:S(2)}) async-start(s8[4718592]{0:T(1024)(128)(4,1)} %bitcast.43), calls=%async_computation | async-start | bytes 8388608
  275.6 73.1 %slice-start.1 = ((s8[4718592]{0:T(1024)(128)(4,1)}), s8[524288]{0:T(1024)(128)(4,1)S(1)}, s32[]{:S(2)}) async-start(s8[4718592]{0:T(1024)(128)(4,1)} %bitcast.43), calls=%async_computation.1 | async-start | bytes 1048576
  275.6 33.3 %collective-permute-start.43 = (bf16[48,8192]{1,0:T(8,128)(2,1)S(1)}, bf16[48,8192]{1,0:T(8,128)(2,1)S(1)}, u32[]{:S(2)}, u32[]{:S(2)}) collective-permute-start(bf16[48,8192]{1,0:T(8,128)(2,1)S(1)} %add_convert_fusion.4), channel_id=1, source_target_pairs={{0,6},{1,7},{2,0},{3,1},{4,2},{5,3},{6,4},{7,5},{8,14},{9,15},{10,... | collective-permute-start | bytes 2359304 | tf_op jit(solution)/shard_map/ppermute | solution.py:41
  307.1 7.6 %collective-permute-start.56 = (f32[256,1]{1,0:T(8,128)S(1)}, f32[256,1]{1,0:T(8,128)S(1)}, u32[]{:S(2)}, u32[]{:S(2)}) collective-permute-start(f32[256,1]{1,0:T(8,128)S(1)} %get-tuple-element.103), channel_id=1, source_target_pairs={{0,32},{16,48},{32,64},{48,80},{64,96},{80,112},{96,0},{112,16},{1... | collective-permute-start | bytes 3080 | tf_op jit(solution)/shard_map/ppermute | solution.py:53
  308.9 20.4 %collective-permute-start.53 = (bf16[3,256,512]{2,1,0:T(8,128)(2,1)S(1)}, bf16[3,256,512]{2,1,0:T(8,128)(2,1)S(1)}, u32[]{:S(2)}, u32[]{:S(2)}) collective-permute-start(bf16[3,256,512]{2,1,0:T(8,128)(2,1)S(1)} %get-tuple-element.96), channel_id=1, source_target_pairs={{0,96},{16,112},{32,0},{48,16},{64,32},{80,48},{96,64},{112,80},{1... | collective-permute-start | bytes 2359304 | tf_op jit(solution)/shard_map/ppermute | solution.py:53
  310.4 21.6 %collective-permute-start.46 = (bf16[3,256,512]{2,1,0:T(8,128)(2,1)S(1)}, bf16[3,256,512]{2,1,0:T(8,128)(2,1)S(1)}, u32[]{:S(2)}, u32[]{:S(2)}) collective-permute-start(bf16[3,256,512]{2,1,0:T(8,128)(2,1)S(1)} %get-tuple-element.97), channel_id=1, source_target_pairs={{0,32},{16,48},{32,64},{48,80},{64,96},{80,112},{96,0},{112,16},{1... | collective-permute-start | bytes 2359304 | tf_op jit(solution)/shard_map/ppermute | solution.py:53
  310.9 34.8 %collective-permute-start.50 = (bf16[3,256,512]{2,1,0:T(8,128)(2,1)S(1)}, bf16[3,256,512]{2,1,0:T(8,128)(2,1)S(1)}, u32[]{:S(2)}, u32[]{:S(2)}) collective-permute-start(bf16[3,256,512]{2,1,0:T(8,128)(2,1)S(1)} %copy-done.30), channel_id=1, source_target_pairs={{0,32},{16,48},{32,64},{48,80},{64,96},{80,112},{96,0},{112,16},{1... | collective-permute-start | bytes 2359304 | tf_op jit(solution)/shard_map/ppermute | solution.py:53
  311.8 33.9 %collective-permute-start.51 = (bf16[3,256,512]{2,1,0:T(8,128)(2,1)S(1)}, bf16[3,256,512]{2,1,0:T(8,128)(2,1)S(1)}, u32[]{:S(2)}, u32[]{:S(2)}) collective-permute-start(bf16[3,256,512]{2,1,0:T(8,128)(2,1)S(1)} %copy-done.29), channel_id=1, source_target_pairs={{0,96},{16,112},{32,0},{48,16},{64,32},{80,48},{96,64},{112,80},{1... | collective-permute-start | bytes 2359304 | tf_op jit(solution)/shard_map/ppermute | solution.py:53
  314.7 33.9 %collective-permute-start.54 = (bf16[3,256,512]{2,1,0:T(8,128)(2,1)S(1)}, bf16[3,256,512]{2,1,0:T(8,128)(2,1)S(1)}, u32[]{:S(2)}, u32[]{:S(2)}) collective-permute-start(bf16[3,256,512]{2,1,0:T(8,128)(2,1)S(1)} %get-tuple-element.74), channel_id=1, source_target_pairs={{0,16},{16,0},{32,48},{48,32},{64,80},{80,64},{96,112},{112,96},{1... | collective-permute-start | bytes 2359304 | tf_op jit(solution)/shard_map/ppermute | solution.py:57
  329.3 19.3 %collective-permute-start.55 = (bf16[3,256,512]{2,1,0:T(8,128)(2,1)S(1)}, bf16[3,256,512]{2,1,0:T(8,128)(2,1)S(1)}, u32[]{:S(2)}, u32[]{:S(2)}) collective-permute-start(bf16[3,256,512]{2,1,0:T(8,128)(2,1)S(1)} %get-tuple-element.75), channel_id=1, source_target_pairs={{0,16},{16,0},{32,48},{48,32},{64,80},{80,64},{96,112},{112,96},{1... | collective-permute-start | bytes 2359304 | tf_op jit(solution)/shard_map/ppermute | solution.py:57
  332.0 18.9 %collective-permute-start.40 = (bf16[48,8192]{1,0:T(8,128)(2,1)S(1)}, bf16[48,8192]{1,0:T(8,128)(2,1)S(1)}, u32[]{:S(2)}, u32[]{:S(2)}) collective-permute-start(bf16[48,8192]{1,0:T(8,128)(2,1)S(1)} %slice.93), channel_id=1, source_target_pairs={{0,6},{1,7},{2,0},{3,1},{4,2},{5,3},{6,4},{7,5},{8,14},{9,15},{10,... | collective-permute-start | bytes 2359304 | tf_op jit(solution)/shard_map/ppermute | solution.py:41
  345.7 17.6 %collective-permute-start.39 = (bf16[48,8192]{1,0:T(8,128)(2,1)S(1)}, bf16[48,8192]{1,0:T(8,128)(2,1)S(1)}, u32[]{:S(2)}, u32[]{:S(2)}) collective-permute-start(bf16[48,8192]{1,0:T(8,128)(2,1)S(1)} %get-tuple-element.98), channel_id=1, source_target_pairs={{0,2},{1,3},{2,4},{3,5},{4,6},{5,7},{6,0},{7,1},{8,10},{9,11},{10,... | collective-permute-start | bytes 2359304 | tf_op jit(solution)/shard_map/ppermute | solution.py:41
  345.7 19.3 %collective-permute-start.44 = (bf16[48,8192]{1,0:T(8,128)(2,1)S(1)}, bf16[48,8192]{1,0:T(8,128)(2,1)S(1)}, u32[]{:S(2)}, u32[]{:S(2)}) collective-permute-start(bf16[48,8192]{1,0:T(8,128)(2,1)S(1)} %get-tuple-element.99), channel_id=1, source_target_pairs={{0,8},{1,9},{2,10},{3,11},{4,12},{5,13},{6,14},{7,15},{8,0},{9,1},... | collective-permute-start | bytes 2359304 | tf_op jit(solution)/shard_map/ppermute | solution.py:45
  (28 other events, 507.7 us)
